TPU v7x, 32 devices: a whole 2x2x4 slice. The times are simulated.
32 devices in a mesh: dp: 16 (over z, y, x), tensor: 2 (over core).
Axes of the slice: x: 2, y: 2, z: 4, core: 2. Of those that a mesh axis runs over, the one named last changes fastest.
Arguments:
- tokens: bfloat16 [32768, 768], P(('dp', 'tensor')), may hold values from -6 to 6
- lengths: int32 [64], P('dp'), may hold values from 64 to 512, as said below
- qkv_weight: bfloat16 [3, 768, 768], P(None, None, 'tensor'), may hold values from -0.21875 to 0.21875
- qv_bias: float32 [2, 768], P(None, 'tensor'), may hold values from -3 to 3
- out_weight: bfloat16 [768, 768], P('tensor'), may hold values from -0.625 to 0.625
- out_bias: float32 [768], replicated, may hold values from -2 to 2
- first_gain: float32 [768], replicated, may hold values from 0.5 to 1.5
- first_shift: float32 [768], replicated, may hold values from -2 to 2
- up_weight: bfloat16 [768, 3072], P(None, 'tensor'), may hold values from -0.21875 to 0.21875
- up_bias: float32 [3072], P('tensor'), may hold values from -3 to 3
- down_weight: bfloat16 [3072, 768], P('tensor'), may hold values from -0.109375 to 0.109375
- down_bias: float32 [768], replicated, may hold values from -2 to 2
- second_gain: float32 [768], replicated, may hold values from 0.5 to 1.5
- second_shift: float32 [768], replicated, may hold values from -2 to 2
- cotangent: bfloat16 [32768, 768], P(('dp', 'tensor')), may hold values from -6 to 6
Outputs:
- layer_out: float32 [32768, 768], P(('dp', 'tensor'))
- grad_tokens: float32 [32768, 768], P(('dp', 'tensor'))
- grad_qkv_weight: float32 [3, 768, 768], P(None, None, 'tensor')
- grad_qv_bias: float32 [2, 768], P(None, 'tensor')
- grad_out_weight: float32 [768, 768], P('tensor')
- grad_out_bias: float32 [768], replicated
- grad_first_gain: float32 [768], replicated
- grad_first_shift: float32 [768], replicated
- grad_up_weight: float32 [768, 3072], P(None, 'tensor')
- grad_up_bias: float32 [3072], P('tensor')
- grad_down_weight: float32 [3072, 768], P('tensor')
- grad_down_bias: float32 [768], replicated
- grad_second_gain: float32 [768], replicated
- grad_second_shift: float32 [768], replicated
Inputs may be any that keep to these rules, and one draw needn't show every extreme that they name: The valid positions of a sequence are its first lengths[s]; in every draw some sequence has all 512 positions valid.
All inputs are finite; a program needn't handle non-finite values.
Results may differ from a plain program's by a relative error of at most 0.019.
The roundings to bfloat16 on the way count: a program that leaves them out, or rounds other values in their place, can miss the bound.
Values may be sent and summed in bfloat16 or wider, within the bound.
A program may use at most 192 MiB of HBM per device.

v0:
```python
import jax
import jax.numpy as jnp
from jax import lax
from jax.sharding import PartitionSpec as P

HD = 64


EPS = 1e-06


def layer_norm(inputs, gain, shift):
    centre = inputs - jnp.mean(inputs, axis=-1, keepdims=True)
    spread = jnp.mean(centre * centre, axis=-1, keepdims=True)
    return centre * lax.rsqrt(spread + EPS) * gain + shift


def gelu_exact(inputs):
    return jax.nn.gelu(inputs, approximate=False)


def softmax_rows(query_rows, key_block, length, scale):
    scores = (
        jnp.einsum("qhe,khe->hqk", query_rows, key_block, preferred_element_type=jnp.float32)
        * scale
    )
    is_valid = jnp.arange(key_block.shape[0]) < length
    scores = jnp.where(is_valid[None, None, :], scores, -1000000000.0)
    return jax.nn.softmax(scores, axis=-1)


def attend_back(query_rows, key_block, value_block, grad_block, weights, scale):
    grad_probs = jnp.einsum(
        "qhe,khe->hqk", grad_block, value_block, preferred_element_type=jnp.float32
    )
    grad_values = jnp.einsum(
        "hqk,qhe->khe", weights.astype(jnp.bfloat16), grad_block, preferred_element_type=jnp.float32
    )
    row_terms = jnp.sum(weights * grad_probs, axis=-1, keepdims=True)
    grad_scores = (weights * (grad_probs - row_terms)).astype(jnp.bfloat16)
    grad_queries = (
        jnp.einsum("hqk,khe->qhe", grad_scores, key_block, preferred_element_type=jnp.float32)
        * scale
    )
    grad_keys = (
        jnp.einsum("hqk,qhe->khe", grad_scores, query_rows, preferred_element_type=jnp.float32)
        * scale
    )
    return (
        grad_queries.astype(jnp.bfloat16),
        grad_keys.astype(jnp.bfloat16),
        grad_values.astype(jnp.bfloat16),
    )


def body(
    tokens,
    lengths,
    qkv_weight,
    qv_bias,
    out_weight,
    out_bias,
    first_gain,
    first_shift,
    up_weight,
    up_bias,
    down_weight,
    down_bias,
    second_gain,
    second_shift,
    cotangent,
):
    scale = HD ** (-0.5)
    whole_x = lax.all_gather(tokens, "tensor", axis=0, tiled=True)
    row_count = whole_x.shape[0]
    seq_count = lengths.shape[0]
    seq_len = row_count // seq_count
    local_width = qkv_weight.shape[2]
    local_heads = local_width // HD

    def split_heads(matrix):
        return matrix.reshape(seq_count, seq_len, local_heads, HD)

    projected = jnp.einsum("rd,kde->kre", whole_x, qkv_weight, preferred_element_type=jnp.float32)
    queries = (projected[0] + qv_bias[0]).astype(jnp.bfloat16)
    key_rows = projected[1].astype(jnp.bfloat16)
    value_rows = (projected[2] + qv_bias[1]).astype(jnp.bfloat16)
    seq_inputs = (split_heads(queries), split_heads(key_rows), split_heads(value_rows), lengths)

    def attend(element):
        weights = softmax_rows(element[0], element[1], element[3], scale)
        context_block = jnp.einsum(
            "hqk,khe->qhe",
            weights.astype(jnp.bfloat16),
            element[2],
            preferred_element_type=jnp.float32,
        )
        return (context_block.astype(jnp.bfloat16), weights)

    context = lax.map(lambda element: attend(element)[0], seq_inputs)
    context = context.reshape(row_count, local_width)
    attn_sum = lax.psum_scatter(
        jnp.dot(context, out_weight, preferred_element_type=jnp.float32).astype(jnp.bfloat16),
        "tensor",
        scatter_dimension=0,
        tiled=True,
    ).astype(jnp.float32)
    first_in = tokens.astype(jnp.float32) + attn_sum + out_bias
    first_out = layer_norm(first_in, first_gain, first_shift)
    whole_mid = lax.all_gather(first_out.astype(jnp.bfloat16), "tensor", axis=0, tiled=True)
    up_act = jnp.dot(whole_mid, up_weight, preferred_element_type=jnp.float32) + up_bias
    hidden = gelu_exact(up_act).astype(jnp.bfloat16)
    ffn_sum = lax.psum_scatter(
        jnp.dot(hidden, down_weight, preferred_element_type=jnp.float32).astype(jnp.bfloat16),
        "tensor",
        scatter_dimension=0,
        tiled=True,
    ).astype(jnp.float32)
    second_in = first_out + ffn_sum + down_bias
    layer_out = layer_norm(second_in, second_gain, second_shift)
    unused_second, second_back = jax.vjp(layer_norm, second_in, second_gain, second_shift)
    grad_second, grad_second_gain, grad_second_shift = second_back(cotangent.astype(jnp.float32))
    grad_down_bias = jnp.sum(grad_second, axis=0)
    whole_second = lax.all_gather(grad_second.astype(jnp.bfloat16), "tensor", axis=0, tiled=True)
    grad_hidden = jnp.einsum(
        "rd,fd->rf", whole_second, down_weight, preferred_element_type=jnp.float32
    )
    grad_down_weight = jnp.einsum(
        "rf,rd->fd", hidden, whole_second, preferred_element_type=jnp.float32
    )
    unused_gelu, gelu_back = jax.vjp(gelu_exact, up_act)
    grad_up_act = gelu_back(grad_hidden)[0].astype(jnp.bfloat16)
    grad_up_bias = jnp.sum(grad_up_act.astype(jnp.float32), axis=0)
    grad_up_weight = jnp.einsum(
        "rd,rf->df", whole_mid, grad_up_act, preferred_element_type=jnp.float32
    )
    grad_first_out = grad_second + lax.psum_scatter(
        jnp.einsum("rf,df->rd", grad_up_act, up_weight, preferred_element_type=jnp.float32).astype(
            jnp.bfloat16
        ),
        "tensor",
        scatter_dimension=0,
        tiled=True,
    ).astype(jnp.float32)
    unused_first, first_back = jax.vjp(layer_norm, first_in, first_gain, first_shift)
    grad_first, grad_first_gain, grad_first_shift = first_back(grad_first_out)
    grad_out_bias = jnp.sum(grad_first, axis=0)
    whole_first = lax.all_gather(grad_first.astype(jnp.bfloat16), "tensor", axis=0, tiled=True)
    grad_context = jnp.einsum(
        "rd,ed->re", whole_first, out_weight, preferred_element_type=jnp.float32
    ).astype(jnp.bfloat16)
    grad_out_weight = jnp.einsum(
        "re,rd->ed", context, whole_first, preferred_element_type=jnp.float32
    )
    back_inputs = seq_inputs + (split_heads(grad_context),)

    def again(element):
        weights = softmax_rows(element[0], element[1], element[3], scale)
        return attend_back(element[0], element[1], element[2], element[4], weights, scale)

    grad_parts = lax.map(again, back_inputs)
    grad_proj = jnp.stack(
        [
            grad_parts[0].reshape(row_count, local_width),
            grad_parts[1].reshape(row_count, local_width),
            grad_parts[2].reshape(row_count, local_width),
        ]
    )
    grad_qkv_weight = jnp.einsum(
        "rd,kre->kde", whole_x, grad_proj, preferred_element_type=jnp.float32
    )
    grad_qv_bias = jnp.stack(
        [
            jnp.sum(grad_proj[0].astype(jnp.float32), axis=0),
            jnp.sum(grad_proj[2].astype(jnp.float32), axis=0),
        ]
    )
    grad_tokens = grad_first + lax.psum_scatter(
        jnp.einsum("kre,kde->rd", grad_proj, qkv_weight, preferred_element_type=jnp.float32).astype(
            jnp.bfloat16
        ),
        "tensor",
        scatter_dimension=0,
        tiled=True,
    ).astype(jnp.float32)
    (
        grad_qkv_weight,
        grad_qv_bias,
        grad_out_weight,
        grad_up_weight,
        grad_up_bias,
        grad_down_weight,
    ) = lax.psum(
        (
            grad_qkv_weight,
            grad_qv_bias,
            grad_out_weight,
            grad_up_weight,
            grad_up_bias,
            grad_down_weight,
        ),
        "dp",
    )
    small_sums = lax.psum(
        (
            grad_out_bias,
            grad_first_gain,
            grad_first_shift,
            grad_down_bias,
            grad_second_gain,
            grad_second_shift,
        ),
        ("dp", "tensor"),
    )
    return (
        layer_out,
        grad_tokens,
        grad_qkv_weight,
        grad_qv_bias,
        grad_out_weight,
        small_sums[0],
        small_sums[1],
        small_sums[2],
        grad_up_weight,
        grad_up_bias,
        grad_down_weight,
        small_sums[3],
        small_sums[4],
        small_sums[5],
    )


def solution(mesh):
    return jax.shard_map(
        body,
        mesh=mesh,
        in_specs=(
            P(("dp", "tensor"), None),
            P("dp"),
            P(None, None, "tensor"),
            P(None, "tensor"),
            P("tensor", None),
            P(),
            P(),
            P(),
            P(None, "tensor"),
            P("tensor"),
            P("tensor", None),
            P(),
            P(),
            P(),
            P(("dp", "tensor"), None),
        ),
        out_specs=(
            P(("dp", "tensor"), None),
            P(("dp", "tensor"), None),
            P(None, None, "tensor"),
            P(None, "tensor"),
            P("tensor", None),
            P(),
            P(),
            P(),
            P(None, "tensor"),
            P("tensor"),
            P("tensor", None),
            P(),
            P(),
            P(),
        ),
        check_vma=False,
    )
```

profile of v0, /device:TPU:0, one launch (start us, length us, event | category | flops | bytes accessed | tf_op | source)
XLA Modules:
  0.0 877.3 jit_solution(13176357742483971452)
XLA Ops:
  8.9 15.5 %all-gather.5.cloned.1.call-done = bf16[2048,768]{1,0:T(8,128)(2,1)} async-done(((bf16[1024,768]{1,0:T(8,128)(2,1)}), bf16[2048,768]{1,0:T(8,128)(2,1)}) %all-gather.5.cloned.1.call-update) | async-done | bytes 3145744 | tf_op jit(solution)/shard_map/all_gather | solution.py:74
  24.4 6.3 convolution_bitcast_fusion
  30.8 3.1 fusion.151
  35.3 5.7 squeeze.36
  40.9 5.2 squeeze.37
  46.1 3.8 convert_element_type.108
  50.0 3.1 copy.51
  53.1 5.6 fusion.116
  60.0 46.9 %while.24 = (s32[]{:T(128)}, bf16[4,512,6,64]{1,3,2,0:T(8,128)(2,1)}, bf16[4,512,6,64]{1,3,2,0:T(8,128)(2,1)}, s32[4]{0:T(128)S(1)}, bf16[4,512,6,64]{1,3,2,0:T(...) while((s32[]{:T(128)}, bf16[4,512,6,64]{1,3,2,0:T(8,128)(2,1)}, bf16[4,512,6,64]{1,3,2,0:T(8,128)(2,1)}, ...), condition=%wide.region_3.4_spmd, body=%wide.region_0.3_spmd.sunk | while | flops 412288000 | bytes 14183517 | solution.py:100
  61.2 6.1 fusion.197
  67.3 4.4 fusion.198
  72.9 6.1 fusion.197
  79.1 4.4 fusion.198
  84.6 6.1 fusion.197
  90.8 4.4 fusion.198
  96.4 6.1 fusion.197
  102.5 4.4 fusion.198
  111.2 3.5 convolution_convert_fusion
  115.0 12.3 %reduce-scatter.5.cloned.1.call-done = bf16[1024,768]{1,0:T(8,128)(2,1)} async-done(((bf16[2048,768]{1,0:T(8,128)(2,1)}), bf16[1024,768]{1,0:T(8,128)(2,1)}) %reduce-scatter.5.cloned.1.call-update) | async-done | bytes 1572880 | tf_op jit(solution)/shard_map/reduce_scatter | solution.py:102
  133.7 13.5 %all-gather.7.cloned.1.call-done = bf16[2048,768]{1,0:T(8,128)(2,1)} async-done(((bf16[1024,768]{1,0:T(8,128)(2,1)}), bf16[2048,768]{1,0:T(8,128)(2,1)}) %all-gather.7.cloned.1.call-update) | async-done | bytes 3145744 | tf_op jit(solution)/shard_map/all_gather | solution.py:110
  147.2 33.9 %multiply_convert_fusion.1 = (bf16[2048,1536]{1,0:T(8,128)(2,1)S(1)}, f32[2048,1536]{1,0:T(8,128)}, f32[2048,1536]{1,0:T(8,128)}) fusion(f32[1536]{0:T(1024)S(1)} %copy-done.40, bf16[2048,768]{1,0:T(8,128)(2,1)} %all-gather.7.cloned.1.call-done, bf16[768,1536]{1,0:T(8,128)(2,1)S(1)} %copy-done), kind=kOutput, calls=%fused_computation.87 | convolution fusion | flops 5039456256 | bytes 36968448 | tf_op jit(solution)/shard_map/dot_general | solution.py:111
  183.8 6.4 convolution_convert_fusion.2
  190.2 12.4 %reduce-scatter.7.cloned.1.call-done = bf16[1024,768]{1,0:T(8,128)(2,1)} async-done(((bf16[2048,768]{1,0:T(8,128)(2,1)}), bf16[1024,768]{1,0:T(8,128)(2,1)}) %reduce-scatter.7.cloned.1.call-update) | async-done | bytes 1572880 | tf_op jit(solution)/shard_map/reduce_scatter | solution.py:113
  202.6 3.4 fusion.131
  215.4 13.3 %all-gather.9.cloned.1.call-done = bf16[2048,768]{1,0:T(8,128)(2,1)} async-done(((bf16[1024,768]{1,0:T(8,128)(2,1)}), bf16[2048,768]{1,0:T(8,128)(2,1)}) %all-gather.9.cloned.1.call-update) | async-done | bytes 3145744 | tf_op jit(solution)/shard_map/all_gather | solution.py:124
  228.7 17.5 %convert_reduce_fusion = (f32[1536]{0:T(1024)}, bf16[2048,1536]{1,0:T(8,128)(2,1)S(1)}) fusion(f32[2048,1536]{1,0:T(8,128)} %get-tuple-element.215, bf16[2048,768]{1,0:T(8,128)(2,1)} %all-gather.9.cloned.1.call-done, bf16[1536,768]{1,0:T(8,128)(2,1)} %param.29, f32[2048,1536]{1,0:T(8,128)} %get-tuple-element.227, f32[1536]{0:T(1024)S(1)} %copy-done.40), kind=kOutput, calls=%fused_computation.85 | convolution fusion | flops 4885314048 | bytes 36974592 | tf_op jit(solution)/shard_map/rd,fd->rf/dot_general | solution.py:125
  248.8 6.4 convolution_convert_fusion.1
  255.3 12.4 %reduce-scatter.9.cloned.1.call-done = bf16[1024,768]{1,0:T(8,128)(2,1)} async-done(((bf16[2048,768]{1,0:T(8,128)(2,1)}), bf16[1024,768]{1,0:T(8,128)(2,1)}) %reduce-scatter.9.cloned.1.call-update) | async-done | bytes 1572880 | tf_op jit(solution)/shard_map/reduce_scatter | solution.py:137
  267.8 4.8 multiply_reduce_fusion.1
  272.6 3.2 fusion.129
  279.6 13.5 %all-gather.11.cloned.1.call-done = bf16[2048,768]{1,0:T(8,128)(2,1)} async-done(((bf16[1024,768]{1,0:T(8,128)(2,1)}), bf16[2048,768]{1,0:T(8,128)(2,1)}) %all-gather.11.cloned.1.call-update) | async-done | bytes 3145744 | tf_op jit(solution)/shard_map/all_gather | solution.py:148
  293.1 4.9 convolution_convert_fusion.3
  302.5 2.9 copy.55
  308.1 85.3 %while.25 = (s32[]{:T(128)}, bf16[4,512,6,64]{1,3,2,0:T(8,128)(2,1)S(1)}, bf16[4,512,6,64]{1,3,2,0:T(8,128)(2,1)}, bf16[4,512,6,64]{1,3,2,0:T(8,128)(2,1)}, bf16...) while((s32[]{:T(128)}, ...), condition=%wide.region_19.20_spmd, body=%wide.region_15.19_spmd.sunk | while | flops 1028061184 | bytes 70072488 | solution.py:161
  309.4 6.1 fusion.207
  315.5 4.2 multiply_reduce_fusion.6
  322.2 2.8 fusion.209
  326.6 2.9 fusion.210
  330.7 6.1 fusion.207
  336.8 4.2 multiply_reduce_fusion.6
  343.5 2.8 fusion.209
  348.0 2.8 fusion.210
  352.0 6.1 fusion.207
  358.1 4.2 multiply_reduce_fusion.6
  364.8 2.8 fusion.209
  369.3 2.8 fusion.210
  373.4 6.1 fusion.207
  379.5 4.2 multiply_reduce_fusion.6
  390.6 2.8 fusion.210
  395.8 3.8 stack_reshape.9
  402.2 3.8 copy.57
  406.0 3.8 stack_reshape.10
  412.5 3.8 copy.58
  416.3 3.8 stack_reshape.11
  422.7 8.9 %bitcast_convert_fusion = bf16[2048,768]{1,0:T(8,128)(2,1)} fusion(bf16[3,768,384]{2,1,0:T(8,128)(2,1)} %param.21, bf16[1,2048,384]{2,1,0:T(8,128)(2,1)} %copy.61, bf16[1,2048,384]{2,1,0:T(8,128)(2,1)} %copy.60, bf16[1,2048,384]{2,1,0:T(8,128)(2,1)} %copy.59), kind=kOutput, calls=%fused_computation.101 | convolution fusion | flops 3630170112 | bytes 9633792 | tf_op jit(solution)/shard_map/kre,kde->rd/dot_general | solution.py:179
  431.7 9.8 %fusion.154 = f32[1536,768]{1,0:T(8,128)} fusion(bf16[2048,1536]{1,0:T(8,128)(2,1)} %copy-done.43, bf16[2048,768]{1,0:T(8,128)(2,1)} %all-gather.9.cloned.1.call-done), kind=kOutput, calls=%fused_computation.169 | convolution fusion | flops 4831838208 | bytes 14155776 | tf_op jit(solution)/shard_map/rf,rd->fd/dot_general | solution.py:128
  441.5 10.1 %fusion.153 = f32[768,1536]{1,0:T(8,128)} fusion(bf16[2048,768]{1,0:T(8,128)(2,1)S(1)} %copy-done.35, bf16[2048,1536]{1,0:T(8,128)(2,1)} %copy-done.44), kind=kOutput, calls=%fused_computation.168 | convolution fusion | flops 4831838208 | bytes 14155776 | tf_op jit(solution)/shard_map/rd,rf->df/dot_general | solution.py:134
  455.4 5.8 fusion.121
  461.9 45.5 %all-reduce = (f32[768]{0:T(1024)}, f32[768]{0:T(1024)}, f32[768]{0:T(1024)}, f32[768]{0:T(1024)}, f32[768]{0:T(1024)}, /*index=5*/f32[768]{0:T(1024)}) all-reduce(f32[768]{0:T(1024)S(1)} %copy-done.29, f32[768]{0:T(1024)S(1)} %copy-done.23, f32[768]{0:T(1024)S(1)} %copy-done.24, ...), channel_id=1, replica_groups=mesh['dp'=16,'tensor'=2] {'dp','tensor'}, use_global_device_ids=true, to_apply=%region_27.28 | all-reduce | flops 4608 | bytes 36864 | tf_op jit(solution)/shard_map/psum | solution.py:204
  509.6 79.3 %all-reduce.1 = (f32[2,384]{1,0:T(2,128)}, f32[1536]{0:T(1024)}) all-reduce(f32[2,384]{1,0:T(2,128)S(1)} %pad_maximum_fusion.3, f32[1536]{0:T(1024)S(1)} %copy-done.31), channel_id=1, replica_groups=mesh['dp'=16,'tensor'=2] {'dp'}, use_global_device_ids=true, to_apply=%region_24.25 | all-reduce | flops 2304 | bytes 18432 | tf_op jit(solution)/shard_map/psum | solution.py:193
  588.9 4.4 convert_add_fusion
  593.3 263.3 %all-reduce.5.cloned.1.call-done = (f32[3,768,384]{1,2,0:T(8,128)}, f32[384,768]{1,0:T(8,128)}, f32[768,1536]{1,0:T(8,128)}, f32[1536,768]{1,0:T(8,128)}) async-done(((f32[3,768,384]{1,2,0:T(8,128)}, f32[384,768]{1,0:T(8,128)}, f32[768,1536]{1,0:T(8,128)}, f32[1536,768]{1,0:T(8,128)}), (f32[3,768,384]{1,2,0:T(8,128)}, f32[384,768]{1,0:T(8,128)}, f32[768,1536]{1,0:T(8,128)}, ...) | async-done | bytes 14155792 | tf_op jit(solution)/shard_map/psum | solution.py:193
  856.6 5.2 copy.63
  862.9 5.5 copy.106
  (199 shorter events, 90.4 us)
Async XLA Ops:
  7.2 140.0 %copy-start = (bf16[768,1536]{1,0:T(8,128)(2,1)S(1)}, bf16[768,1536]{1,0:T(8,128)(2,1)}, u32[]{:S(2)}) copy-start(bf16[768,1536]{1,0:T(8,128)(2,1)} %param.27) | copy-start | bytes 7077892
  7.2 17.2 %all-gather.5.cloned.1.call-start = ((), (), s32[]{:S(2)}) async-start(), calls=%async_computation.4 | async-start | bytes 4718592 | tf_op jit(solution)/shard_map/all_gather | solution.py:74
  7.9 119.3 %reduce-scatter.5.cloned.1.call-start = ((), (), s32[]{:S(2)}) async-start(), calls=%async_computation.5 | async-start | bytes 4718592 | tf_op jit(solution)/shard_map/reduce_scatter | solution.py:102
  50.0 3.1 copy-start.8
  53.1 6.9 copy-start.41
  106.9 4.4 copy-start.38
  110.0 1.2 copy-start.11
  114.7 12.5 %copy-start.17 = (f32[768]{0:T(1024)S(1)}, f32[768]{0:T(1024)}, u32[]{:S(2)}) copy-start(f32[768]{0:T(1024)} %param.24) | copy-start | bytes 9220
  114.8 16.8 %copy-start.18 = (f32[768]{0:T(1024)S(1)}, f32[768]{0:T(1024)}, u32[]{:S(2)}) copy-start(f32[768]{0:T(1024)} %param.25) | copy-start | bytes 9220
  114.8 16.8 %copy-start.30 = (f32[768]{0:T(1024)S(1)}, f32[768]{0:T(1024)}, u32[]{:S(2)}) copy-start(f32[768]{0:T(1024)} %param.26) | copy-start | bytes 9220
  114.8 32.4 %all-gather.7.cloned.1.call-start = ((), (), s32[]{:S(2)}) async-start(), calls=%async_computation.6 | async-start | bytes 4718592 | tf_op jit(solution)/shard_map/all_gather | solution.py:110
  127.3 2.6 copy-start.2
  127.3 2.8 copy-start.4
  131.0 0.6 copy-start.21
  131.6 15.6 %copy-start.40 = (f32[1536]{0:T(1024)S(1)}, f32[1536]{0:T(1024)}, u32[]{:S(2)}) copy-start(f32[1536]{0:T(1024)} %param.28) | copy-start | bytes 18436
  133.7 69.0 %reduce-scatter.7.cloned.1.call-start = ((), (), s32[]{:S(2)}) async-start(), calls=%async_computation.7 | async-start | bytes 4718592 | tf_op jit(solution)/shard_map/reduce_scatter | solution.py:113
  147.2 36.6 %copy-start.37 = (bf16[1536,768]{1,0:T(8,128)(2,1)S(1)}, bf16[1536,768]{1,0:T(8,128)(2,1)}, u32[]{:S(2)}) copy-start(bf16[1536,768]{1,0:T(8,128)(2,1)} %param.29) | copy-start | bytes 7077892
  181.1 2.7 copy-start.43
  190.1 12.5 %copy-start.32 = (f32[768]{0:T(1024)S(1)}, f32[768]{0:T(1024)}, u32[]{:S(2)}) copy-start(f32[768]{0:T(1024)} %param.30) | copy-start | bytes 9220
  190.2 38.5 %all-gather.9.cloned.1.call-start = ((), (), s32[]{:S(2)}) async-start(), calls=%async_computation.8 | async-start | bytes 4718592 | tf_op jit(solution)/shard_map/all_gather | solution.py:124
  206.0 1.4 copy-start.9
  206.0 1.4 copy-start.26
  206.6 2.7 copy-start.33
  212.0 1.7 copy-start.5
  215.1 52.6 %reduce-scatter.9.cloned.1.call-start = ((), (), s32[]{:S(2)}) async-start(), calls=%async_computation.9 | async-start | bytes 4718592 | tf_op jit(solution)/shard_map/reduce_scatter | solution.py:137
  246.2 2.7 copy-start.44
  255.3 12.5 %copy-start.3 = (bf16[1024,768]{1,0:T(8,128)(2,1)S(1)}, bf16[1024,768]{1,0:T(8,128)(2,1)}, u32[]{:S(2)}) copy-start(bf16[1024,768]{1,0:T(8,128)(2,1)} %param.19) | copy-start | bytes 4718596
  255.3 17.3 %copy-start.22 = (f32[1024]{0:T(1024)S(1)}, f32[1024]{0:T(1024)}, u32[]{:S(2)}) copy-start(f32[1024]{0:T(1024)} %copy-done.21) | copy-start | bytes 12292
  255.3 37.8 %all-gather.11.cloned.1.call-start = ((), (), s32[]{:S(2)}) async-start(), calls=%async_computation.10 | async-start | bytes 4718592 | tf_op jit(solution)/shard_map/all_gather | solution.py:148
  267.8 4.8 copy-start.6
  267.8 4.8 copy-start.10
  275.8 1.6 copy-start.7
  275.8 3.7 copy-start.19
  277.4 15.6 %copy-start.39 = (bf16[384,768]{1,0:T(8,128)(2,1)S(1)}, bf16[384,768]{1,0:T(8,128)(2,1)}, u32[]{:S(2)}) copy-start(bf16[384,768]{1,0:T(8,128)(2,1)} %param.23) | copy-start | bytes 1769476
  279.5 309.3 %reduce-scatter.11.cloned.1.call-start = ((), (), s32[]{:S(2)}) async-start(), calls=%async_computation.11 | async-start | bytes 4718592 | tf_op jit(solution)/shard_map/reduce_scatter | solution.py:178
  305.4 2.8 copy-start.42
  315.5 4.2 slice-start
  315.5 4.9 slice-start.1
  336.8 4.2 slice-start
  336.8 4.9 slice-start.1
  358.1 4.2 slice-start
  358.1 4.9 slice-start.1
  379.5 4.2 slice-start
  379.5 4.9 slice-start.1
  431.7 424.9 %all-reduce.5.cloned.1.call-start = ((), (), s32[]{:S(2)}) async-start(), calls=%async_computation.12 | async-start | bytes 28311552 | tf_op jit(solution)/shard_map/psum | solution.py:193
  431.7 9.8 %copy-start.35 = (bf16[2048,768]{1,0:T(8,128)(2,1)S(1)}, bf16[2048,768]{1,0:T(8,128)(2,1)}, u32[]{:S(2)}) copy-start(bf16[2048,768]{1,0:T(8,128)(2,1)} %all-gather.7.cloned.1.call-done) | copy-start | bytes 9437188
  441.5 10.1 %copy-start.12 = (bf16[48,8,4,512]{3,1,2,0:T(8,128)(2,1)S(1)}, bf16[48,8,4,512]{3,1,2,0:T(8,128)(2,1)}, u32[]{:S(2)}) copy-start(bf16[48,8,4,512]{3,1,2,0:T(8,128)(2,1)} %copy-done.11) | copy-start | bytes 4718596
  441.5 10.1 %copy-start.36 = (bf16[2048,768]{1,0:T(8,128)(2,1)S(1)}, bf16[2048,768]{1,0:T(8,128)(2,1)}, u32[]{:S(2)}) copy-start(bf16[2048,768]{1,0:T(8,128)(2,1)} %all-gather.11.cloned.1.call-done) | copy-start | bytes 9437188
  451.6 2.5 copy-start.13
  451.6 2.4 copy-start.14
  451.6 2.4 copy-start.15
  451.7 3.7 copy-start.34
  461.1 0.7 copy-start.23
  461.1 0.7 copy-start.24
  461.1 0.7 copy-start.25
  461.1 0.7 copy-start.27
  461.1 0.7 copy-start.28
  461.2 0.7 copy-start.29
  461.2 48.4 %copy-start.31 = (f32[1536]{0:T(1024)S(1)}, f32[1536]{0:T(1024)}, u32[]{:S(2)}) copy-start(f32[1536]{0:T(1024)} %get-tuple-element.228) | copy-start | bytes 18436
  461.2 127.6 %copy-start.20 = (f32[1024]{0:T(1024)S(1)}, f32[1024]{0:T(1024)}, u32[]{:S(2)}) copy-start(f32[1024]{0:T(1024)} %copy-done.19) | copy-start | bytes 12292
  856.6 5.3 copy-start.16
  861.9 6.5 slice-start.2
  862.9 5.5 slice-start.3
  862.9 7.7 copy-start.1
Sparse Core Ops, SparseCore 0:
  9.5 14.8 all-gather.4
  114.9 12.3 reduce-scatter.4
  133.8 13.3 all-gather.6
  190.3 12.2 reduce-scatter.6
  215.2 13.3 all-gather.8
  255.4 12.3 reduce-scatter.8
  279.6 13.3 all-gather.10
  431.8 12.3 reduce-scatter.10
  461.3 395.2 all-reduce.4
where the time goes:
time: 883 us; the launch traced here: 877 us
  waiting for transfers between devices  357 us (40%)
  matrix products  228 us (26%)
  blocking collectives  125 us (14%)
  local copies, waits for them, and re-layouts  102 us (12%)
  other arithmetic  49.9 us (6%)
  between operations  14.4 us (2%)
    psum x1, waiting for transfers between devices, body(): lax.psum((grad_qkv_weight, grad_qv_bias, grad_out_weight, grad_up_weight,...  263 us
    psum x1, blocking collectives, body(): lax.psum((grad_qkv_weight, grad_qv_bias, grad_out_weight, grad_up_weight,...  79.3 us
    sub x8, matrix products, softmax_rows(): return jax.nn.softmax(scores, axis=-1)  48.9 us
    psum x1, blocking collectives, body(): lax.psum((grad_out_bias, grad_first_gain, grad_first_shift, grad_down_bia...  45.5 us
    dot_general x1, matrix products, body(): jnp.dot(whole_mid, up_weight, preferred_element_type=jnp.float32) + up_bias  33.9 us
    unnamed x99, local copies, waits for them, and re-layouts  28 us
    another operation x6, local copies, waits for them, and re-layouts, body(): jnp.stack([grad_parts[0].reshape(row_count, local_width), grad_parts[1].r...  19.4 us
  transfers between devices with their start and end apart: 9, of which 8 were waited for; matrix products, arithmetic and copies ran while one was open for 4% of the time, Pallas kernels for 0%

commit v1 on v0

v1 whole, which is shorter than its diff:
```python
import functools

import jax
import jax.numpy as jnp
from jax import lax
from jax.experimental import pallas as pl
from jax.experimental.pallas import tpu as pltpu
from jax.sharding import PartitionSpec as P

HD = 64
EPS = 1e-06
BF = jnp.bfloat16
F32 = jnp.float32
NEG = -1000000000.0
JR, JC = 256, 384


def dot(a, b):
    return lax.dot_general(a, b, (((1,), (0,)), ((), ())), preferred_element_type=F32)


def dot_nt(a, b):
    return lax.dot_general(a, b, (((1,), (1,)), ((), ())), preferred_element_type=F32)


def dot_tn(a, b):
    return lax.dot_general(a, b, (((0,), (0,)), ((), ())), preferred_element_type=F32)


def half_masks(shape, dim):
    low = lax.broadcasted_iota(jnp.int32, shape, dim) % (2 * HD) < HD
    return low


def attn_kernel(qb, lens_ref, x_ref, w_ref, b_ref, q_ref, k_ref, v_ref, c_ref):
    length = lens_ref[pl.program_id(0)]
    x = x_ref[...]
    rows, width = q_ref.shape
    scale = HD ** (-0.5)
    q_ref[...] = (dot(x, w_ref[0]) + b_ref[0:1, :]).astype(BF) * jnp.asarray(scale, BF)
    k_ref[...] = dot(x, w_ref[1]).astype(BF)
    v_ref[...] = (dot(x, w_ref[2]) + b_ref[1:2, :]).astype(BF)
    for pair in range(width // 128):
        lanes = slice(pair * 128, pair * 128 + 128)
        k = k_ref[:, lanes]
        v_t = v_ref[:, lanes].T
        for block in range(rows // qb):
            span = slice(block * qb, block * qb + qb)
            q = q_ref[span, lanes]
            low = half_masks(q.shape, 1)
            zero = jnp.zeros_like(q)
            parts = []
            for head in range(2):
                q_head = jnp.where(low, q, zero) if head == 0 else jnp.where(low, zero, q)
                s = dot_nt(k, q_head)
                is_valid = lax.broadcasted_iota(jnp.int32, s.shape, 0) < length
                s = jnp.where(is_valid, s, NEG)
                top = jnp.max(s, axis=0, keepdims=True)
                e = jnp.exp(s - top)
                total = jnp.sum(e, axis=0, keepdims=True)
                c_t = dot(v_t[head * HD:(head + 1) * HD], e.astype(BF))
                parts.append(c_t * (1.0 / total))
            c_ref[span, lanes] = jnp.concatenate(parts, axis=0).T.astype(BF)


def attention(lens, x, weight, bias, qb=256):
    rows, depth = x.shape
    seqs = lens.shape[0]
    seq_len = rows // seqs
    width = weight.shape[2]
    row_spec = pl.BlockSpec((seq_len, width), lambda s, _: (s, 0))
    out = jax.ShapeDtypeStruct((rows, width), BF)
    flops = 2 * rows * depth * width * 3 + 4 * rows * seq_len * width
    return pl.pallas_call(
        functools.partial(attn_kernel, qb),
        out_shape=(out, out, out, out),
        grid_spec=pltpu.PrefetchScalarGridSpec(
            num_scalar_prefetch=1,
            grid=(seqs,),
            in_specs=[
                pl.BlockSpec((seq_len, depth), lambda s, _: (s, 0)),
                pl.BlockSpec(weight.shape, lambda s, _: (0, 0, 0)),
                pl.BlockSpec(bias.shape, lambda s, _: (0, 0)),
            ],
            out_specs=[row_spec] * 4,
        ),
        compiler_params=pltpu.CompilerParams(vmem_limit_bytes=56 << 20),
        cost_estimate=pl.CostEstimate(flops=flops * 3, bytes_accessed=12 << 20, transcendentals=rows * seq_len * width // HD),
        name="attend",
    )(lens, x, weight, bias)


def norm_stats(rows_in):
    centre = rows_in - jnp.mean(rows_in, axis=-1, keepdims=True)
    spread = jnp.mean(centre * centre, axis=-1, keepdims=True)
    root = lax.rsqrt(spread + EPS)
    return centre * root, root


def norm_back(grad, normed, root):
    first = jnp.mean(grad, axis=-1, keepdims=True)
    second = jnp.mean(grad * normed, axis=-1, keepdims=True)
    return root * (grad - first - normed * second)


def gelu_both(u):
    z = jnp.abs(u) * (0.5 ** 0.5)
    t = 1.0 / (1.0 + 0.3275911 * z)
    poly = 1.061405429 * t - 1.453152027
    poly = poly * t + 1.421413741
    poly = poly * t - 0.284496736
    poly = poly * t + 0.254829592
    bell = jnp.exp(-0.5 * (u * u))
    tail = 0.5 * (poly * t) * bell
    phi_cdf = jnp.where(u < 0.0, tail, 1.0 - tail)
    return u * phi_cdf, phi_cdf + u * (bell * 0.3989422804014327)


def ffn_kernel(
    chunk,
    c_own, c_peer, x_ref, cot_ref, wo_own, wo_peer, wu_own, wu_peer, bu_own, bu_peer, wd_own, wd_peer, vec_ref,
    out_ref, h_own, h_peer, gu_own, gu_peer, mid_ref, glow_ref, flow_ref, gctx_ref, gf_ref, small_ref,
    gp_ref,
):
    step = pl.program_id(0)
    wide = wu_own.shape[1]
    out_bias, gain1, shift1, down_bias, gain2, shift2 = (vec_ref[i:i + 1, :] for i in range(6))

    @pl.when(step == 0)
    def _():
        small_ref[...] = jnp.zeros_like(small_ref)

    def colsum(index, value):
        small_ref[index:index + 1, :] += jnp.sum(value, axis=0, keepdims=True)

    attn_sum = dot(c_own[...], wo_own[...]) + dot(c_peer[...], wo_peer[...])
    n1, root1 = norm_stats(x_ref[...].astype(F32) + attn_sum + out_bias)
    first_out = n1 * gain1 + shift1
    middle = first_out.astype(BF)
    mid_ref[...] = middle
    ffn_sum = jnp.zeros_like(first_out)
    groups = ((wu_own, bu_own, wd_own, h_own, gu_own, 0), (wu_peer, bu_peer, wd_peer, h_peer, gu_peer, wide))
    for wu, bu, wd, h_ref, _, base in groups:
        for at in range(0, wide, chunk):
            cols = slice(at, at + chunk)
            u = dot(middle, wu[:, cols]) + bu[:, cols]
            act, slope = gelu_both(u)
            act = act.astype(BF)
            h_ref[:, cols] = act
            gp_ref[:, base + at:base + at + chunk] = slope
            ffn_sum = ffn_sum + dot(act, wd[cols, :])
    n2, root2 = norm_stats(first_out + ffn_sum + down_bias)
    out_ref[...] = n2 * gain2 + shift2
    cot = cot_ref[...].astype(F32)
    colsum(4, cot * n2)
    colsum(5, cot)
    grad_second = norm_back(cot * gain2, n2, root2)
    colsum(3, grad_second)
    glow = grad_second.astype(BF)
    glow_ref[...] = glow
    grad_first_out = grad_second
    for wu, _, wd, _, gu_ref, base in groups:
        for at in range(0, wide, chunk):
            cols = slice(at, at + chunk)
            grad_hidden = dot_nt(glow, wd[cols, :])
            gu = (grad_hidden * gp_ref[:, base + at:base + at + chunk]).astype(BF)
            gu_ref[:, cols] = gu
            colsum(8 + (base + at) // chunk, gu.astype(F32))
            grad_first_out = grad_first_out + dot_nt(gu, wu[:, cols])
    colsum(1, grad_first_out * n1)
    colsum(2, grad_first_out)
    grad_first = norm_back(grad_first_out * gain1, n1, root1)
    colsum(0, grad_first)
    gf_ref[...] = grad_first
    flow = grad_first.astype(BF)
    flow_ref[...] = flow
    half = wo_own.shape[0]
    gctx_ref[:, :half] = dot_nt(flow, wo_own[...]).astype(BF)
    gctx_ref[:, half:] = dot_nt(flow, wo_peer[...]).astype(BF)


def ffn(c_own, c_peer, x, cot, wo_own, wo_peer, wu_own, wu_peer, bu_own, bu_peer, wd_own, wd_peer, vecs, tile=256):
    rows, depth = x.shape
    half = c_own.shape[1]
    wide = wu_own.shape[1]
    chunk = depth

    def tiled(cols):
        return pl.BlockSpec((tile, cols), lambda i: (i, 0))

    def fixed(shape):
        return pl.BlockSpec(shape, lambda i: (0, 0), pipeline_mode=pl.Buffered(1))

    def sds(cols, dtype):
        return jax.ShapeDtypeStruct((rows, cols), dtype)

    fixed_in = (wo_own, wo_peer, wu_own, wu_peer, bu_own, bu_peer, wd_own, wd_peer, vecs)
    return pl.pallas_call(
        functools.partial(ffn_kernel, chunk),
        grid=(rows // tile,),
        out_shape=(
            sds(depth, F32), sds(wide, BF), sds(wide, BF), sds(wide, BF), sds(wide, BF),
            sds(depth, BF), sds(depth, BF), sds(depth, BF), sds(2 * half, BF), sds(depth, F32),
            jax.ShapeDtypeStruct((16, depth), F32),
        ),
        in_specs=[tiled(half), tiled(half), tiled(depth), tiled(depth)] + [fixed(a.shape) for a in fixed_in],
        out_specs=[
            tiled(depth), tiled(wide), tiled(wide), tiled(wide), tiled(wide),
            tiled(depth), tiled(depth), tiled(depth), tiled(2 * half), tiled(depth),
            pl.BlockSpec((16, depth), lambda i: (0, 0)),
        ],
        scratch_shapes=[pltpu.VMEM((tile, 2 * wide), F32)],
        compiler_params=pltpu.CompilerParams(vmem_limit_bytes=60 << 20),
        cost_estimate=pl.CostEstimate(flops=rows * depth * (8 * 2 * wide + 8 * depth), bytes_accessed=48 << 20, transcendentals=rows * wide * 2),
        name="feed",
    )(c_own, c_peer, x, cot, *fixed_in)


LAGS = (1, 3, 5, 6, 8, 10, 11, 12, 14)
GROUPS = 12
JOBS = 3 * GROUPS


def back_kernel(
    levels,
    lens_ref, h_own, h_peer, gu_own, gu_peer, glow_in, mid_in, flow_in, c_own, c_peer, q_own, q_peer, k_own, k_peer, v_own, v_peer, gctx_in, x_in, w_own, w_peer, small_in,
    job_out, dx_out, small_out,
    buf, ring, prec, rbuf, blocks, glow, mid, flow, ctx, qv, kv, vv, dov, xv, wv, dq, dk, dv, dxs, small, small_sum, small_send, small_recv,
    load_sem, blk_sem, core_send, core_recv, hop_send, hop_recv, out_sem, dx_sem, small_sem, sum_send, sum_recv,
):
    dp = lax.axis_index("dp")
    core = lax.axis_index("tensor")
    half = ctx.shape[1] // 2
    rows, depth = glow.shape
    seqs = lens_ref.shape[0]
    seq_len = rows // seqs
    pairs = qv.shape[1] // 128
    scale = HD ** (-0.5)
    other = (dp, 1 - core)

    def partner(level, job):
        flip = job % 2
        mask = (1 + flip, 4, 2 - flip, 8)[level]
        bit = (dp // mask) % 2
        return bit, (dp + mask * (1 - 2 * bit), core)

    def loads():
        return (
            (glow_in, glow, 0), (mid_in, mid, 1), (c_own, ctx.at[:, :half], 2), (c_peer, ctx.at[:, half:], 3), (flow_in, flow, 4),
            (q_own, qv.at[:, :half], 5), (q_peer, qv.at[:, half:], 6), (k_own, kv.at[:, :half], 7), (k_peer, kv.at[:, half:], 8),
            (v_own, vv.at[:, :half], 9), (v_peer, vv.at[:, half:], 10), (gctx_in, dov, 11), (x_in, xv, 12), (w_own, wv.at[0], 13), (w_peer, wv.at[1], 14), (small_in, small, 15),
        )

    def load(index):
        src, dst, sem = loads()[index]
        return pltpu.make_async_copy(src, dst, load_sem.at[sem])

    def block_copies(src_own, src_peer, index, slot):
        cols = pl.ds(pl.multiple_of(index * JC, 128), JC)
        return (
            pltpu.make_async_copy(src_own.at[:, cols], blocks.at[slot, 0], blk_sem.at[slot, 0]),
            pltpu.make_async_copy(src_peer.at[:, cols], blocks.at[slot, 1], blk_sem.at[slot, 1]),
        )

    def start_blocks(index):
        @pl.when(index < 4)
        def _():
            for copy in block_copies(h_own, h_peer, index, index % 2):
                copy.start()

        @pl.when((index >= 4) & (index < 8))
        def _():
            for copy in block_copies(gu_own, gu_peer, index - 4, index % 2):
                copy.start()

    def core_copy(job):
        return pltpu.make_async_remote_copy(
            src_ref=ring.at[job % 9], dst_ref=prec.at[job], send_sem=core_send.at[job], recv_sem=core_recv.at[job],
            device_id=other, device_id_type=pl.DeviceIdType.MESH,
        )

    def offsets(job):
        spots = [0]
        for level in range(levels):
            bit, _ = partner(level, job)
            spots.append(spots[-1] + bit * (JR >> (level + 1)))
        return spots

    def hop(job, stage):
        if stage < levels:
            level = stage
            size = JR >> (level + 1)
            bit, device = partner(level, job)
            at = pl.multiple_of(offsets(job)[level] + (1 - bit) * size, 16)
            src = buf.at[job, pl.ds(at, size)]
            begin = JR - (JR >> level)
            dst = rbuf.at[job, begin:begin + size]
        else:
            level = 2 * levels - 1 - stage
            size = JR >> (level + 1)
            bit, device = partner(level, job)
            at = pl.multiple_of(offsets(job)[level + 1], 16)
            src = prec.at[job, pl.ds(at, size)]
            dst = prec.at[job, pl.ds(at, size)]
        return pltpu.make_async_remote_copy(
            src_ref=src, dst_ref=dst, send_sem=hop_send.at[stage, job], recv_sem=hop_recv.at[stage, job],
            device_id=device, device_id_type=pl.DeviceIdType.MESH,
        )

    def stage_op(stage, job):
        if stage == 0:
            core_copy(job).wait_recv()
            buf[job] = (buf[job].astype(F32) + prec[job].astype(F32)).astype(BF)
            hop(job, 0).start()
            return
        before = hop(job, stage - 1)
        before.wait_recv()
        before.wait_send()
        if stage <= levels:
            level = stage - 1
            size = JR >> stage
            at = pl.multiple_of(offsets(job)[stage], 16)
            begin = JR - (JR >> level)
            keep = buf[job, pl.ds(at, size)].astype(F32) + rbuf[job, begin:begin + size].astype(F32)
            target = prec if stage == levels else buf
            target[job, pl.ds(at, size)] = keep.astype(BF)
        if stage < 2 * levels:
            hop(job, stage).start()
        else:
            pltpu.make_async_copy(prec.at[job], job_out.at[job], out_sem.at[job]).start()

    def emit(group, own, peer):
        for which, pieces in ((0, own), (1, peer)):
            for i, (top, bottom) in enumerate(pieces):
                job = group * 3 + i
                if which == 0:
                    target = buf.at[job]
                else:
                    target = ring.at[job % 9]
                cut = top.shape[0]
                target[:cut, :] = top.astype(BF)
                if bottom is not None:
                    target[cut:, :] = bottom.astype(BF)
                if which == 1:
                    core_copy(job).start()

    def free_ring(group):
        @pl.when(group >= 3)
        def _():
            for i in range(3):
                core_copy((group - 3) * 3 + i).wait_send()

    def slabs(block):
        return [(block[i * 128:(i + 1) * 128, :JC], block[i * 128:(i + 1) * 128, JC:]) for i in range(3)]

    def tall(block):
        return [(block[i * JR:(i + 1) * JR], None) for i in range(3)]

    def down_phase(index):
        @pl.when(index == 0)
        def _():
            load(0).wait()

        for copy in block_copies(h_own, h_peer, index, index % 2):
            copy.wait()
        free_ring(index)
        right = glow[...]
        slot = index % 2
        emit(index, slabs(dot_tn(blocks[slot, 0], right)), slabs(dot_tn(blocks[slot, 1], right)))
        start_blocks(index + 2)

    def up_phase(index):
        @pl.when(index == 0)
        def _():
            load(1).wait()

        slot = index % 2
        for copy in block_copies(gu_own, gu_peer, index, slot):
            copy.wait()
        free_ring(index + 4)
        left = mid[...]
        emit(index + 4, tall(dot_tn(left, blocks[slot, 0])), tall(dot_tn(left, blocks[slot, 1])))
        start_blocks(index + 6)

    def out_phase():
        for i in (2, 3, 4):
            load(i).wait()
        free_ring(8)
        right = flow[...]
        emit(8, slabs(dot_tn(ctx[:, :half], right)), slabs(dot_tn(ctx[:, half:], right)))

    def add_bias(pair, offset, value):
        total = jnp.sum(value.astype(F32), axis=0, keepdims=True)
        for side in range(2):
            @pl.when(pair // (pairs // 2) == side)
            def _():
                lanes = pl.ds(pl.multiple_of(offset + (pair - side * (pairs // 2)) * 128, 128), 128)
                small[12 + side:13 + side, lanes] += total

    def sum_hop(stage):
        if stage == 0:
            src, device = small_send, other
        else:
            src, device = small_sum.at[stage - 1], partner(stage - 1, 0)[1]
        return pltpu.make_async_remote_copy(
            src_ref=src, dst_ref=small_recv.at[stage], send_sem=sum_send.at[stage], recv_sem=sum_recv.at[stage],
            device_id=device, device_id_type=pl.DeviceIdType.MESH,
        )

    def sum_phase(stage):
        if stage == 0:
            small_send[0:8, :] = small[0:8, :]
            small_send[8:10, :] = small[10:12, :]
            small_send[10:11, :] = small[13:14, :]
            small_send[11:16, :] = jnp.zeros((5, depth), F32)
        else:
            sum_hop(stage - 1).wait_recv()
            sum_hop(stage - 1).wait_send()
            if stage == 1:
                got = small_recv[0]
                small_sum[0, 0:8, :] = small[0:8, :] + got[0:8, :]
                small_sum[0, 8:10, :] = small[8:10, :] + got[8:10, :]
                small_sum[0, 10:11, :] = small[12:13, :] + got[10:11, :]
                small_sum[0, 11:16, :] = jnp.zeros((5, depth), F32)
            else:
                small_sum[stage - 1] = small_sum[stage - 2] + small_recv[stage - 1]
        if stage <= levels:
            sum_hop(stage).start()
        else:
            pltpu.make_async_copy(small_sum.at[levels], small_out, small_sem).start()

    def attend_phase(unit):
        @pl.when(unit == 0)
        def _():
            for i in range(5, 12):
                load(i).wait()
            load(15).wait()
            small[12:14, :] = jnp.zeros((2, depth), F32)

        seq = unit // pairs
        pair = unit % pairs
        length = lens_ref[seq]
        span = pl.ds(pl.multiple_of(seq * seq_len, seq_len), seq_len)
        lanes = pl.ds(pl.multiple_of(pair * 128, 128), 128)
        k = kv[span, lanes]
        v = vv[span, lanes]
        k_t = k.T
        low = half_masks((1, 128), 1)
        qb = seq_len // 2
        grad_k = jnp.zeros((seq_len, 128), F32)
        grad_v = jnp.zeros((seq_len, 128), F32)
        for block in range(2):
            part = pl.ds(pl.multiple_of(seq * seq_len + block * qb, qb), qb)
            q = qv[part, lanes]
            do = dov[part, lanes]
            grad_q = []
            for head in range(2):
                pick = low if head == 0 else jnp.logical_not(low)
                q_head = jnp.where(pick, q, jnp.zeros_like(q))
                do_head = jnp.where(pick, do, jnp.zeros_like(do))
                s = dot_nt(k, q_head)
                is_valid = lax.broadcasted_iota(jnp.int32, s.shape, 0) < length
                s = jnp.where(is_valid, s, NEG)
                e = jnp.exp(s - jnp.max(s, axis=0, keepdims=True))
                weights = e * (1.0 / jnp.sum(e, axis=0, keepdims=True))
                grad_probs = dot_nt(v, do_head)
                grad_v = grad_v + dot(weights.astype(BF), do_head)
                row_terms = jnp.sum(weights * grad_probs, axis=0, keepdims=True)
                grad_s = (weights * (grad_probs - row_terms)).astype(BF)
                grad_k = grad_k + dot(grad_s, q_head)
                grad_q.append(dot(k_t[head * HD:(head + 1) * HD], grad_s) * scale)
            grad_q = jnp.concatenate(grad_q, axis=0).T.astype(BF)
            dq[part, lanes] = grad_q
            add_bias(pair, 0, grad_q)
        grad_v = grad_v.astype(BF)
        dk[span, lanes] = grad_k.astype(BF)
        dv[span, lanes] = grad_v
        add_bias(pair, half, grad_v)

    def proj_phase(index):
        if index == 0:
            load(12).wait()
        free_ring(jnp.int32(index + 9))
        left = xv[...]
        grad = (dq, dk, dv)[index]
        emit(index + 9, tall(dot_tn(left, grad[:, :half])), tall(dot_tn(left, grad[:, half:])))

    def dx_copy(index):
        span = pl.ds(pl.multiple_of(index * JR, JR), JR)
        return pltpu.make_async_copy(dxs.at[index % 2], dx_out.at[span], dx_sem.at[index % 2])

    def dx_phase(index):
        @pl.when(index == 0)
        def _():
            load(13).wait()
            load(14).wait()

        @pl.when(index >= 2)
        def _():
            dx_copy(index - 2).wait()

        span = pl.ds(pl.multiple_of(index * JR, JR), JR)
        total = jnp.zeros((JR, depth), F32)
        for side in range(2):
            cols = slice(side * half, side * half + half)
            part = jnp.zeros((JR, depth), F32)
            for i, grad in enumerate((dq, dk, dv)):
                part = part + dot_nt(grad[span, cols], wv[side, i])
            total = total + part
        dxs[index % 2] = total
        dx_copy(index).start()

    barrier = pltpu.get_barrier_semaphore()
    pl.semaphore_signal(barrier, inc=1, device_id=other, device_id_type=pl.DeviceIdType.MESH)
    for level in range(levels):
        pl.semaphore_signal(barrier, inc=1, device_id=partner(level, 0)[1], device_id_type=pl.DeviceIdType.MESH)
    load(0).start()
    start_blocks(0)
    start_blocks(1)
    for i in range(1, 16):
        load(i).start()
    pl.semaphore_wait(barrier, levels + 1)

    units = seqs * pairs
    first = 9 + units
    ticks = max(JOBS + LAGS[2 * levels], first + 3 + rows // JR)

    def tick(t, carry):
        for stage in range(2 * levels, -1, -1):
            job = t - LAGS[stage]

            @pl.when((job >= 0) & (job < JOBS))
            def _():
                stage_op(stage, job)

        @pl.when(t < 4)
        def _():
            down_phase(t)

        @pl.when((t >= 4) & (t < 8))
        def _():
            up_phase(t - 4)

        @pl.when(t == 8)
        def _():
            out_phase()

        @pl.when((t >= 9) & (t < first))
        def _():
            attend_phase(t - 9)

        for i in range(3):
            @pl.when(t == first + i)
            def _():
                proj_phase(i)

        @pl.when((t >= first + 3) & (t < first + 3 + rows // JR))
        def _():
            dx_phase(t - first - 3)

        for stage in range(levels + 2):
            @pl.when(t == first + 1 + 2 * stage)
            def _():
                sum_phase(stage)

        return carry

    lax.fori_loop(0, ticks, tick, 0)
    for group in (GROUPS - 3, GROUPS - 2, GROUPS - 1):
        for i in range(3):
            core_copy(group * 3 + i).wait_send()
    dx_copy(rows // JR - 2).wait()
    dx_copy(rows // JR - 1).wait()

    def finish(job, carry):
        pltpu.make_async_copy(prec.at[job], job_out.at[job], out_sem.at[job]).wait()
        return carry

    lax.fori_loop(0, JOBS, finish, 0)
    pltpu.make_async_copy(small_sum.at[levels], small_out, small_sem).wait()


def backward(levels, lens, arrays):
    h_own, glow, c_own, x = arrays[0], arrays[4], arrays[7], arrays[16]
    rows, depth = glow.shape
    half = c_own.shape[1]
    hbm = pl.BlockSpec(memory_space=pl.ANY)
    square = pltpu.VMEM((rows, depth), BF)
    dma = pltpu.SemaphoreType.DMA
    return pl.pallas_call(
        functools.partial(back_kernel, levels),
        out_shape=(
            jax.ShapeDtypeStruct((JOBS, JR, JC), BF),
            jax.ShapeDtypeStruct((rows, depth), F32),
            jax.ShapeDtypeStruct((16, depth), F32),
        ),
        in_specs=[pl.BlockSpec(memory_space=pltpu.SMEM)] + [hbm] * len(arrays),
        out_specs=(hbm, hbm, hbm),
        scratch_shapes=[
            pltpu.VMEM((JOBS, JR, JC), BF), pltpu.VMEM((9, JR, JC), BF), pltpu.VMEM((JOBS, JR, JC), BF),
            pltpu.VMEM((JOBS, JR - (JR >> levels), JC), BF), pltpu.VMEM((2, 2, rows, JC), BF),
            square, square, square, square, square, square, square, square, square,
            pltpu.VMEM((2, 3, depth, half), BF), square, square, square,
            pltpu.VMEM((2, JR, depth), F32), pltpu.VMEM((16, depth), F32),
            pltpu.VMEM((levels + 1, 16, depth), F32), pltpu.VMEM((16, depth), F32), pltpu.VMEM((levels + 1, 16, depth), F32),
            dma((16,)), dma((2, 2)), dma((JOBS,)), dma((JOBS,)), dma((2 * levels, JOBS)), dma((2 * levels, JOBS)), dma((JOBS,)), dma((2,)), dma(()), dma((levels + 1,)), dma((levels + 1,)),
        ],
        compiler_params=pltpu.CompilerParams(vmem_limit_bytes=67043328, collective_id=1, has_side_effects=True),
        cost_estimate=pl.CostEstimate(flops=60 << 30, bytes_accessed=64 << 20, transcendentals=8 << 20),
        name="backward",
    )(lens, *arrays)


def unpack_kernel(jobs_ref, gf_ref, dx_ref, small_ref, tok_ref, qkv_ref, qvb_ref, out_ref, up_ref, upb_ref, down_ref, *vec_refs):
    step = pl.program_id(0)

    def unslab(target):
        for i in range(3):
            rows = slice(i * 128, i * 128 + 128)
            target[rows, :JC] = jobs_ref[i, :128, :].astype(F32)
            target[rows, JC:] = jobs_ref[i, 128:, :].astype(F32)

    def tall(store):
        for i in range(3):
            store(i, jobs_ref[i].astype(F32))

    @pl.when(step < 4)
    def _():
        unslab(down_ref)
        tok_ref[...] = gf_ref[...] + dx_ref[...]

    @pl.when((step >= 4) & (step < 8))
    def _():
        for i in range(3):
            up_ref[i * JR:(i + 1) * JR, :] = jobs_ref[i].astype(F32)

    @pl.when(step == 8)
    def _():
        unslab(out_ref)
        for i, ref in enumerate(vec_refs):
            ref[...] = small_ref[i:i + 1, :]
        upb_ref[...] = small_ref[8:10, :]
        qvb_ref[0:1, :] = small_ref[10:11, :JC]
        qvb_ref[1:2, :] = small_ref[10:11, JC:]

    @pl.when(step >= 9)
    def _():
        for i in range(3):
            qkv_ref[0, i * JR:(i + 1) * JR, :] = jobs_ref[i].astype(F32)


def unpack(jobs, grad_first, dx, small, wide):
    rows, depth = grad_first.shape

    def rows_at(i):
        return (jnp.minimum(i, 3), 0)

    quarter = pl.BlockSpec((rows // 4, depth), rows_at)

    def whole(shape):
        return pl.BlockSpec(shape, lambda i: (0, 0))

    vec = jax.ShapeDtypeStruct((1, depth), F32)
    return pl.pallas_call(
        unpack_kernel,
        grid=(GROUPS,),
        out_shape=(
            jax.ShapeDtypeStruct((rows, depth), F32), jax.ShapeDtypeStruct((3, depth, JC), F32), jax.ShapeDtypeStruct((2, JC), F32),
            jax.ShapeDtypeStruct((JC, depth), F32), jax.ShapeDtypeStruct((depth, wide), F32), jax.ShapeDtypeStruct((2, depth), F32),
            jax.ShapeDtypeStruct((wide, depth), F32), vec, vec, vec, vec, vec, vec,
        ),
        in_specs=[pl.BlockSpec((3, JR, JC), lambda i: (i, 0, 0)), quarter, quarter, whole((16, depth))],
        out_specs=[
            quarter, pl.BlockSpec((1, depth, JC), lambda i: (jnp.clip(i - 9, 0, 2), 0, 0)), whole((2, JC)), whole((JC, depth)),
            pl.BlockSpec((depth, JC), lambda i: (0, jnp.clip(i - 4, 0, 3))), whole((2, depth)), pl.BlockSpec((JC, depth), rows_at),
        ] + [whole((1, depth))] * 6,
        name="unpack",
    )(jobs, grad_first, dx, small)


def body(tokens, lengths, qkv_weight, qv_bias, out_weight, out_bias, first_gain, first_shift, up_weight, up_bias, down_weight, down_bias, second_gain, second_shift, cotangent):
    n_tensor = lax.axis_size("tensor")
    n_dp = lax.axis_size("dp")
    core = lax.axis_index("tensor")
    seqs = lengths.shape[0] // n_tensor
    lens = lax.dynamic_slice(lengths, (core * seqs,), (seqs,))
    levels = 4

    def swap(value):
        return lax.ppermute(value, "tensor", [(0, 1), (1, 0)])

    up_row = up_bias.reshape(1, -1)
    peer_qkv, peer_qv_bias = swap(qkv_weight), swap(qv_bias)
    peer_out, peer_up, peer_up_row, peer_down = swap(out_weight), swap(up_weight), swap(up_row), swap(down_weight)
    q_own, k_own, v_own, c_own = attention(lens, tokens, qkv_weight, qv_bias)
    q_peer, k_peer, v_peer, c_peer = attention(lens, tokens, peer_qkv, peer_qv_bias)
    vecs = jnp.stack([out_bias, first_gain, first_shift, down_bias, second_gain, second_shift, out_bias, out_bias])
    layer_out, h_own, h_peer, gu_own, gu_peer, mid, glow, flow, gctx, grad_first, sums = ffn(
        c_own, c_peer, tokens, cotangent, out_weight, peer_out, up_weight, peer_up, up_row, peer_up_row, down_weight, peer_down, vecs
    )
    jobs, dx, sums = backward(
        levels, lens,
        (h_own, h_peer, gu_own, gu_peer, glow, mid, flow, c_own, c_peer, q_own, q_peer, k_own, k_peer, v_own, v_peer, gctx, tokens, qkv_weight, peer_qkv, sums),
    )
    inner = 1 << levels
    if n_dp > inner:
        groups = [[i + inner * g for g in range(n_dp // inner)] for i in range(inner)]
        jobs, sums = lax.psum((jobs, sums), "dp", axis_index_groups=groups)
    grad_tokens, grad_qkv, grad_qv_bias, grad_out, grad_up, grad_up_bias, grad_down, *vectors = unpack(jobs, grad_first, dx, sums, up_bias.shape[0])
    vectors = [item.reshape(-1) for item in vectors]
    return (
        layer_out, grad_tokens, grad_qkv, grad_qv_bias, grad_out, vectors[0], vectors[1], vectors[2],
        grad_up, grad_up_bias.reshape(-1), grad_down, vectors[3], vectors[4], vectors[5],
    )


def solution(mesh):
    tokens = P(("dp", "tensor"), None)
    columns = P(None, "tensor")
    cube = P(None, None, "tensor")
    split = P("tensor", None)
    return jax.shard_map(
        body,
        mesh=mesh,
        in_specs=(tokens, P("dp"), cube, columns, split, P(), P(), P(), columns, P("tensor"), split, P(), P(), P(), tokens),
        out_specs=(tokens, tokens, cube, columns, split, P(), P(), P(), columns, P("tensor"), split, P(), P(), P()),
        check_vma=False,
    )
```

time: 883 us -> 282 us (0.32)
  waiting for transfers between devices: 357 us -> 0.02 us
  Pallas kernels: 0 us -> 265 us
  matrix products: 228 us -> 0 us
  blocking collectives: 125 us -> 0 us
  local copies, waits for them, and re-layouts: 102 us -> 5.92 us
  other arithmetic: 49.9 us -> 7.71 us
  between operations: 14.4 us -> 0.83 us
    pallas_call x0 -> x5, Pallas kernels: none -> 265 us  [the longest x1 175 us: backward(): pl.pallas_call(functools.partial(back_kernel, levels), out_shape=(jax.Sha...]
    psum x1 -> x0, waiting for transfers between devices: 263 us -> none  [body(): lax.psum((grad_qkv_weight, grad_qv_bias, grad_out_weight, grad_up_weight,...]
    dot_general x32 -> x0, matrix products: 179 us -> none  [the longest x1 33.9 us: body(): jnp.dot(whole_mid, up_weight, preferred_element_type=jnp.float32) + up_bias]
    psum x2 -> x0, blocking collectives: 125 us -> none  [the longest x1 79.3 us: body(): lax.psum((grad_qkv_weight, grad_qv_bias, grad_out_weight, grad_up_weight,...]
    all_gather x4 -> x0, waiting for transfers between devices: 55.8 us -> none  [the longest x1 15.5 us: body(): whole_x = lax.all_gather(tokens, 'tensor', axis=0, tiled=True)]
    sub x8 -> x0, matrix products: 48.9 us -> none  [softmax_rows(): return jax.nn.softmax(scores, axis=-1)]
    reduce_scatter x4 -> x0, waiting for transfers between devices: 37.1 us -> none  [the longest x1 12.4 us: body(): lax.psum_scatter(jnp.einsum('rf,df->rd', grad_up_act, up_weight, preferre...]
    unnamed x99 -> x24, local copies, waits for them, and re-layouts: 28 us -> 2.02 us
  transfers between devices with their start and end apart: 9 -> 6, of which waited for: 8 -> 0; matrix products, arithmetic and copies ran while one was open for 4% -> 1% of each run, Pallas kernels for 0% -> 12%
where the time goes in v1:
time: 282 us; the launch traced here: 281 us
  Pallas kernels  265 us (94%)
  other arithmetic  7.71 us (3%)
  local copies, waits for them, and re-layouts  5.92 us (2%)
    pallas_call x1, Pallas kernels, backward(): pl.pallas_call(functools.partial(back_kernel, levels), out_shape=(jax.Sha...  175 us
    pallas_call x1, Pallas kernels, ffn(): pl.pallas_call(functools.partial(ffn_kernel, chunk), grid=(rows // tile,)...  43.5 us
    pallas_call x2, Pallas kernels, attention(): pl.pallas_call(functools.partial(attn_kernel, qb), out_shape=(out, out, o...  32.4 us
    pallas_call x1, Pallas kernels, unpack(): pl.pallas_call(unpack_kernel, grid=(GROUPS,), out_shape=(jax.ShapeDtypeSt...  14.8 us
    pallas_call x6, other arithmetic, unpack(): pl.pallas_call(unpack_kernel, grid=(GROUPS,), out_shape=(jax.ShapeDtypeSt...  7.71 us
  transfers between devices with their start and end apart: 6, of which 0 were waited for; matrix products, arithmetic and copies ran while one was open for 1% of the time, Pallas kernels for 12%

profile of v1, /device:TPU:0, one launch (start us, length us, event | category | flops | bytes accessed | tf_op | source)
XLA Modules:
  0.0 281.4 jit_solution(17927755411156382466)
XLA Ops:
  0.6 0.6 collective-permute-start
  1.2 0.1 collective-permute-start.3
  1.3 0.4 collective-permute-start.5
  1.7 0.1 collective-permute-start.1
  1.8 0.7 reshape.52.bu_own
  2.5 0.0 copy-start
  2.5 0.4 collective-permute-start.4
  2.9 1.2 dynamic_slice.3.lens_ref
  4.2 0.0 copy-start.1
  4.2 0.0 copy-start.2
  4.2 0.0 copy-start.3
  4.2 0.0 copy-start.4
  4.2 0.0 copy-start.5
  4.2 0.0 copy-start.6
  4.2 0.0 copy-start.8
  4.2 16.3 %attend.2 = (bf16[1024,384]{1,0:T(8,128)(2,1)}, bf16[1024,384]{1,0:T(8,128)(2,1)}, bf16[1024,384]{1,0:T(8,128)(2,1)}, bf16[1024,384]{1,0:T(8,128)(2,1)}) custom-call(s32[2]{0:T(128)} %dynamic_slice.3.lens_ref, bf16[1024,768]{1,0:T(8,128)(2,1)} %x_in.1, bf16[3,768,384]{2,1,0:T(8,128)(2,1)} %w_own.1, f32[2,384]{1,0:T(2,128)} %b_ref.1), custom_call_target="tpu_custom_call" | custom-call | flops 7851737088 | bytes 12582912 | tf_op jit(solution)/shard_map/attend/pallas_call | solution.py:74
  20.5 0.0 copy-done
  20.5 0.0 copy-done.1
  20.5 0.0 copy-done.2
  20.5 0.0 copy-done.3
  20.5 0.0 copy-done.4
  20.6 0.0 copy-done.5
  20.6 0.0 copy-done.6
  20.6 0.6 stack.29.vec_ref
  21.2 0.0 collective-permute-done.1.b_ref
  21.3 0.0 copy-done.8
  21.3 0.0 copy-start.11
  21.3 0.1 collective-permute-start.2
  21.4 0.0 collective-permute-done.w_ref.w_peer
  21.4 0.4 copy-done.11
  21.8 16.1 %attend.3 = (bf16[1024,384]{1,0:T(8,128)(2,1)}, bf16[1024,384]{1,0:T(8,128)(2,1)}, bf16[1024,384]{1,0:T(8,128)(2,1)}, bf16[1024,384]{1,0:T(8,128)(2,1)}) custom-call(s32[2]{0:T(128)} %dynamic_slice.3.lens_ref, bf16[1024,768]{1,0:T(8,128)(2,1)} %x_in.1, bf16[3,768,384]{2,1,0:T(8,128)(2,1)} %collective-permute-done.w_ref.w_peer, f32[2,384]{1,0:T(2,128)} %copy-done.11), custom_call_target="tpu_custom_call" | custom-call | flops 7851737088 | bytes 12582912 | tf_op jit(solution)/shard_map/attend/pallas_call | solution.py:74
  38.0 0.0 collective-permute-done.4.bu_peer
  38.0 0.0 copy-start.10
  38.0 0.0 collective-permute-done.2.wo_peer
  38.0 0.0 copy-start.9
  38.0 0.0 collective-permute-done.3.wu_peer
  38.0 0.0 copy-start.7
  38.0 0.0 collective-permute-done.5.wd_peer
  38.0 0.5 copy-done.10
  38.6 0.2 copy-done.9
  38.8 0.8 copy-done.7
  39.6 43.5 %feed.1 = (f32[1024,768]{1,0:T(8,128)}, bf16[1024,1536]{1,0:T(8,128)(2,1)}, bf16[1024,1536]{1,0:T(8,128)(2,1)}, bf16[1024,1536]{1,0:T(8,128)(2,1)}, bf16[1024,15...) custom-call(bf16[1024,384]{1,0:T(8,128)(2,1)} %get-tuple-element.49., ...), custom_call_target="tpu_custom_call" | custom-call | flops 24159191040 | bytes 50331648 | tf_op jit(solution)/shard_map/feed/pallas_call | solution.py:198
  83.1 174.5 %backward.1 = (bf16[36,256,384]{2,1,0:T(8,128)(2,1)}, f32[1024,768]{1,0:T(8,128)}, f32[16,768]{1,0:T(8,128)}) custom-call(s32[2]{0:T(128)} %dynamic_slice.3.lens_ref, bf16[1024,1536]{1,0:T(8,128)(2,1)} %get-tuple-element.52.h_own, bf16[1024,1536]{1,0:T(8,128)(2,1)} %get-tuple-element.53.h_peer, bf16[1024,1536]{1,0:T(8,128)(2,1)} %get-tuple-element.54.gu_own, ...), custom_call_target="tpu_custom_call" | custom-call | flops 64424509440 | bytes 67108864 | tf_op jit(solution)/shard_map/backward/pallas_call | solution.py:590
  257.7 14.8 %unpack.1 = (f32[1024,768]{1,0:T(8,128)}, f32[3,768,384]{2,1,0:T(8,128)}, f32[2,384]{1,0:T(2,128)}, f32[384,768]{1,0:T(8,128)}, f32[768,1536]{1,0:T(8,128)}, /*i...) custom-call(bf16[36,256,384]{2,1,0:T(8,128)(2,1)} %get-tuple-element, ...), custom_call_target="tpu_custom_call" | custom-call | tf_op jit(solution)/shard_map/unpack/pallas_call | solution.py:664
  272.4 1.3 reduce
  273.7 1.3 reduce.1
  275.0 1.3 reduce.2
  276.3 1.3 reduce.3
  277.6 1.3 reduce.4
  278.9 1.3 reduce.5
  280.1 1.3 reshape.56
  (6 shorter events, 0.0 us)
Async XLA Ops:
  0.6 20.8 %collective-permute-start = (bf16[3,768,384]{2,1,0:T(8,128)(2,1)}, bf16[3,768,384]{2,1,0:T(8,128)(2,1)}, u32[]{:S(2)}, u32[]{:S(2)}) collective-permute-start(bf16[3,768,384]{2,1,0:T(8,128)(2,1)} %w_own.1), channel_id=1, source_target_pairs={{0,1},{1,0},{2,3},{3,2},{4,5},{5,4},{6,7},{7,6},{8,9},{9,8},{10,11... | collective-permute-start | bytes 5308424 | tf_op jit(solution)/shard_map/ppermute | solution.py:690
  1.2 36.8 %collective-permute-start.3 = (bf16[768,1536]{1,0:T(8,128)(2,1)}, bf16[768,1536]{1,0:T(8,128)(2,1)S(1)}, u32[]{:S(2)}, u32[]{:S(2)}) collective-permute-start(bf16[768,1536]{1,0:T(8,128)(2,1)} %wu_own.1), channel_id=1, source_target_pairs={{0,1},{1,0},{2,3},{3,2},{4,5},{5,4},{6,7},{7,6},{8,9},{9,8},{10,11... | collective-permute-start | bytes 7077896 | tf_op jit(solution)/shard_map/ppermute | solution.py:690
  1.3 36.7 %collective-permute-start.5 = (bf16[1536,768]{1,0:T(8,128)(2,1)}, bf16[1536,768]{1,0:T(8,128)(2,1)}, u32[]{:S(2)}, u32[]{:S(2)}) collective-permute-start(bf16[1536,768]{1,0:T(8,128)(2,1)} %wd_own.1), channel_id=1, source_target_pairs={{0,1},{1,0},{2,3},{3,2},{4,5},{5,4},{6,7},{7,6},{8,9},{9,8},{10,11... | collective-permute-start | bytes 7077896 | tf_op jit(solution)/shard_map/ppermute | solution.py:690
  1.7 19.5 %collective-permute-start.1 = (f32[2,384]{1,0:T(2,128)}, f32[2,384]{1,0:T(2,128)S(1)}, u32[]{:S(2)}, u32[]{:S(2)}) collective-permute-start(f32[2,384]{1,0:T(2,128)} %b_ref.1), channel_id=1, source_target_pairs={{0,1},{1,0},{2,3},{3,2},{4,5},{5,4},{6,7},{7,6},{8,9},{9,8},{10,11... | collective-permute-start | bytes 9224 | tf_op jit(solution)/shard_map/ppermute | solution.py:690
  2.5 18.0 %copy-start = (f32[1,1536]{1,0:T(1,128)}, f32[1,1536]{1,0:T(1,128)S(1)}, u32[]{:S(2)}) copy-start(f32[1,1536]{1,0:T(1,128)S(1)} %reshape.52.bu_own) | copy-start | bytes 18436
  2.5 35.5 %collective-permute-start.4 = (f32[1,1536]{1,0:T(1,128)S(1)}, f32[1,1536]{1,0:T(1,128)S(1)}, u32[]{:S(2)}, u32[]{:S(2)}) collective-permute-start(f32[1,1536]{1,0:T(1,128)S(1)} %reshape.52.bu_own), channel_id=1, source_target_pairs={{0,1},{1,0},{2,3},{3,2},{4,5},{5,4},{6,7},{7,6},{8,9},{9,8},{10,11... | collective-permute-start | bytes 18440 | tf_op jit(solution)/shard_map/ppermute | solution.py:690
  4.2 16.3 %copy-start.1 = (f32[768]{0:T(1024)S(1)}, f32[768]{0:T(1024)}, u32[]{:S(2)}) copy-start(f32[768]{0:T(1024)} %param.20) | copy-start | bytes 9220
  4.2 16.3 %copy-start.2 = (f32[768]{0:T(1024)S(1)}, f32[768]{0:T(1024)}, u32[]{:S(2)}) copy-start(f32[768]{0:T(1024)} %param.21) | copy-start | bytes 9220
  4.2 16.4 %copy-start.3 = (f32[768]{0:T(1024)S(1)}, f32[768]{0:T(1024)}, u32[]{:S(2)}) copy-start(f32[768]{0:T(1024)} %param.22) | copy-start | bytes 9220
  4.2 16.4 %copy-start.4 = (f32[768]{0:T(1024)S(1)}, f32[768]{0:T(1024)}, u32[]{:S(2)}) copy-start(f32[768]{0:T(1024)} %param.26) | copy-start | bytes 9220
  4.2 16.4 %copy-start.5 = (f32[768]{0:T(1024)S(1)}, f32[768]{0:T(1024)}, u32[]{:S(2)}) copy-start(f32[768]{0:T(1024)} %param.27) | copy-start | bytes 9220
  4.2 16.4 %copy-start.6 = (f32[768]{0:T(1024)S(1)}, f32[768]{0:T(1024)}, u32[]{:S(2)}) copy-start(f32[768]{0:T(1024)} %param.28) | copy-start | bytes 9220
  4.2 17.1 %copy-start.8 = (bf16[384,768]{1,0:T(8,128)(2,1)S(1)}, bf16[384,768]{1,0:T(8,128)(2,1)}, u32[]{:S(2)}) copy-start(bf16[384,768]{1,0:T(8,128)(2,1)} %wo_own.1) | copy-start | bytes 1769476
  21.3 0.6 copy-start.11
  21.3 16.7 %collective-permute-start.2 = (bf16[384,768]{1,0:T(8,128)(2,1)S(1)}, bf16[384,768]{1,0:T(8,128)(2,1)S(1)}, u32[]{:S(2)}, u32[]{:S(2)}) collective-permute-start(bf16[384,768]{1,0:T(8,128)(2,1)S(1)} %copy-done.8), channel_id=1, source_target_pairs={{0,1},{1,0},{2,3},{3,2},{4,5},{5,4},{6,7},{7,6},{8,9},{9,8},{10,11... | collective-permute-start | bytes 1769480 | tf_op jit(solution)/shard_map/ppermute | solution.py:690
  38.0 0.6 copy-start.10
  38.0 0.8 copy-start.9
  38.0 1.6 copy-start.7

commit v2 on v1

--- a/solution.py
+++ b/solution.py
@@ -63,7 +63,7 @@
             c_ref[span, lanes] = jnp.concatenate(parts, axis=0).T.astype(BF)
 
 
-def attention(lens, x, weight, bias, qb=256):
+def attention(lens, x, weight, bias, qb=512):
     rows, depth = x.shape
     seqs = lens.shape[0]
     seq_len = rows // seqs
@@ -216,8 +216,9 @@
     )(c_own, c_peer, x, cot, *fixed_in)
 
 
-LAGS = (1, 3, 5, 6, 8, 10, 11, 12, 14)
+LAGS = (1, 4, 7, 9, 12, 15, 17, 19, 22)
 GROUPS = 12
+BLOCKS = 1
 JOBS = 3 * GROUPS
 
 
@@ -310,7 +311,7 @@
     def stage_op(stage, job):
         if stage == 0:
             core_copy(job).wait_recv()
-            buf[job] = (buf[job].astype(F32) + prec[job].astype(F32)).astype(BF)
+            buf[job] = buf[job] + prec[job]
             hop(job, 0).start()
             return
         before = hop(job, stage - 1)
@@ -321,9 +322,9 @@
             size = JR >> stage
             at = pl.multiple_of(offsets(job)[stage], 16)
             begin = JR - (JR >> level)
-            keep = buf[job, pl.ds(at, size)].astype(F32) + rbuf[job, begin:begin + size].astype(F32)
+            keep = buf[job, pl.ds(at, size)] + rbuf[job, begin:begin + size]
             target = prec if stage == levels else buf
-            target[job, pl.ds(at, size)] = keep.astype(BF)
+            target[job, pl.ds(at, size)] = keep
         if stage < 2 * levels:
             hop(job, stage).start()
         else:
@@ -446,10 +447,10 @@
         v = vv[span, lanes]
         k_t = k.T
         low = half_masks((1, 128), 1)
-        qb = seq_len // 2
+        qb = seq_len // BLOCKS
         grad_k = jnp.zeros((seq_len, 128), F32)
         grad_v = jnp.zeros((seq_len, 128), F32)
-        for block in range(2):
+        for block in range(BLOCKS):
             part = pl.ds(pl.multiple_of(seq * seq_len + block * qb, qb), qb)
             q = qv[part, lanes]
             do = dov[part, lanes]
@@ -507,7 +508,7 @@
             for i, grad in enumerate((dq, dk, dv)):
                 part = part + dot_nt(grad[span, cols], wv[side, i])
             total = total + part
-        dxs[index % 2] = total
+        dxs[index % 2] = total.astype(BF)
         dx_copy(index).start()
 
     barrier = pltpu.get_barrier_semaphore()
@@ -591,7 +592,7 @@
         functools.partial(back_kernel, levels),
         out_shape=(
             jax.ShapeDtypeStruct((JOBS, JR, JC), BF),
-            jax.ShapeDtypeStruct((rows, depth), F32),
+            jax.ShapeDtypeStruct((rows, depth), BF),
             jax.ShapeDtypeStruct((16, depth), F32),
         ),
         in_specs=[pl.BlockSpec(memory_space=pltpu.SMEM)] + [hbm] * len(arrays),
@@ -601,7 +602,7 @@
             pltpu.VMEM((JOBS, JR - (JR >> levels), JC), BF), pltpu.VMEM((2, 2, rows, JC), BF),
             square, square, square, square, square, square, square, square, square,
             pltpu.VMEM((2, 3, depth, half), BF), square, square, square,
-            pltpu.VMEM((2, JR, depth), F32), pltpu.VMEM((16, depth), F32),
+            pltpu.VMEM((2, JR, depth), BF), pltpu.VMEM((16, depth), F32),
             pltpu.VMEM((levels + 1, 16, depth), F32), pltpu.VMEM((16, depth), F32), pltpu.VMEM((levels + 1, 16, depth), F32),
             dma((16,)), dma((2, 2)), dma((JOBS,)), dma((JOBS,)), dma((2 * levels, JOBS)), dma((2 * levels, JOBS)), dma((JOBS,)), dma((2,)), dma(()), dma((levels + 1,)), dma((levels + 1,)),
         ],
@@ -613,6 +614,7 @@
 
 def unpack_kernel(jobs_ref, gf_ref, dx_ref, small_ref, tok_ref, qkv_ref, qvb_ref, out_ref, up_ref, upb_ref, down_ref, *vec_refs):
     step = pl.program_id(0)
+    depth = small_ref.shape[1]
 
     def unslab(target):
         for i in range(3):
@@ -627,7 +629,7 @@
     @pl.when(step < 4)
     def _():
         unslab(down_ref)
-        tok_ref[...] = gf_ref[...] + dx_ref[...]
+        tok_ref[...] = gf_ref[...] + dx_ref[...].astype(F32)
 
     @pl.when((step >= 4) & (step < 8))
     def _():
@@ -638,8 +640,9 @@
     def _():
         unslab(out_ref)
         for i, ref in enumerate(vec_refs):
-            ref[...] = small_ref[i:i + 1, :]
-        upb_ref[...] = small_ref[8:10, :]
+            ref[...] = small_ref[i]
+        upb_ref[:depth] = small_ref[8]
+        upb_ref[depth:] = small_ref[9]
         qvb_ref[0:1, :] = small_ref[10:11, :JC]
         qvb_ref[1:2, :] = small_ref[10:11, JC:]
 
@@ -660,20 +663,24 @@
     def whole(shape):
         return pl.BlockSpec(shape, lambda i: (0, 0))
 
-    vec = jax.ShapeDtypeStruct((1, depth), F32)
+    def flat(size):
+        return pl.BlockSpec((size,), lambda i: (0,))
+
+    vec = jax.ShapeDtypeStruct((depth,), F32)
     return pl.pallas_call(
         unpack_kernel,
         grid=(GROUPS,),
         out_shape=(
             jax.ShapeDtypeStruct((rows, depth), F32), jax.ShapeDtypeStruct((3, depth, JC), F32), jax.ShapeDtypeStruct((2, JC), F32),
-            jax.ShapeDtypeStruct((JC, depth), F32), jax.ShapeDtypeStruct((depth, wide), F32), jax.ShapeDtypeStruct((2, depth), F32),
+            jax.ShapeDtypeStruct((JC, depth), F32), jax.ShapeDtypeStruct((depth, wide), F32), jax.ShapeDtypeStruct((wide,), F32),
             jax.ShapeDtypeStruct((wide, depth), F32), vec, vec, vec, vec, vec, vec,
         ),
         in_specs=[pl.BlockSpec((3, JR, JC), lambda i: (i, 0, 0)), quarter, quarter, whole((16, depth))],
         out_specs=[
             quarter, pl.BlockSpec((1, depth, JC), lambda i: (jnp.clip(i - 9, 0, 2), 0, 0)), whole((2, JC)), whole((JC, depth)),
-            pl.BlockSpec((depth, JC), lambda i: (0, jnp.clip(i - 4, 0, 3))), whole((2, depth)), pl.BlockSpec((JC, depth), rows_at),
-        ] + [whole((1, depth))] * 6,
+            pl.BlockSpec((depth, JC), lambda i: (0, jnp.clip(i - 4, 0, 3))), flat(wide), pl.BlockSpec((JC, depth), rows_at),
+        ] + [flat(depth)] * 6,
+        compiler_params=pltpu.CompilerParams(vmem_limit_bytes=62 << 20),
         name="unpack",
     )(jobs, grad_first, dx, small)
 
@@ -707,10 +714,9 @@
         groups = [[i + inner * g for g in range(n_dp // inner)] for i in range(inner)]
         jobs, sums = lax.psum((jobs, sums), "dp", axis_index_groups=groups)
     grad_tokens, grad_qkv, grad_qv_bias, grad_out, grad_up, grad_up_bias, grad_down, *vectors = unpack(jobs, grad_first, dx, sums, up_bias.shape[0])
-    vectors = [item.reshape(-1) for item in vectors]
     return (
         layer_out, grad_tokens, grad_qkv, grad_qv_bias, grad_out, vectors[0], vectors[1], vectors[2],
-        grad_up, grad_up_bias.reshape(-1), grad_down, vectors[3], vectors[4], vectors[5],
+        grad_up, grad_up_bias, grad_down, vectors[3], vectors[4], vectors[5],
     )
 
 

time: 282 us -> 239 us (0.85)
  Pallas kernels: 265 us -> 231 us
  other arithmetic: 7.71 us -> 0 us
    pallas_call x1, Pallas kernels: 175 us -> 148 us  [backward(): pl.pallas_call(functools.partial(back_kernel, levels), out_shape=(jax.Sha...]
    pallas_call x6 -> x0, other arithmetic: 7.71 us -> none  [unpack(): pl.pallas_call(unpack_kernel, grid=(GROUPS,), out_shape=(jax.ShapeDtypeSt...]
    pallas_call x2, Pallas kernels: 32.4 us -> 24.9 us  [attention(): pl.pallas_call(functools.partial(attn_kernel, qb), out_shape=(out, out, o...]
  transfers between devices with their start and end apart: 6 -> 6, of which waited for: 0 -> 0; matrix products, arithmetic and copies ran while one was open for 1% -> 1% of each run, Pallas kernels for 12% -> 10%
where the time goes in v2:
time: 239 us
  Pallas kernels  231 us (97%)
  local copies, waits for them, and re-layouts  4.67 us (2%)
    pallas_call x1, Pallas kernels, backward(): pl.pallas_call(functools.partial(back_kernel, levels), out_shape=(jax.Sha...  148 us
    pallas_call x1, Pallas kernels, ffn(): pl.pallas_call(functools.partial(ffn_kernel, chunk), grid=(rows // tile,)...  43.6 us
    pallas_call x2, Pallas kernels, attention(): pl.pallas_call(functools.partial(attn_kernel, qb), out_shape=(out, out, o...  24.9 us
    pallas_call x1, Pallas kernels, unpack(): pl.pallas_call(unpack_kernel, grid=(GROUPS,), out_shape=(jax.ShapeDtypeSt...  14.5 us
  transfers between devices with their start and end apart: 6, of which 0 were waited for; matrix products, arithmetic and copies ran while one was open for 1% of the time, Pallas kernels for 10%

profile of v2, /device:TPU:0, one launch (start us, length us, event | category | flops | bytes accessed | tf_op | source)
XLA Modules:
  0.0 238.6 jit_solution(10000623674776238056)
XLA Ops:
  0.6 0.6 collective-permute-start
  1.2 0.1 collective-permute-start.3
  1.3 0.4 collective-permute-start.5
  1.7 0.1 collective-permute-start.1
  1.8 0.7 reshape.31.bu_own
  2.5 0.0 copy-start
  2.5 0.4 collective-permute-start.4
  2.9 1.2 dynamic_slice.3.lens_ref
  4.2 0.0 copy-start.1
  4.2 0.0 copy-start.2
  4.2 0.0 copy-start.3
  4.2 0.0 copy-start.4
  4.2 0.0 copy-start.5
  4.2 0.0 copy-start.6
  4.2 0.0 copy-start.8
  4.2 12.5 %attend.2 = (bf16[1024,384]{1,0:T(8,128)(2,1)}, bf16[1024,384]{1,0:T(8,128)(2,1)}, bf16[1024,384]{1,0:T(8,128)(2,1)}, bf16[1024,384]{1,0:T(8,128)(2,1)}) custom-call(s32[2]{0:T(128)} %dynamic_slice.3.lens_ref, bf16[1024,768]{1,0:T(8,128)(2,1)} %x_in.1, bf16[3,768,384]{2,1,0:T(8,128)(2,1)} %w_own.1, f32[2,384]{1,0:T(2,128)} %b_ref.1), custom_call_target="tpu_custom_call" | custom-call | flops 7851737088 | bytes 12582912 | tf_op jit(solution)/shard_map/attend/pallas_call | solution.py:74
  16.7 0.0 copy-done
  16.7 0.0 copy-done.1
  16.8 0.0 copy-done.2
  16.8 0.0 copy-done.3
  16.8 0.0 copy-done.4
  16.8 0.0 copy-done.5
  16.8 0.0 copy-done.6
  16.9 0.6 stack.29.vec_ref
  17.5 0.0 collective-permute-done.1.b_ref
  17.5 0.0 copy-done.8
  17.5 0.0 copy-start.11
  17.5 0.1 collective-permute-start.2
  17.6 0.0 collective-permute-done.w_ref.w_peer
  17.7 0.4 copy-done.11
  18.1 12.4 %attend.3 = (bf16[1024,384]{1,0:T(8,128)(2,1)}, bf16[1024,384]{1,0:T(8,128)(2,1)}, bf16[1024,384]{1,0:T(8,128)(2,1)}, bf16[1024,384]{1,0:T(8,128)(2,1)}) custom-call(s32[2]{0:T(128)} %dynamic_slice.3.lens_ref, bf16[1024,768]{1,0:T(8,128)(2,1)} %x_in.1, bf16[3,768,384]{2,1,0:T(8,128)(2,1)} %collective-permute-done.w_ref.w_peer, f32[2,384]{1,0:T(2,128)} %copy-done.11), custom_call_target="tpu_custom_call" | custom-call | flops 7851737088 | bytes 12582912 | tf_op jit(solution)/shard_map/attend/pallas_call | solution.py:74
  30.5 0.0 collective-permute-done.4.bu_peer
  30.5 0.0 copy-start.10
  30.5 0.0 collective-permute-done.2.wo_peer
  30.5 0.0 copy-start.9
  30.5 0.0 collective-permute-done.3.wu_peer
  30.5 0.0 copy-start.7
  30.5 0.0 collective-permute-done.5.wd_peer
  30.5 0.5 copy-done.10
  31.1 0.2 copy-done.9
  31.3 0.8 copy-done.7
  32.1 43.6 %feed.1 = (f32[1024,768]{1,0:T(8,128)}, bf16[1024,1536]{1,0:T(8,128)(2,1)}, bf16[1024,1536]{1,0:T(8,128)(2,1)}, bf16[1024,1536]{1,0:T(8,128)(2,1)}, bf16[1024,15...) custom-call(bf16[1024,384]{1,0:T(8,128)(2,1)} %get-tuple-element.49., ...), custom_call_target="tpu_custom_call" | custom-call | flops 24159191040 | bytes 50331648 | tf_op jit(solution)/shard_map/feed/pallas_call | solution.py:198
  75.7 148.3 %backward.1 = (bf16[36,256,384]{2,1,0:T(8,128)(2,1)}, bf16[1024,768]{1,0:T(8,128)(2,1)}, f32[16,768]{1,0:T(8,128)}) custom-call(s32[2]{0:T(128)} %dynamic_slice.3.lens_ref, bf16[1024,1536]{1,0:T(8,128)(2,1)} %get-tuple-element.52.h_own, bf16[1024,1536]{1,0:T(8,128)(2,1)} %get-tuple-element.53.h_peer, bf16[1024,1536]{1,0:T(8,128)(2,1)} %get-tuple-element.54.gu_own, ...), custom_call_target="tpu_custom_call" | custom-call | flops 64424509440 | bytes 67108864 | tf_op jit(solution)/shard_map/backward/pallas_call | solution.py:591
  223.9 14.5 %unpack.1 = (f32[1024,768]{1,0:T(8,128)}, f32[3,768,384]{2,1,0:T(8,128)}, f32[2,384]{1,0:T(2,128)}, f32[384,768]{1,0:T(8,128)}, f32[768,1536]{1,0:T(8,128)}, /*i...) custom-call(bf16[36,256,384]{2,1,0:T(8,128)(2,1)} %get-tuple-element, ...), custom_call_target="tpu_custom_call" | custom-call | tf_op jit(solution)/shard_map/unpack/pallas_call | solution.py:670
  (6 shorter events, 0.0 us)
Async XLA Ops:
  0.6 17.0 %collective-permute-start = (bf16[3,768,384]{2,1,0:T(8,128)(2,1)}, bf16[3,768,384]{2,1,0:T(8,128)(2,1)}, u32[]{:S(2)}, u32[]{:S(2)}) collective-permute-start(bf16[3,768,384]{2,1,0:T(8,128)(2,1)} %w_own.1), channel_id=1, source_target_pairs={{0,1},{1,0},{2,3},{3,2},{4,5},{5,4},{6,7},{7,6},{8,9},{9,8},{10,11... | collective-permute-start | bytes 5308424 | tf_op jit(solution)/shard_map/ppermute | solution.py:697
  1.2 29.3 %collective-permute-start.3 = (bf16[768,1536]{1,0:T(8,128)(2,1)}, bf16[768,1536]{1,0:T(8,128)(2,1)S(1)}, u32[]{:S(2)}, u32[]{:S(2)}) collective-permute-start(bf16[768,1536]{1,0:T(8,128)(2,1)} %wu_own.1), channel_id=1, source_target_pairs={{0,1},{1,0},{2,3},{3,2},{4,5},{5,4},{6,7},{7,6},{8,9},{9,8},{10,11... | collective-permute-start | bytes 7077896 | tf_op jit(solution)/shard_map/ppermute | solution.py:697
  1.3 29.2 %collective-permute-start.5 = (bf16[1536,768]{1,0:T(8,128)(2,1)}, bf16[1536,768]{1,0:T(8,128)(2,1)}, u32[]{:S(2)}, u32[]{:S(2)}) collective-permute-start(bf16[1536,768]{1,0:T(8,128)(2,1)} %wd_own.1), channel_id=1, source_target_pairs={{0,1},{1,0},{2,3},{3,2},{4,5},{5,4},{6,7},{7,6},{8,9},{9,8},{10,11... | collective-permute-start | bytes 7077896 | tf_op jit(solution)/shard_map/ppermute | solution.py:697
  1.7 15.8 %collective-permute-start.1 = (f32[2,384]{1,0:T(2,128)}, f32[2,384]{1,0:T(2,128)S(1)}, u32[]{:S(2)}, u32[]{:S(2)}) collective-permute-start(f32[2,384]{1,0:T(2,128)} %b_ref.1), channel_id=1, source_target_pairs={{0,1},{1,0},{2,3},{3,2},{4,5},{5,4},{6,7},{7,6},{8,9},{9,8},{10,11... | collective-permute-start | bytes 9224 | tf_op jit(solution)/shard_map/ppermute | solution.py:697
  2.5 14.2 %copy-start = (f32[1,1536]{1,0:T(1,128)}, f32[1,1536]{1,0:T(1,128)S(1)}, u32[]{:S(2)}) copy-start(f32[1,1536]{1,0:T(1,128)S(1)} %reshape.31.bu_own) | copy-start | bytes 18436
  2.5 28.0 %collective-permute-start.4 = (f32[1,1536]{1,0:T(1,128)S(1)}, f32[1,1536]{1,0:T(1,128)S(1)}, u32[]{:S(2)}, u32[]{:S(2)}) collective-permute-start(f32[1,1536]{1,0:T(1,128)S(1)} %reshape.31.bu_own), channel_id=1, source_target_pairs={{0,1},{1,0},{2,3},{3,2},{4,5},{5,4},{6,7},{7,6},{8,9},{9,8},{10,11... | collective-permute-start | bytes 18440 | tf_op jit(solution)/shard_map/ppermute | solution.py:697
  4.2 12.6 %copy-start.1 = (f32[768]{0:T(1024)S(1)}, f32[768]{0:T(1024)}, u32[]{:S(2)}) copy-start(f32[768]{0:T(1024)} %param.20) | copy-start | bytes 9220
  4.2 12.6 %copy-start.2 = (f32[768]{0:T(1024)S(1)}, f32[768]{0:T(1024)}, u32[]{:S(2)}) copy-start(f32[768]{0:T(1024)} %param.21) | copy-start | bytes 9220
  4.2 12.6 %copy-start.3 = (f32[768]{0:T(1024)S(1)}, f32[768]{0:T(1024)}, u32[]{:S(2)}) copy-start(f32[768]{0:T(1024)} %param.22) | copy-start | bytes 9220
  4.2 12.6 %copy-start.4 = (f32[768]{0:T(1024)S(1)}, f32[768]{0:T(1024)}, u32[]{:S(2)}) copy-start(f32[768]{0:T(1024)} %param.26) | copy-start | bytes 9220
  4.2 12.6 %copy-start.5 = (f32[768]{0:T(1024)S(1)}, f32[768]{0:T(1024)}, u32[]{:S(2)}) copy-start(f32[768]{0:T(1024)} %param.27) | copy-start | bytes 9220
  4.2 12.7 %copy-start.6 = (f32[768]{0:T(1024)S(1)}, f32[768]{0:T(1024)}, u32[]{:S(2)}) copy-start(f32[768]{0:T(1024)} %param.28) | copy-start | bytes 9220
  4.2 13.3 %copy-start.8 = (bf16[384,768]{1,0:T(8,128)(2,1)S(1)}, bf16[384,768]{1,0:T(8,128)(2,1)}, u32[]{:S(2)}) copy-start(bf16[384,768]{1,0:T(8,128)(2,1)} %wo_own.1) | copy-start | bytes 1769476
  17.5 0.6 copy-start.11
  17.5 13.0 %collective-permute-start.2 = (bf16[384,768]{1,0:T(8,128)(2,1)S(1)}, bf16[384,768]{1,0:T(8,128)(2,1)S(1)}, u32[]{:S(2)}, u32[]{:S(2)}) collective-permute-start(bf16[384,768]{1,0:T(8,128)(2,1)S(1)} %copy-done.8), channel_id=1, source_target_pairs={{0,1},{1,0},{2,3},{3,2},{4,5},{5,4},{6,7},{7,6},{8,9},{9,8},{10,11... | collective-permute-start | bytes 1769480 | tf_op jit(solution)/shard_map/ppermute | solution.py:697
  30.5 0.6 copy-start.10
  30.5 0.8 copy-start.9
  30.5 1.6 copy-start.7

commit v3 on v2

--- a/solution.py
+++ b/solution.py
@@ -523,17 +523,18 @@
     pl.semaphore_wait(barrier, levels + 1)
 
     units = seqs * pairs
-    first = 9 + units
-    ticks = max(JOBS + LAGS[2 * levels], first + 3 + rows // JR)
-
-    def tick(t, carry):
+
+    def comm(step):
         for stage in range(2 * levels, -1, -1):
-            job = t - LAGS[stage]
+            job = step - LAGS[stage]
 
             @pl.when((job >= 0) & (job < JOBS))
             def _():
                 stage_op(stage, job)
 
+    def early(t, carry):
+        comm(t)
+
         @pl.when(t < 4)
         def _():
             down_phase(t)
@@ -546,27 +547,40 @@
         def _():
             out_phase()
 
-        @pl.when((t >= 9) & (t < first))
-        def _():
-            attend_phase(t - 9)
-
+        return carry
+
+    lax.fori_loop(0, 9, early, 0)
+
+    def middle(i, carry):
+        comm(9 + 3 * i)
+        attend_phase(2 * i)
+        comm(10 + 3 * i)
+        attend_phase(2 * i + 1)
+        comm(11 + 3 * i)
+        return carry
+
+    lax.fori_loop(0, units // 2, middle, 0)
+    at = 9 + 3 * (units // 2)
+
+    def late(t, carry):
+        comm(at + t)
         for i in range(3):
-            @pl.when(t == first + i)
+            @pl.when(t == i)
             def _():
                 proj_phase(i)
 
-        @pl.when((t >= first + 3) & (t < first + 3 + rows // JR))
-        def _():
-            dx_phase(t - first - 3)
+        @pl.when((t >= 3) & (t < 3 + rows // JR))
+        def _():
+            dx_phase(t - 3)
 
         for stage in range(levels + 2):
-            @pl.when(t == first + 1 + 2 * stage)
+            @pl.when(t == 1 + 2 * stage)
             def _():
                 sum_phase(stage)
 
         return carry
 
-    lax.fori_loop(0, ticks, tick, 0)
+    lax.fori_loop(0, max(JOBS + LAGS[2 * levels] - at, 2 * levels + 4), late, 0)
     for group in (GROUPS - 3, GROUPS - 2, GROUPS - 1):
         for i in range(3):
             core_copy(group * 3 + i).wait_send()

time: 239 us -> 232 us (0.971)
  Pallas kernels: 231 us -> 224 us
    pallas_call x1, Pallas kernels: 148 us -> 141 us  [backward(): pl.pallas_call(functools.partial(back_kernel, levels), out_shape=(jax.Sha...]
  transfers between devices with their start and end apart: 6 -> 6, of which waited for: 0 -> 0; matrix products, arithmetic and copies ran while one was open for 1% -> 1% of each run, Pallas kernels for 10% -> 11%
where the time goes in v3:
time: 232 us
  Pallas kernels  224 us (97%)
  local copies, waits for them, and re-layouts  4.67 us (2%)
    pallas_call x1, Pallas kernels, backward(): pl.pallas_call(functools.partial(back_kernel, levels), out_shape=(jax.Sha...  141 us
    pallas_call x1, Pallas kernels, ffn(): pl.pallas_call(functools.partial(ffn_kernel, chunk), grid=(rows // tile,)...  43.6 us
    pallas_call x2, Pallas kernels, attention(): pl.pallas_call(functools.partial(attn_kernel, qb), out_shape=(out, out, o...  24.9 us
    pallas_call x1, Pallas kernels, unpack(): pl.pallas_call(unpack_kernel, grid=(GROUPS,), out_shape=(jax.ShapeDtypeSt...  14.5 us
  transfers between devices with their start and end apart: 6, of which 0 were waited for; matrix products, arithmetic and copies ran while one was open for 1% of the time, Pallas kernels for 11%

profile of v3, /device:TPU:0, one launch (start us, length us, event | category | flops | bytes accessed | tf_op | source)
XLA Modules:
  0.0 231.7 jit_solution(17000756933173026075)
XLA Ops:
  0.6 0.6 collective-permute-start
  1.2 0.1 collective-permute-start.3
  1.3 0.4 collective-permute-start.5
  1.7 0.1 collective-permute-start.1
  1.8 0.7 reshape.31.bu_own
  2.5 0.0 copy-start
  2.5 0.4 collective-permute-start.4
  2.9 1.2 dynamic_slice.3.lens_ref
  4.2 0.0 copy-start.1
  4.2 0.0 copy-start.2
  4.2 0.0 copy-start.3
  4.2 0.0 copy-start.4
  4.2 0.0 copy-start.5
  4.2 0.0 copy-start.6
  4.2 0.0 copy-start.8
  4.2 12.5 %attend.2 = (bf16[1024,384]{1,0:T(8,128)(2,1)}, bf16[1024,384]{1,0:T(8,128)(2,1)}, bf16[1024,384]{1,0:T(8,128)(2,1)}, bf16[1024,384]{1,0:T(8,128)(2,1)}) custom-call(s32[2]{0:T(128)} %dynamic_slice.3.lens_ref, bf16[1024,768]{1,0:T(8,128)(2,1)} %x_in.1, bf16[3,768,384]{2,1,0:T(8,128)(2,1)} %w_own.1, f32[2,384]{1,0:T(2,128)} %b_ref.1), custom_call_target="tpu_custom_call" | custom-call | flops 7851737088 | bytes 12582912 | tf_op jit(solution)/shard_map/attend/pallas_call | solution.py:74
  16.7 0.0 copy-done
  16.7 0.0 copy-done.1
  16.8 0.0 copy-done.2
  16.8 0.0 copy-done.3
  16.8 0.0 copy-done.4
  16.8 0.0 copy-done.5
  16.8 0.0 copy-done.6
  16.9 0.6 stack.29.vec_ref
  17.5 0.0 collective-permute-done.1.b_ref
  17.5 0.0 copy-done.8
  17.5 0.0 copy-start.11
  17.5 0.1 collective-permute-start.2
  17.6 0.0 collective-permute-done.w_ref.w_peer
  17.7 0.4 copy-done.11
  18.1 12.4 %attend.3 = (bf16[1024,384]{1,0:T(8,128)(2,1)}, bf16[1024,384]{1,0:T(8,128)(2,1)}, bf16[1024,384]{1,0:T(8,128)(2,1)}, bf16[1024,384]{1,0:T(8,128)(2,1)}) custom-call(s32[2]{0:T(128)} %dynamic_slice.3.lens_ref, bf16[1024,768]{1,0:T(8,128)(2,1)} %x_in.1, bf16[3,768,384]{2,1,0:T(8,128)(2,1)} %collective-permute-done.w_ref.w_peer, f32[2,384]{1,0:T(2,128)} %copy-done.11), custom_call_target="tpu_custom_call" | custom-call | flops 7851737088 | bytes 12582912 | tf_op jit(solution)/shard_map/attend/pallas_call | solution.py:74
  30.5 0.0 collective-permute-done.4.bu_peer
  30.5 0.0 copy-start.10
  30.5 0.0 collective-permute-done.2.wo_peer
  30.5 0.0 copy-start.9
  30.5 0.0 collective-permute-done.3.wu_peer
  30.5 0.0 copy-start.7
  30.5 0.0 collective-permute-done.5.wd_peer
  30.5 0.5 copy-done.10
  31.1 0.2 copy-done.9
  31.3 0.8 copy-done.7
  32.1 43.6 %feed.1 = (f32[1024,768]{1,0:T(8,128)}, bf16[1024,1536]{1,0:T(8,128)(2,1)}, bf16[1024,1536]{1,0:T(8,128)(2,1)}, bf16[1024,1536]{1,0:T(8,128)(2,1)}, bf16[1024,15...) custom-call(bf16[1024,384]{1,0:T(8,128)(2,1)} %get-tuple-element.49., ...), custom_call_target="tpu_custom_call" | custom-call | flops 24159191040 | bytes 50331648 | tf_op jit(solution)/shard_map/feed/pallas_call | solution.py:198
  75.7 141.4 %backward.1 = (bf16[36,256,384]{2,1,0:T(8,128)(2,1)}, bf16[1024,768]{1,0:T(8,128)(2,1)}, f32[16,768]{1,0:T(8,128)}) custom-call(s32[2]{0:T(128)} %dynamic_slice.3.lens_ref, bf16[1024,1536]{1,0:T(8,128)(2,1)} %get-tuple-element.52.h_own, bf16[1024,1536]{1,0:T(8,128)(2,1)} %get-tuple-element.53.h_peer, bf16[1024,1536]{1,0:T(8,128)(2,1)} %get-tuple-element.54.gu_own, ...), custom_call_target="tpu_custom_call" | custom-call | flops 64424509440 | bytes 67108864 | tf_op jit(solution)/shard_map/backward/pallas_call | solution.py:605
  217.1 14.5 %unpack.1 = (f32[1024,768]{1,0:T(8,128)}, f32[3,768,384]{2,1,0:T(8,128)}, f32[2,384]{1,0:T(2,128)}, f32[384,768]{1,0:T(8,128)}, f32[768,1536]{1,0:T(8,128)}, /*i...) custom-call(bf16[36,256,384]{2,1,0:T(8,128)(2,1)} %get-tuple-element, ...), custom_call_target="tpu_custom_call" | custom-call | tf_op jit(solution)/shard_map/unpack/pallas_call | solution.py:684
  (6 shorter events, 0.0 us)
Async XLA Ops:
  0.6 17.0 %collective-permute-start = (bf16[3,768,384]{2,1,0:T(8,128)(2,1)}, bf16[3,768,384]{2,1,0:T(8,128)(2,1)}, u32[]{:S(2)}, u32[]{:S(2)}) collective-permute-start(bf16[3,768,384]{2,1,0:T(8,128)(2,1)} %w_own.1), channel_id=1, source_target_pairs={{0,1},{1,0},{2,3},{3,2},{4,5},{5,4},{6,7},{7,6},{8,9},{9,8},{10,11... | collective-permute-start | bytes 5308424 | tf_op jit(solution)/shard_map/ppermute | solution.py:711
  1.2 29.3 %collective-permute-start.3 = (bf16[768,1536]{1,0:T(8,128)(2,1)}, bf16[768,1536]{1,0:T(8,128)(2,1)S(1)}, u32[]{:S(2)}, u32[]{:S(2)}) collective-permute-start(bf16[768,1536]{1,0:T(8,128)(2,1)} %wu_own.1), channel_id=1, source_target_pairs={{0,1},{1,0},{2,3},{3,2},{4,5},{5,4},{6,7},{7,6},{8,9},{9,8},{10,11... | collective-permute-start | bytes 7077896 | tf_op jit(solution)/shard_map/ppermute | solution.py:711
  1.3 29.2 %collective-permute-start.5 = (bf16[1536,768]{1,0:T(8,128)(2,1)}, bf16[1536,768]{1,0:T(8,128)(2,1)}, u32[]{:S(2)}, u32[]{:S(2)}) collective-permute-start(bf16[1536,768]{1,0:T(8,128)(2,1)} %wd_own.1), channel_id=1, source_target_pairs={{0,1},{1,0},{2,3},{3,2},{4,5},{5,4},{6,7},{7,6},{8,9},{9,8},{10,11... | collective-permute-start | bytes 7077896 | tf_op jit(solution)/shard_map/ppermute | solution.py:711
  1.7 15.8 %collective-permute-start.1 = (f32[2,384]{1,0:T(2,128)}, f32[2,384]{1,0:T(2,128)S(1)}, u32[]{:S(2)}, u32[]{:S(2)}) collective-permute-start(f32[2,384]{1,0:T(2,128)} %b_ref.1), channel_id=1, source_target_pairs={{0,1},{1,0},{2,3},{3,2},{4,5},{5,4},{6,7},{7,6},{8,9},{9,8},{10,11... | collective-permute-start | bytes 9224 | tf_op jit(solution)/shard_map/ppermute | solution.py:711
  2.5 14.2 %copy-start = (f32[1,1536]{1,0:T(1,128)}, f32[1,1536]{1,0:T(1,128)S(1)}, u32[]{:S(2)}) copy-start(f32[1,1536]{1,0:T(1,128)S(1)} %reshape.31.bu_own) | copy-start | bytes 18436
  2.5 28.0 %collective-permute-start.4 = (f32[1,1536]{1,0:T(1,128)S(1)}, f32[1,1536]{1,0:T(1,128)S(1)}, u32[]{:S(2)}, u32[]{:S(2)}) collective-permute-start(f32[1,1536]{1,0:T(1,128)S(1)} %reshape.31.bu_own), channel_id=1, source_target_pairs={{0,1},{1,0},{2,3},{3,2},{4,5},{5,4},{6,7},{7,6},{8,9},{9,8},{10,11... | collective-permute-start | bytes 18440 | tf_op jit(solution)/shard_map/ppermute | solution.py:711
  4.2 12.6 %copy-start.1 = (f32[768]{0:T(1024)S(1)}, f32[768]{0:T(1024)}, u32[]{:S(2)}) copy-start(f32[768]{0:T(1024)} %param.20) | copy-start | bytes 9220
  4.2 12.6 %copy-start.2 = (f32[768]{0:T(1024)S(1)}, f32[768]{0:T(1024)}, u32[]{:S(2)}) copy-start(f32[768]{0:T(1024)} %param.21) | copy-start | bytes 9220
  4.2 12.6 %copy-start.3 = (f32[768]{0:T(1024)S(1)}, f32[768]{0:T(1024)}, u32[]{:S(2)}) copy-start(f32[768]{0:T(1024)} %param.22) | copy-start | bytes 9220
  4.2 12.6 %copy-start.4 = (f32[768]{0:T(1024)S(1)}, f32[768]{0:T(1024)}, u32[]{:S(2)}) copy-start(f32[768]{0:T(1024)} %param.26) | copy-start | bytes 9220
  4.2 12.6 %copy-start.5 = (f32[768]{0:T(1024)S(1)}, f32[768]{0:T(1024)}, u32[]{:S(2)}) copy-start(f32[768]{0:T(1024)} %param.27) | copy-start | bytes 9220
  4.2 12.7 %copy-start.6 = (f32[768]{0:T(1024)S(1)}, f32[768]{0:T(1024)}, u32[]{:S(2)}) copy-start(f32[768]{0:T(1024)} %param.28) | copy-start | bytes 9220
  4.2 13.3 %copy-start.8 = (bf16[384,768]{1,0:T(8,128)(2,1)S(1)}, bf16[384,768]{1,0:T(8,128)(2,1)}, u32[]{:S(2)}) copy-start(bf16[384,768]{1,0:T(8,128)(2,1)} %wo_own.1) | copy-start | bytes 1769476
  17.5 0.6 copy-start.11
  17.5 13.0 %collective-permute-start.2 = (bf16[384,768]{1,0:T(8,128)(2,1)S(1)}, bf16[384,768]{1,0:T(8,128)(2,1)S(1)}, u32[]{:S(2)}, u32[]{:S(2)}) collective-permute-start(bf16[384,768]{1,0:T(8,128)(2,1)S(1)} %copy-done.8), channel_id=1, source_target_pairs={{0,1},{1,0},{2,3},{3,2},{4,5},{5,4},{6,7},{7,6},{8,9},{9,8},{10,11... | collective-permute-start | bytes 1769480 | tf_op jit(solution)/shard_map/ppermute | solution.py:711
  30.5 0.6 copy-start.10
  30.5 0.8 copy-start.9
  30.5 1.6 copy-start.7

commit v4 on v2

--- a/solution.py
+++ b/solution.py
@@ -119,8 +119,7 @@
 def ffn_kernel(
     chunk,
     c_own, c_peer, x_ref, cot_ref, wo_own, wo_peer, wu_own, wu_peer, bu_own, bu_peer, wd_own, wd_peer, vec_ref,
-    out_ref, h_own, h_peer, gu_own, gu_peer, mid_ref, glow_ref, flow_ref, gctx_ref, gf_ref, small_ref,
-    gp_ref,
+    out_ref, h_own, h_peer, gp_own, gp_peer, mid_ref, glow_ref, gs_ref, fin_ref, small_ref,
 ):
     step = pl.program_id(0)
     wide = wu_own.shape[1]
@@ -134,20 +133,21 @@
         small_ref[index:index + 1, :] += jnp.sum(value, axis=0, keepdims=True)
 
     attn_sum = dot(c_own[...], wo_own[...]) + dot(c_peer[...], wo_peer[...])
-    n1, root1 = norm_stats(x_ref[...].astype(F32) + attn_sum + out_bias)
+    first_in = x_ref[...].astype(F32) + attn_sum + out_bias
+    fin_ref[...] = first_in
+    n1, _ = norm_stats(first_in)
     first_out = n1 * gain1 + shift1
     middle = first_out.astype(BF)
     mid_ref[...] = middle
     ffn_sum = jnp.zeros_like(first_out)
-    groups = ((wu_own, bu_own, wd_own, h_own, gu_own, 0), (wu_peer, bu_peer, wd_peer, h_peer, gu_peer, wide))
-    for wu, bu, wd, h_ref, _, base in groups:
+    for wu, bu, wd, h_ref, gp_ref in ((wu_own, bu_own, wd_own, h_own, gp_own), (wu_peer, bu_peer, wd_peer, h_peer, gp_peer)):
         for at in range(0, wide, chunk):
             cols = slice(at, at + chunk)
             u = dot(middle, wu[:, cols]) + bu[:, cols]
             act, slope = gelu_both(u)
             act = act.astype(BF)
             h_ref[:, cols] = act
-            gp_ref[:, base + at:base + at + chunk] = slope
+            gp_ref[:, cols] = slope.astype(BF)
             ffn_sum = ffn_sum + dot(act, wd[cols, :])
     n2, root2 = norm_stats(first_out + ffn_sum + down_bias)
     out_ref[...] = n2 * gain2 + shift2
@@ -156,27 +156,8 @@
     colsum(5, cot)
     grad_second = norm_back(cot * gain2, n2, root2)
     colsum(3, grad_second)
-    glow = grad_second.astype(BF)
-    glow_ref[...] = glow
-    grad_first_out = grad_second
-    for wu, _, wd, _, gu_ref, base in groups:
-        for at in range(0, wide, chunk):
-            cols = slice(at, at + chunk)
-            grad_hidden = dot_nt(glow, wd[cols, :])
-            gu = (grad_hidden * gp_ref[:, base + at:base + at + chunk]).astype(BF)
-            gu_ref[:, cols] = gu
-            colsum(8 + (base + at) // chunk, gu.astype(F32))
-            grad_first_out = grad_first_out + dot_nt(gu, wu[:, cols])
-    colsum(1, grad_first_out * n1)
-    colsum(2, grad_first_out)
-    grad_first = norm_back(grad_first_out * gain1, n1, root1)
-    colsum(0, grad_first)
-    gf_ref[...] = grad_first
-    flow = grad_first.astype(BF)
-    flow_ref[...] = flow
-    half = wo_own.shape[0]
-    gctx_ref[:, :half] = dot_nt(flow, wo_own[...]).astype(BF)
-    gctx_ref[:, half:] = dot_nt(flow, wo_peer[...]).astype(BF)
+    glow_ref[...] = grad_second.astype(BF)
+    gs_ref[...] = grad_second
 
 
 def ffn(c_own, c_peer, x, cot, wo_own, wo_peer, wu_own, wu_peer, bu_own, bu_peer, wd_own, wd_peer, vecs, tile=256):
@@ -200,18 +181,17 @@
         grid=(rows // tile,),
         out_shape=(
             sds(depth, F32), sds(wide, BF), sds(wide, BF), sds(wide, BF), sds(wide, BF),
-            sds(depth, BF), sds(depth, BF), sds(depth, BF), sds(2 * half, BF), sds(depth, F32),
+            sds(depth, BF), sds(depth, BF), sds(depth, F32), sds(depth, F32),
             jax.ShapeDtypeStruct((16, depth), F32),
         ),
         in_specs=[tiled(half), tiled(half), tiled(depth), tiled(depth)] + [fixed(a.shape) for a in fixed_in],
         out_specs=[
             tiled(depth), tiled(wide), tiled(wide), tiled(wide), tiled(wide),
-            tiled(depth), tiled(depth), tiled(depth), tiled(2 * half), tiled(depth),
+            tiled(depth), tiled(depth), tiled(depth), tiled(depth),
             pl.BlockSpec((16, depth), lambda i: (0, 0)),
         ],
-        scratch_shapes=[pltpu.VMEM((tile, 2 * wide), F32)],
         compiler_params=pltpu.CompilerParams(vmem_limit_bytes=60 << 20),
-        cost_estimate=pl.CostEstimate(flops=rows * depth * (8 * 2 * wide + 8 * depth), bytes_accessed=48 << 20, transcendentals=rows * wide * 2),
+        cost_estimate=pl.CostEstimate(flops=rows * depth * (4 * 2 * wide + 4 * depth), bytes_accessed=48 << 20, transcendentals=rows * wide * 2),
         name="feed",
     )(c_own, c_peer, x, cot, *fixed_in)
 
@@ -224,10 +204,11 @@
 
 def back_kernel(
     levels,
-    lens_ref, h_own, h_peer, gu_own, gu_peer, glow_in, mid_in, flow_in, c_own, c_peer, q_own, q_peer, k_own, k_peer, v_own, v_peer, gctx_in, x_in, w_own, w_peer, small_in,
+    lens_ref, h_own, h_peer, gp_own, gp_peer, glow_in, mid_in, gs_in, fin_in, c_own, c_peer, q_own, q_peer, k_own, k_peer, v_own, v_peer, x_in, w_own, w_peer, small_in,
+    wu_own, wu_peer, wd_own, wd_peer, wo_own, wo_peer, vec_in,
     job_out, dx_out, small_out,
-    buf, ring, prec, rbuf, blocks, glow, mid, flow, ctx, qv, kv, vv, dov, xv, wv, dq, dk, dv, dxs, small, small_sum, small_send, small_recv,
-    load_sem, blk_sem, core_send, core_recv, hop_send, hop_recv, out_sem, dx_sem, small_sem, sum_send, sum_recv,
+    buf, ring, prec, rbuf, blocks, glow, mid, flow, ctx, qv, kv, vv, dov, wv, wdb, acc, fin, vec, dq, dk, dv, dxs, small, small_sum, small_send, small_recv,
+    load_sem, blk_sem, wt_sem, core_send, core_recv, hop_send, hop_recv, out_sem, dx_sem, small_sem, sum_send, sum_recv,
 ):
     dp = lax.axis_index("dp")
     core = lax.axis_index("tensor")
@@ -247,9 +228,10 @@
 
     def loads():
         return (
-            (glow_in, glow, 0), (mid_in, mid, 1), (c_own, ctx.at[:, :half], 2), (c_peer, ctx.at[:, half:], 3), (flow_in, flow, 4),
+            (glow_in, glow, 0), (mid_in, mid, 1), (c_own, ctx.at[:, :half], 2), (c_peer, ctx.at[:, half:], 3), (gs_in, acc, 4),
             (q_own, qv.at[:, :half], 5), (q_peer, qv.at[:, half:], 6), (k_own, kv.at[:, :half], 7), (k_peer, kv.at[:, half:], 8),
-            (v_own, vv.at[:, :half], 9), (v_peer, vv.at[:, half:], 10), (gctx_in, dov, 11), (x_in, xv, 12), (w_own, wv.at[0], 13), (w_peer, wv.at[1], 14), (small_in, small, 15),
+            (v_own, vv.at[:, :half], 9), (v_peer, vv.at[:, half:], 10), (fin_in, fin, 11), (x_in, mid, 12), (w_own, wv.at[0], 13), (w_peer, wv.at[1], 14), (small_in, small, 15),
+            (vec_in, vec, 16), (wo_own, wdb.at[0, 0], 17), (wo_peer, wdb.at[0, 1], 18),
         )
 
     def load(index):
@@ -271,7 +253,21 @@
 
         @pl.when((index >= 4) & (index < 8))
         def _():
-            for copy in block_copies(gu_own, gu_peer, index - 4, index % 2):
+            for copy in block_copies(gp_own, gp_peer, index - 4, index % 2):
+                copy.start()
+
+    def weight_copies(index, side):
+        slot = index % 2
+        span = pl.ds(pl.multiple_of(index * JC, 128), JC)
+        up, down = ((wu_own, wd_own), (wu_peer, wd_peer))[side]
+        return (
+            pltpu.make_async_copy(up.at[:, span], wv.at[side, slot], wt_sem.at[0, slot, side]),
+            pltpu.make_async_copy(down.at[span], wdb.at[slot, side], wt_sem.at[1, slot, side]),
+        )
+
+    def start_weights(index):
+        for side in range(2):
+            for copy in weight_copies(index, side):
                 copy.start()
 
     def core_copy(job):
@@ -330,20 +326,20 @@
         else:
             pltpu.make_async_copy(prec.at[job], job_out.at[job], out_sem.at[job]).start()
 
+    def emit_side(group, which, pieces):
+        for i, (top, bottom) in enumerate(pieces):
+            job = group * 3 + i
+            target = buf.at[job] if which == 0 else ring.at[job % 9]
+            cut = top.shape[0]
+            target[:cut, :] = top.astype(BF)
+            if bottom is not None:
+                target[cut:, :] = bottom.astype(BF)
+            if which == 1:
+                core_copy(job).start()
+
     def emit(group, own, peer):
-        for which, pieces in ((0, own), (1, peer)):
-            for i, (top, bottom) in enumerate(pieces):
-                job = group * 3 + i
-                if which == 0:
-                    target = buf.at[job]
-                else:
-                    target = ring.at[job % 9]
-                cut = top.shape[0]
-                target[:cut, :] = top.astype(BF)
-                if bottom is not None:
-                    target[cut:, :] = bottom.astype(BF)
-                if which == 1:
-                    core_copy(job).start()
+        emit_side(group, 0, own)
+        emit_side(group, 1, peer)
 
     def free_ring(group):
         @pl.when(group >= 3)
@@ -370,21 +366,72 @@
         emit(index, slabs(dot_tn(blocks[slot, 0], right)), slabs(dot_tn(blocks[slot, 1], right)))
         start_blocks(index + 2)
 
-    def up_phase(index):
+    def up_phase(index, side):
+        slot = index % 2
+        if side == 0:
+            @pl.when(index == 0)
+            def _():
+                for i in (1, 4, 15):
+                    load(i).wait()
+
+            free_ring(index + 4)
+        block_copies(gp_own, gp_peer, index, slot)[side].wait()
+        for copy in weight_copies(index, side):
+            copy.wait()
+        grad_up = (dot_nt(glow[...], wdb[slot, side]) * blocks[slot, side].astype(F32)).astype(BF)
+        total = jnp.sum(grad_up.astype(F32), axis=0, keepdims=True)
+        for row in range(2):
+            @pl.when(index // 2 == row)
+            def _():
+                lanes = pl.ds(pl.multiple_of((index % 2) * JC, 128), JC)
+                small[8 + 2 * side + row:9 + 2 * side + row, lanes] = total
+        emit_side(index + 4, side, tall(dot_tn(mid[...], grad_up)))
+        acc[...] = acc[...] + dot_nt(grad_up, wv[side, slot])
+        if side == 1:
+            start_blocks(index + 6)
+
+            @pl.when(index < 2)
+            def _():
+                start_weights(index + 2)
+
+            @pl.when(index == 2)
+            def _():
+                load(17).start()
+                load(18).start()
+
+            @pl.when(index == 3)
+            def _():
+                for i in (12, 13, 14):
+                    load(i).start()
+
+    def norm_phase(index):
         @pl.when(index == 0)
         def _():
-            load(1).wait()
-
-        slot = index % 2
-        for copy in block_copies(gu_own, gu_peer, index, slot):
-            copy.wait()
-        free_ring(index + 4)
-        left = mid[...]
-        emit(index + 4, tall(dot_tn(left, blocks[slot, 0])), tall(dot_tn(left, blocks[slot, 1])))
-        start_blocks(index + 6)
+            for i in (11, 16, 17, 18):
+                load(i).wait()
+            small[0:3, :] = jnp.zeros((3, depth), F32)
+
+        gain1 = vec[1:2, :]
+
+        def piece(i, carry):
+            span = pl.ds(pl.multiple_of(index * (rows // 2) + i * JR, JR), JR)
+            n1, root1 = norm_stats(fin[span, :])
+            grad = acc[span, :]
+            small[1:2, :] += jnp.sum(grad * n1, axis=0, keepdims=True)
+            small[2:3, :] += jnp.sum(grad, axis=0, keepdims=True)
+            grad_first = norm_back(grad * gain1, n1, root1)
+            small[0:1, :] += jnp.sum(grad_first, axis=0, keepdims=True)
+            acc[span, :] = grad_first
+            low = grad_first.astype(BF)
+            flow[span, :] = low
+            dov[span, :half] = dot_nt(low, wdb[0, 0]).astype(BF)
+            dov[span, half:] = dot_nt(low, wdb[0, 1]).astype(BF)
+            return carry
+
+        lax.fori_loop(0, rows // 2 // JR, piece, 0)
 
     def out_phase():
-        for i in (2, 3, 4):
+        for i in (2, 3):
             load(i).wait()
         free_ring(8)
         right = flow[...]
@@ -433,13 +480,13 @@
     def attend_phase(unit):
         @pl.when(unit == 0)
         def _():
-            for i in range(5, 12):
+            for i in range(5, 11):
                 load(i).wait()
-            load(15).wait()
             small[12:14, :] = jnp.zeros((2, depth), F32)
 
-        seq = unit // pairs
-        pair = unit % pairs
+        inner = unit % (2 * seqs)
+        seq = inner % seqs
+        pair = unit // (2 * seqs) + (inner // seqs) * (pairs // 2)
         length = lens_ref[seq]
         span = pl.ds(pl.multiple_of(seq * seq_len, seq_len), seq_len)
         lanes = pl.ds(pl.multiple_of(pair * 128, 128), 128)
@@ -479,12 +526,16 @@
         add_bias(pair, half, grad_v)
 
     def proj_phase(index):
-        if index == 0:
+        @pl.when(index == 0)
+        def _():
             load(12).wait()
-        free_ring(jnp.int32(index + 9))
-        left = xv[...]
-        grad = (dq, dk, dv)[index]
-        emit(index + 9, tall(dot_tn(left, grad[:, :half])), tall(dot_tn(left, grad[:, half:])))
+
+        free_ring(index + 9)
+        left = mid[...]
+        for side in range(2):
+            lanes = pl.ds(pl.multiple_of(side * half + index * 128, 128), 128)
+            right = jnp.concatenate([dq[:, lanes], dk[:, lanes], dv[:, lanes]], axis=1)
+            emit_side(index + 9, side, tall(dot_tn(left, right)))
 
     def dx_copy(index):
         span = pl.ds(pl.multiple_of(index * JR, JR), JR)
@@ -508,7 +559,7 @@
             for i, grad in enumerate((dq, dk, dv)):
                 part = part + dot_nt(grad[span, cols], wv[side, i])
             total = total + part
-        dxs[index % 2] = total.astype(BF)
+        dxs[index % 2] = total + acc[span, :]
         dx_copy(index).start()
 
     barrier = pltpu.get_barrier_semaphore()
@@ -518,55 +569,69 @@
     load(0).start()
     start_blocks(0)
     start_blocks(1)
-    for i in range(1, 16):
+    load(1).start()
+    start_weights(0)
+    start_weights(1)
+    for i in (4, 15, 11, 16, 2, 3, 5, 6, 7, 8, 9, 10):
         load(i).start()
     pl.semaphore_wait(barrier, levels + 1)
 
     units = seqs * pairs
-    first = 9 + units
-    ticks = max(JOBS + LAGS[2 * levels], first + 3 + rows // JR)
-
-    def tick(t, carry):
+
+    def comm(step):
         for stage in range(2 * levels, -1, -1):
-            job = t - LAGS[stage]
+            job = step - LAGS[stage]
 
             @pl.when((job >= 0) & (job < JOBS))
             def _():
                 stage_op(stage, job)
 
+    first = 4 + 2 * 4 + 3
+    after = first + 3 * (units // 2)
+    turn = 2 * seqs // 2 * 3
+
+    def tick(t, carry):
+        comm(t)
+
         @pl.when(t < 4)
         def _():
             down_phase(t)
 
-        @pl.when((t >= 4) & (t < 8))
-        def _():
-            up_phase(t - 4)
-
-        @pl.when(t == 8)
+        for side in range(2):
+            @pl.when((t >= 4) & (t < 12) & (t % 2 == side))
+            def _():
+                up_phase((t - 4) // 2, side)
+
+        @pl.when((t >= 12) & (t < 14))
+        def _():
+            norm_phase(t - 12)
+
+        @pl.when(t == 14)
         def _():
             out_phase()
 
-        @pl.when((t >= 9) & (t < first))
-        def _():
-            attend_phase(t - 9)
-
-        for i in range(3):
-            @pl.when(t == first + i)
-            def _():
-                proj_phase(i)
-
-        @pl.when((t >= first + 3) & (t < first + 3 + rows // JR))
-        def _():
-            dx_phase(t - first - 3)
+        spot = t - first
+
+        @pl.when((spot > 0) & (spot <= after - first) & (spot % turn == 0))
+        def _():
+            proj_phase(spot // turn - 1)
+
+        @pl.when((spot >= 0) & (t < after) & (spot % 3 < 2))
+        def _():
+            attend_phase(spot // 3 * 2 + spot % 3)
+
+        @pl.when((t > after) & (t <= after + rows // JR))
+        def _():
+            dx_phase(t - after - 1)
 
         for stage in range(levels + 2):
-            @pl.when(t == first + 1 + 2 * stage)
+            @pl.when(t == after + 1 + 2 * stage)
             def _():
                 sum_phase(stage)
 
         return carry
 
-    lax.fori_loop(0, ticks, tick, 0)
+    lax.fori_loop(0, max(JOBS + LAGS[2 * levels], after + 2 * levels + 4), tick, 0)
     for group in (GROUPS - 3, GROUPS - 2, GROUPS - 1):
         for i in range(3):
             core_copy(group * 3 + i).wait_send()
@@ -582,7 +647,7 @@
 
 
 def backward(levels, lens, arrays):
-    h_own, glow, c_own, x = arrays[0], arrays[4], arrays[7], arrays[16]
+    glow, c_own = arrays[4], arrays[8]
     rows, depth = glow.shape
     half = c_own.shape[1]
     hbm = pl.BlockSpec(memory_space=pl.ANY)
@@ -592,7 +657,7 @@
         functools.partial(back_kernel, levels),
         out_shape=(
             jax.ShapeDtypeStruct((JOBS, JR, JC), BF),
-            jax.ShapeDtypeStruct((rows, depth), BF),
+            jax.ShapeDtypeStruct((rows, depth), F32),
             jax.ShapeDtypeStruct((16, depth), F32),
         ),
         in_specs=[pl.BlockSpec(memory_space=pltpu.SMEM)] + [hbm] * len(arrays),
@@ -600,11 +665,11 @@
         scratch_shapes=[
             pltpu.VMEM((JOBS, JR, JC), BF), pltpu.VMEM((9, JR, JC), BF), pltpu.VMEM((JOBS, JR, JC), BF),
             pltpu.VMEM((JOBS, JR - (JR >> levels), JC), BF), pltpu.VMEM((2, 2, rows, JC), BF),
-            square, square, square, square, square, square, square, square, square,
-            pltpu.VMEM((2, 3, depth, half), BF), square, square, square,
-            pltpu.VMEM((2, JR, depth), BF), pltpu.VMEM((16, depth), F32),
+            square, square, square, square, square, square, square, square,
+            pltpu.VMEM((2, 3, depth, half), BF), pltpu.VMEM((2, 2, JC, depth), BF), pltpu.VMEM((rows, depth), F32), pltpu.VMEM((rows, depth), F32), pltpu.VMEM((8, depth), F32), square, square, square,
+            pltpu.VMEM((2, JR, depth), F32), pltpu.VMEM((16, depth), F32),
             pltpu.VMEM((levels + 1, 16, depth), F32), pltpu.VMEM((16, depth), F32), pltpu.VMEM((levels + 1, 16, depth), F32),
-            dma((16,)), dma((2, 2)), dma((JOBS,)), dma((JOBS,)), dma((2 * levels, JOBS)), dma((2 * levels, JOBS)), dma((JOBS,)), dma((2,)), dma(()), dma((levels + 1,)), dma((levels + 1,)),
+            dma((19,)), dma((2, 2)), dma((2, 2, 2)), dma((JOBS,)), dma((JOBS,)), dma((2 * levels, JOBS)), dma((2 * levels, JOBS)), dma((JOBS,)), dma((2,)), dma(()), dma((levels + 1,)), dma((levels + 1,)),
         ],
         compiler_params=pltpu.CompilerParams(vmem_limit_bytes=67043328, collective_id=1, has_side_effects=True),
         cost_estimate=pl.CostEstimate(flops=60 << 30, bytes_accessed=64 << 20, transcendentals=8 << 20),
@@ -612,7 +677,7 @@
     )(lens, *arrays)
 
 
-def unpack_kernel(jobs_ref, gf_ref, dx_ref, small_ref, tok_ref, qkv_ref, qvb_ref, out_ref, up_ref, upb_ref, down_ref, *vec_refs):
+def unpack_kernel(jobs_ref, dx_ref, small_ref, tok_ref, qkv_ref, qvb_ref, out_ref, up_ref, upb_ref, down_ref, *vec_refs):
     step = pl.program_id(0)
     depth = small_ref.shape[1]
 
@@ -629,7 +694,7 @@
     @pl.when(step < 4)
     def _():
         unslab(down_ref)
-        tok_ref[...] = gf_ref[...] + dx_ref[...].astype(F32)
+        tok_ref[...] = dx_ref[...]
 
     @pl.when((step >= 4) & (step < 8))
     def _():
@@ -649,11 +714,12 @@
     @pl.when(step >= 9)
     def _():
         for i in range(3):
-            qkv_ref[0, i * JR:(i + 1) * JR, :] = jobs_ref[i].astype(F32)
-
-
-def unpack(jobs, grad_first, dx, small, wide):
-    rows, depth = grad_first.shape
+            for c in range(3):
+                qkv_ref[c, i * JR:(i + 1) * JR, :] = jobs_ref[i, :, c * 128:c * 128 + 128].astype(F32)
+
+
+def unpack(jobs, dx, small, wide):
+    rows, depth = dx.shape
 
     def rows_at(i):
         return (jnp.minimum(i, 3), 0)
@@ -675,14 +741,14 @@
             jax.ShapeDtypeStruct((JC, depth), F32), jax.ShapeDtypeStruct((depth, wide), F32), jax.ShapeDtypeStruct((wide,), F32),
             jax.ShapeDtypeStruct((wide, depth), F32), vec, vec, vec, vec, vec, vec,
         ),
-        in_specs=[pl.BlockSpec((3, JR, JC), lambda i: (i, 0, 0)), quarter, quarter, whole((16, depth))],
+        in_specs=[pl.BlockSpec((3, JR, JC), lambda i: (i, 0, 0)), quarter, whole((16, depth))],
         out_specs=[
-            quarter, pl.BlockSpec((1, depth, JC), lambda i: (jnp.clip(i - 9, 0, 2), 0, 0)), whole((2, JC)), whole((JC, depth)),
+            quarter, pl.BlockSpec((3, depth, 128), lambda i: (0, 0, jnp.clip(i - 9, 0, 2))), whole((2, JC)), whole((JC, depth)),
             pl.BlockSpec((depth, JC), lambda i: (0, jnp.clip(i - 4, 0, 3))), flat(wide), pl.BlockSpec((JC, depth), rows_at),
         ] + [flat(depth)] * 6,
         compiler_params=pltpu.CompilerParams(vmem_limit_bytes=62 << 20),
         name="unpack",
-    )(jobs, grad_first, dx, small)
+    )(jobs, dx, small)
 
 
 def body(tokens, lengths, qkv_weight, qv_bias, out_weight, out_bias, first_gain, first_shift, up_weight, up_bias, down_weight, down_bias, second_gain, second_shift, cotangent):
@@ -702,18 +768,21 @@
     q_own, k_own, v_own, c_own = attention(lens, tokens, qkv_weight, qv_bias)
     q_peer, k_peer, v_peer, c_peer = attention(lens, tokens, peer_qkv, peer_qv_bias)
     vecs = jnp.stack([out_bias, first_gain, first_shift, down_bias, second_gain, second_shift, out_bias, out_bias])
-    layer_out, h_own, h_peer, gu_own, gu_peer, mid, glow, flow, gctx, grad_first, sums = ffn(
+    layer_out, h_own, h_peer, gp_own, gp_peer, mid, glow, grad_second, first_in, sums = ffn(
         c_own, c_peer, tokens, cotangent, out_weight, peer_out, up_weight, peer_up, up_row, peer_up_row, down_weight, peer_down, vecs
     )
     jobs, dx, sums = backward(
         levels, lens,
-        (h_own, h_peer, gu_own, gu_peer, glow, mid, flow, c_own, c_peer, q_own, q_peer, k_own, k_peer, v_own, v_peer, gctx, tokens, qkv_weight, peer_qkv, sums),
+        (
+            h_own, h_peer, gp_own, gp_peer, glow, mid, grad_second, first_in, c_own, c_peer, q_own, q_peer, k_own, k_peer, v_own, v_peer, tokens, qkv_weight, peer_qkv, sums,
+            up_weight, peer_up, down_weight, peer_down, out_weight, peer_out, vecs,
+        ),
     )
     inner = 1 << levels
     if n_dp > inner:
         groups = [[i + inner * g for g in range(n_dp // inner)] for i in range(inner)]
         jobs, sums = lax.psum((jobs, sums), "dp", axis_index_groups=groups)
-    grad_tokens, grad_qkv, grad_qv_bias, grad_out, grad_up, grad_up_bias, grad_down, *vectors = unpack(jobs, grad_first, dx, sums, up_bias.shape[0])
+    grad_tokens, grad_qkv, grad_qv_bias, grad_out, grad_up, grad_up_bias, grad_down, *vectors = unpack(jobs, dx, sums, up_bias.shape[0])
     return (
         layer_out, grad_tokens, grad_qkv, grad_qv_bias, grad_out, vectors[0], vectors[1], vectors[2],
         grad_up, grad_up_bias, grad_down, vectors[3], vectors[4], vectors[5],

time: 239 us -> 231 us (0.967)
  Pallas kernels: 231 us -> 224 us
    pallas_call x1, Pallas kernels: 43.6 us -> 30.6 us  [ffn(): pl.pallas_call(functools.partial(ffn_kernel, chunk), grid=(rows // tile,)...]
    pallas_call x1, Pallas kernels: 148 us -> 155 us  [backward(): pl.pallas_call(functools.partial(back_kernel, levels), out_shape=(jax.Sha...]
  transfers between devices with their start and end apart: 6 -> 6, of which waited for: 0 -> 0; matrix products, arithmetic and copies ran while one was open for 1% -> 1% of each run, Pallas kernels for 10% -> 11%
where the time goes in v4:
time: 231 us
  Pallas kernels  224 us (97%)
  local copies, waits for them, and re-layouts  4.01 us (2%)
    pallas_call x1, Pallas kernels, backward(): pl.pallas_call(functools.partial(back_kernel, levels), out_shape=(jax.Sha...  155 us
    pallas_call x1, Pallas kernels, ffn(): pl.pallas_call(functools.partial(ffn_kernel, chunk), grid=(rows // tile,)...  30.6 us
    pallas_call x2, Pallas kernels, attention(): pl.pallas_call(functools.partial(attn_kernel, qb), out_shape=(out, out, o...  24.8 us
    pallas_call x1, Pallas kernels, unpack(): pl.pallas_call(unpack_kernel, grid=(GROUPS,), out_shape=(jax.ShapeDtypeSt...  13.8 us
  transfers between devices with their start and end apart: 6, of which 0 were waited for; matrix products, arithmetic and copies ran while one was open for 1% of the time, Pallas kernels for 11%

profile of v4, /device:TPU:0, one launch (start us, length us, event | category | flops | bytes accessed | tf_op | source)
XLA Modules:
  0.0 230.7 jit_solution(1149779907654401146)
XLA Ops:
  0.6 0.6 collective-permute-start
  1.2 0.1 collective-permute-start.3
  1.3 0.4 collective-permute-start.5
  1.7 0.1 collective-permute-start.1
  1.8 0.4 collective-permute-start.2
  2.2 1.2 dynamic_slice.3.lens_ref
  3.5 0.0 copy-start
  3.5 0.0 copy-start.2
  3.5 0.0 copy-start.3
  3.5 0.0 copy-start.4
  3.5 0.0 copy-start.5
  3.5 0.0 copy-start.6
  3.5 0.0 copy-start.7
  3.5 12.5 %attend.2 = (bf16[1024,384]{1,0:T(8,128)(2,1)}, bf16[1024,384]{1,0:T(8,128)(2,1)}, bf16[1024,384]{1,0:T(8,128)(2,1)}, bf16[1024,384]{1,0:T(8,128)(2,1)}) custom-call(s32[2]{0:T(128)} %dynamic_slice.3.lens_ref, bf16[1024,768]{1,0:T(8,128)(2,1)} %x_in.1, bf16[3,768,384]{2,1,0:T(8,128)(2,1)} %w_own.1, f32[2,384]{1,0:T(2,128)} %b_ref.1), custom_call_target="tpu_custom_call" | custom-call | flops 7851737088 | bytes 12582912 | tf_op jit(solution)/shard_map/attend/pallas_call | solution.py:74
  16.0 0.0 copy-done
  16.0 0.0 copy-done.2
  16.0 0.0 copy-start.1
  16.0 0.0 copy-done.3
  16.1 0.0 copy-done.4
  16.1 0.0 copy-done.5
  16.1 0.0 copy-done.6
  16.1 0.0 copy-done.7
  16.1 0.7 stack.29.vec_ref.vec_in
  16.8 0.0 collective-permute-done.1.b_ref
  16.8 0.0 copy-start.11
  16.8 0.1 collective-permute-start.4
  16.9 0.0 collective-permute-done.w_ref.w_peer
  16.9 0.5 copy-done.11
  17.4 12.4 %attend.3 = (bf16[1024,384]{1,0:T(8,128)(2,1)}, bf16[1024,384]{1,0:T(8,128)(2,1)}, bf16[1024,384]{1,0:T(8,128)(2,1)}, bf16[1024,384]{1,0:T(8,128)(2,1)}) custom-call(s32[2]{0:T(128)} %dynamic_slice.3.lens_ref, bf16[1024,768]{1,0:T(8,128)(2,1)} %x_in.1, bf16[3,768,384]{2,1,0:T(8,128)(2,1)} %collective-permute-done.w_ref.w_peer, f32[2,384]{1,0:T(2,128)} %copy-done.11), custom_call_target="tpu_custom_call" | custom-call | flops 7851737088 | bytes 12582912 | tf_op jit(solution)/shard_map/attend/pallas_call | solution.py:74
  29.7 0.0 copy-done.1
  29.7 0.0 collective-permute-done.4.bu_peer
  29.8 0.0 copy-start.10
  29.8 0.0 collective-permute-done.2.wo_peer
  29.8 0.0 copy-start.9
  29.8 0.0 collective-permute-done.3.wu_peer
  29.8 0.0 copy-start.8
  29.8 0.0 collective-permute-done.5.wd_peer
  29.8 0.5 copy-done.10
  30.3 0.3 copy-done.9
  30.6 0.7 copy-done.8
  31.4 30.6 %feed.1 = (f32[1024,768]{1,0:T(8,128)}, bf16[1024,1536]{1,0:T(8,128)(2,1)}, bf16[1024,1536]{1,0:T(8,128)(2,1)}, bf16[1024,1536]{1,0:T(8,128)(2,1)}, bf16[1024,15...) custom-call(bf16[1024,384]{1,0:T(8,128)(2,1)} %get-tuple-element.48., ...), custom_call_target="tpu_custom_call" | custom-call | flops 12079595520 | bytes 50331648 | tf_op jit(solution)/shard_map/feed/pallas_call | solution.py:179
  61.9 154.8 %backward.1 = (bf16[36,256,384]{2,1,0:T(8,128)(2,1)}, f32[1024,768]{1,0:T(8,128)}, f32[16,768]{1,0:T(8,128)}) custom-call(s32[2]{0:T(128)} %dynamic_slice.3.lens_ref, bf16[1024,1536]{1,0:T(8,128)(2,1)} %get-tuple-element.51.h_own, bf16[1024,1536]{1,0:T(8,128)(2,1)} %get-tuple-element.52.h_peer, bf16[1024,1536]{1,0:T(8,128)(2,1)} %get-tuple-element.53.gp_own, ...), custom_call_target="tpu_custom_call" | custom-call | flops 64424509440 | bytes 67108864 | tf_op jit(solution)/shard_map/backward/pallas_call | solution.py:656
  216.7 13.8 %unpack.1 = (f32[1024,768]{1,0:T(8,128)}, f32[3,768,384]{2,1,0:T(8,128)}, f32[2,384]{1,0:T(2,128)}, f32[384,768]{1,0:T(8,128)}, f32[768,1536]{1,0:T(8,128)}, /*i...) custom-call(bf16[36,256,384]{2,1,0:T(8,128)(2,1)} %get-tuple-element, ...), custom_call_target="tpu_custom_call" | custom-call | tf_op jit(solution)/shard_map/unpack/pallas_call | solution.py:736
  (7 shorter events, 0.0 us)
Async XLA Ops:
  0.6 16.3 %collective-permute-start = (bf16[3,768,384]{2,1,0:T(8,128)(2,1)}, bf16[3,768,384]{2,1,0:T(8,128)(2,1)}, u32[]{:S(2)}, u32[]{:S(2)}) collective-permute-start(bf16[3,768,384]{2,1,0:T(8,128)(2,1)} %w_own.1), channel_id=1, source_target_pairs={{0,1},{1,0},{2,3},{3,2},{4,5},{5,4},{6,7},{7,6},{8,9},{9,8},{10,11... | collective-permute-start | bytes 5308424 | tf_op jit(solution)/shard_map/ppermute | solution.py:763
  1.2 28.6 %collective-permute-start.3 = (bf16[768,1536]{1,0:T(8,128)(2,1)}, bf16[768,1536]{1,0:T(8,128)(2,1)S(1)}, u32[]{:S(2)}, u32[]{:S(2)}) collective-permute-start(bf16[768,1536]{1,0:T(8,128)(2,1)} %wu_own.3), channel_id=1, source_target_pairs={{0,1},{1,0},{2,3},{3,2},{4,5},{5,4},{6,7},{7,6},{8,9},{9,8},{10,11... | collective-permute-start | bytes 7077896 | tf_op jit(solution)/shard_map/ppermute | solution.py:763
  1.3 28.5 %collective-permute-start.5 = (bf16[1536,768]{1,0:T(8,128)(2,1)}, bf16[1536,768]{1,0:T(8,128)(2,1)}, u32[]{:S(2)}, u32[]{:S(2)}) collective-permute-start(bf16[1536,768]{1,0:T(8,128)(2,1)} %wd_own.3), channel_id=1, source_target_pairs={{0,1},{1,0},{2,3},{3,2},{4,5},{5,4},{6,7},{7,6},{8,9},{9,8},{10,11... | collective-permute-start | bytes 7077896 | tf_op jit(solution)/shard_map/ppermute | solution.py:763
  1.7 15.1 %collective-permute-start.1 = (f32[2,384]{1,0:T(2,128)}, f32[2,384]{1,0:T(2,128)S(1)}, u32[]{:S(2)}, u32[]{:S(2)}) collective-permute-start(f32[2,384]{1,0:T(2,128)} %b_ref.1), channel_id=1, source_target_pairs={{0,1},{1,0},{2,3},{3,2},{4,5},{5,4},{6,7},{7,6},{8,9},{9,8},{10,11... | collective-permute-start | bytes 9224 | tf_op jit(solution)/shard_map/ppermute | solution.py:763
  1.8 28.0 %collective-permute-start.2 = (bf16[384,768]{1,0:T(8,128)(2,1)}, bf16[384,768]{1,0:T(8,128)(2,1)S(1)}, u32[]{:S(2)}, u32[]{:S(2)}) collective-permute-start(bf16[384,768]{1,0:T(8,128)(2,1)} %wo_own.3), channel_id=1, source_target_pairs={{0,1},{1,0},{2,3},{3,2},{4,5},{5,4},{6,7},{7,6},{8,9},{9,8},{10,11... | collective-permute-start | bytes 1769480 | tf_op jit(solution)/shard_map/ppermute | solution.py:763
  3.5 12.5 %copy-start = (f32[1536]{0:T(1024)S(1)}, f32[1536]{0:T(1024)}, u32[]{:S(2)}) copy-start(f32[1536]{0:T(1024)} %param.24) | copy-start | bytes 18436
  3.5 12.5 %copy-start.2 = (f32[768]{0:T(1024)S(1)}, f32[768]{0:T(1024)}, u32[]{:S(2)}) copy-start(f32[768]{0:T(1024)} %param.20) | copy-start | bytes 9220
  3.5 12.6 %copy-start.3 = (f32[768]{0:T(1024)S(1)}, f32[768]{0:T(1024)}, u32[]{:S(2)}) copy-start(f32[768]{0:T(1024)} %param.21) | copy-start | bytes 9220
  3.5 12.6 %copy-start.4 = (f32[768]{0:T(1024)S(1)}, f32[768]{0:T(1024)}, u32[]{:S(2)}) copy-start(f32[768]{0:T(1024)} %param.22) | copy-start | bytes 9220
  3.5 12.6 %copy-start.5 = (f32[768]{0:T(1024)S(1)}, f32[768]{0:T(1024)}, u32[]{:S(2)}) copy-start(f32[768]{0:T(1024)} %param.26) | copy-start | bytes 9220
  3.5 12.6 %copy-start.6 = (f32[768]{0:T(1024)S(1)}, f32[768]{0:T(1024)}, u32[]{:S(2)}) copy-start(f32[768]{0:T(1024)} %param.27) | copy-start | bytes 9220
  3.5 12.6 %copy-start.7 = (f32[768]{0:T(1024)S(1)}, f32[768]{0:T(1024)}, u32[]{:S(2)}) copy-start(f32[768]{0:T(1024)} %param.28) | copy-start | bytes 9220
  16.0 13.7 %copy-start.1 = (f32[1,1536]{1,0:T(1,128)}, f32[1,1536]{1,0:T(1,128)S(1)}, u32[]{:S(2)}) copy-start(f32[1,1536]{1,0:T(1,128)S(1)} %reshape.31.bu_own) | copy-start | bytes 18436
  16.8 0.6 copy-start.11
  16.8 12.9 %collective-permute-start.4 = (f32[1,1536]{1,0:T(1,128)S(1)}, f32[1,1536]{1,0:T(1,128)S(1)}, u32[]{:S(2)}, u32[]{:S(2)}) collective-permute-start(f32[1,1536]{1,0:T(1,128)S(1)} %reshape.31.bu_own), channel_id=1, source_target_pairs={{0,1},{1,0},{2,3},{3,2},{4,5},{5,4},{6,7},{7,6},{8,9},{9,8},{10,11... | collective-permute-start | bytes 18440 | tf_op jit(solution)/shard_map/ppermute | solution.py:763
  29.8 0.6 copy-start.10
  29.8 0.8 copy-start.9
  29.8 1.6 copy-start.8

commit v5 on v4

--- a/solution.py
+++ b/solution.py
@@ -196,7 +196,7 @@
     )(c_own, c_peer, x, cot, *fixed_in)
 
 
-LAGS = (1, 4, 7, 9, 12, 15, 17, 19, 22)
+LAGS = (1, 3, 5, 7, 9, 12, 14, 16, 19)
 GROUPS = 12
 BLOCKS = 1
 JOBS = 3 * GROUPS
@@ -221,10 +221,10 @@
     other = (dp, 1 - core)
 
     def partner(level, job):
-        flip = job % 2
-        mask = (1 + flip, 4, 2 - flip, 8)[level]
-        bit = (dp // mask) % 2
-        return bit, (dp + mask * (1 - 2 * bit), core)
+        flip = job & 1
+        shift = (flip, 2, 1 - flip, 3)[level]
+        bit = (dp >> shift) & 1
+        return bit, (dp ^ (1 << shift), core)
 
     def loads():
         return (
@@ -248,16 +248,16 @@
     def start_blocks(index):
         @pl.when(index < 4)
         def _():
-            for copy in block_copies(h_own, h_peer, index, index % 2):
+            for copy in block_copies(h_own, h_peer, index, (index & 1)):
                 copy.start()
 
         @pl.when((index >= 4) & (index < 8))
         def _():
-            for copy in block_copies(gp_own, gp_peer, index - 4, index % 2):
+            for copy in block_copies(gp_own, gp_peer, index - 4, (index & 1)):
                 copy.start()
 
     def weight_copies(index, side):
-        slot = index % 2
+        slot = (index & 1)
         span = pl.ds(pl.multiple_of(index * JC, 128), JC)
         up, down = ((wu_own, wd_own), (wu_peer, wd_peer))[side]
         return (
@@ -272,7 +272,7 @@
 
     def core_copy(job):
         return pltpu.make_async_remote_copy(
-            src_ref=ring.at[job % 9], dst_ref=prec.at[job], send_sem=core_send.at[job], recv_sem=core_recv.at[job],
+            src_ref=ring.at[job - 9 * (job * 57 >> 9)], dst_ref=prec.at[job], send_sem=core_send.at[job], recv_sem=core_recv.at[job],
             device_id=other, device_id_type=pl.DeviceIdType.MESH,
         )
 
@@ -280,7 +280,7 @@
         spots = [0]
         for level in range(levels):
             bit, _ = partner(level, job)
-            spots.append(spots[-1] + bit * (JR >> (level + 1)))
+            spots.append(spots[-1] + (bit << ((JR >> (level + 1)).bit_length() - 1)))
         return spots
 
     def hop(job, stage):
@@ -329,7 +329,7 @@
     def emit_side(group, which, pieces):
         for i, (top, bottom) in enumerate(pieces):
             job = group * 3 + i
-            target = buf.at[job] if which == 0 else ring.at[job % 9]
+            target = buf.at[job] if which == 0 else ring.at[job - 9 * (job * 57 >> 9)]
             cut = top.shape[0]
             target[:cut, :] = top.astype(BF)
             if bottom is not None:
@@ -358,16 +358,16 @@
         def _():
             load(0).wait()
 
-        for copy in block_copies(h_own, h_peer, index, index % 2):
+        for copy in block_copies(h_own, h_peer, index, (index & 1)):
             copy.wait()
         free_ring(index)
         right = glow[...]
-        slot = index % 2
+        slot = (index & 1)
         emit(index, slabs(dot_tn(blocks[slot, 0], right)), slabs(dot_tn(blocks[slot, 1], right)))
         start_blocks(index + 2)
 
     def up_phase(index, side):
-        slot = index % 2
+        slot = (index & 1)
         if side == 0:
             @pl.when(index == 0)
             def _():
@@ -383,7 +383,7 @@
         for row in range(2):
             @pl.when(index // 2 == row)
             def _():
-                lanes = pl.ds(pl.multiple_of((index % 2) * JC, 128), JC)
+                lanes = pl.ds(pl.multiple_of(((index & 1)) * JC, 128), JC)
                 small[8 + 2 * side + row:9 + 2 * side + row, lanes] = total
         emit_side(index + 4, side, tall(dot_tn(mid[...], grad_up)))
         acc[...] = acc[...] + dot_nt(grad_up, wv[side, slot])
@@ -539,7 +539,7 @@
 
     def dx_copy(index):
         span = pl.ds(pl.multiple_of(index * JR, JR), JR)
-        return pltpu.make_async_copy(dxs.at[index % 2], dx_out.at[span], dx_sem.at[index % 2])
+        return pltpu.make_async_copy(dxs.at[(index & 1)], dx_out.at[span], dx_sem.at[(index & 1)])
 
     def dx_phase(index):
         @pl.when(index == 0)
@@ -559,7 +559,7 @@
             for i, grad in enumerate((dq, dk, dv)):
                 part = part + dot_nt(grad[span, cols], wv[side, i])
             total = total + part
-        dxs[index % 2] = total + acc[span, :]
+        dxs[(index & 1)] = total + acc[span, :]
         dx_copy(index).start()
 
     barrier = pltpu.get_barrier_semaphore()
@@ -576,53 +576,63 @@
         load(i).start()
     pl.semaphore_wait(barrier, levels + 1)
 
-    units = seqs * pairs
-
-    def comm(step):
+    norm_at = 4 + 2 * 4
+    first = norm_at + 2 + 1
+    turn = 3 * seqs
+    after = first + turn * (pairs // 2)
+    end = max(JOBS + LAGS[2 * levels], after + 2 * levels + 4)
+
+    def comm(step, low, high):
         for stage in range(2 * levels, -1, -1):
             job = step - LAGS[stage]
-
-            @pl.when((job >= 0) & (job < JOBS))
+            most, least = high - LAGS[stage], low - LAGS[stage]
+            if most < 0 or least >= JOBS:
+                continue
+            if least >= 0 and most < JOBS:
+                stage_op(stage, job)
+            else:
+                @pl.when((job >= 0) & (job < JOBS))
+                def _():
+                    stage_op(stage, job)
+
+    def down_part(t, carry):
+        comm(t, 0, 3)
+        down_phase(t)
+        return carry
+
+    def up_part(i, carry):
+        for side in range(2):
+            comm(4 + 2 * i + side, 4, norm_at - 1)
+            up_phase(i, side)
+        return carry
+
+    def norm_part(i, carry):
+        comm(norm_at + i, norm_at, norm_at + 1)
+        norm_phase(i)
+        return carry
+
+    def head_part(p, carry):
+        def unit_part(u, inner):
+            t = first + turn * p + (u >> 1) * 3 + (u & 1)
+            comm(t, first, after - 1)
+            attend_phase(p * (2 * seqs) + u)
+
+            @pl.when((u & 1) == 1)
             def _():
-                stage_op(stage, job)
-
-    first = 4 + 2 * 4 + 3
-    after = first + 3 * (units // 2)
-    turn = 2 * seqs // 2 * 3
-
-    def tick(t, carry):
-        comm(t)
-
-        @pl.when(t < 4)
-        def _():
-            down_phase(t)
-
-        for side in range(2):
-            @pl.when((t >= 4) & (t < 12) & (t % 2 == side))
-            def _():
-                up_phase((t - 4) // 2, side)
-
-        @pl.when((t >= 12) & (t < 14))
-        def _():
-            norm_phase(t - 12)
-
-        @pl.when(t == 14)
-        def _():
-            out_phase()
-
-        spot = t - first
-
-        @pl.when((spot > 0) & (spot <= after - first) & (spot % turn == 0))
-        def _():
-            proj_phase(spot // turn - 1)
-
-        @pl.when((spot >= 0) & (t < after) & (spot % 3 < 2))
-        def _():
-            attend_phase(spot // 3 * 2 + spot % 3)
-
-        @pl.when((t > after) & (t <= after + rows // JR))
-        def _():
-            dx_phase(t - after - 1)
+                comm(t + 1, first, after - 1)
+
+            return inner
+
+        lax.fori_loop(0, 2 * seqs, unit_part, 0)
+        proj_phase(p)
+        return carry
+
+    def last_part(t, carry):
+        comm(t, after, end - 1)
+
+        @pl.when(t < after + rows // JR)
+        def _():
+            dx_phase(t - after)
 
         for stage in range(levels + 2):
             @pl.when(t == after + 1 + 2 * stage)
@@ -631,7 +641,13 @@
 
         return carry
 
-    lax.fori_loop(0, max(JOBS + LAGS[2 * levels], after + 2 * levels + 4), tick, 0)
+    lax.fori_loop(0, 4, down_part, 0)
+    lax.fori_loop(0, 4, up_part, 0)
+    lax.fori_loop(0, 2, norm_part, 0)
+    comm(jnp.int32(first - 1), first - 1, first - 1)
+    out_phase()
+    lax.fori_loop(0, pairs // 2, head_part, 0)
+    lax.fori_loop(after, end, last_part, 0)
     for group in (GROUPS - 3, GROUPS - 2, GROUPS - 1):
         for i in range(3):
             core_copy(group * 3 + i).wait_send()

time: 231 us -> 224 us (0.970)
  Pallas kernels: 224 us -> 217 us
    pallas_call x1, Pallas kernels: 155 us -> 148 us  [backward(): pl.pallas_call(functools.partial(back_kernel, levels), out_shape=(jax.Sha...]
where the time goes in v5:
time: 224 us
  Pallas kernels  217 us (97%)
  local copies, waits for them, and re-layouts  4.01 us (2%)
    pallas_call x1, Pallas kernels, backward(): pl.pallas_call(functools.partial(back_kernel, levels), out_shape=(jax.Sha...  148 us
    pallas_call x1, Pallas kernels, ffn(): pl.pallas_call(functools.partial(ffn_kernel, chunk), grid=(rows // tile,)...  30.6 us
    pallas_call x2, Pallas kernels, attention(): pl.pallas_call(functools.partial(attn_kernel, qb), out_shape=(out, out, o...  24.8 us
    pallas_call x1, Pallas kernels, unpack(): pl.pallas_call(unpack_kernel, grid=(GROUPS,), out_shape=(jax.ShapeDtypeSt...  13.8 us
  transfers between devices with their start and end apart: 6, of which 0 were waited for; matrix products, arithmetic and copies ran while one was open for 1% of the time, Pallas kernels for 11%

profile of v5, /device:TPU:0, one launch (start us, length us, event | category | flops | bytes accessed | tf_op | source)
XLA Modules:
  0.0 223.8 jit_solution(7680165119495036777)
XLA Ops:
  0.6 0.6 collective-permute-start
  1.2 0.1 collective-permute-start.3
  1.3 0.4 collective-permute-start.5
  1.7 0.1 collective-permute-start.1
  1.8 0.4 collective-permute-start.2
  2.2 1.2 dynamic_slice.3.lens_ref
  3.5 0.0 copy-start
  3.5 0.0 copy-start.2
  3.5 0.0 copy-start.3
  3.5 0.0 copy-start.4
  3.5 0.0 copy-start.5
  3.5 0.0 copy-start.6
  3.5 0.0 copy-start.7
  3.5 12.5 %attend.2 = (bf16[1024,384]{1,0:T(8,128)(2,1)}, bf16[1024,384]{1,0:T(8,128)(2,1)}, bf16[1024,384]{1,0:T(8,128)(2,1)}, bf16[1024,384]{1,0:T(8,128)(2,1)}) custom-call(s32[2]{0:T(128)} %dynamic_slice.3.lens_ref, bf16[1024,768]{1,0:T(8,128)(2,1)} %x_in.1, bf16[3,768,384]{2,1,0:T(8,128)(2,1)} %w_own.1, f32[2,384]{1,0:T(2,128)} %b_ref.1), custom_call_target="tpu_custom_call" | custom-call | flops 7851737088 | bytes 12582912 | tf_op jit(solution)/shard_map/attend/pallas_call | solution.py:74
  16.0 0.0 copy-done
  16.0 0.0 copy-done.2
  16.0 0.0 copy-start.1
  16.0 0.0 copy-done.3
  16.1 0.0 copy-done.4
  16.1 0.0 copy-done.5
  16.1 0.0 copy-done.6
  16.1 0.0 copy-done.7
  16.1 0.7 stack.29.vec_ref.vec_in
  16.8 0.0 collective-permute-done.1.b_ref
  16.8 0.0 copy-start.11
  16.8 0.1 collective-permute-start.4
  16.9 0.0 collective-permute-done.w_ref.w_peer
  16.9 0.5 copy-done.11
  17.4 12.4 %attend.3 = (bf16[1024,384]{1,0:T(8,128)(2,1)}, bf16[1024,384]{1,0:T(8,128)(2,1)}, bf16[1024,384]{1,0:T(8,128)(2,1)}, bf16[1024,384]{1,0:T(8,128)(2,1)}) custom-call(s32[2]{0:T(128)} %dynamic_slice.3.lens_ref, bf16[1024,768]{1,0:T(8,128)(2,1)} %x_in.1, bf16[3,768,384]{2,1,0:T(8,128)(2,1)} %collective-permute-done.w_ref.w_peer, f32[2,384]{1,0:T(2,128)} %copy-done.11), custom_call_target="tpu_custom_call" | custom-call | flops 7851737088 | bytes 12582912 | tf_op jit(solution)/shard_map/attend/pallas_call | solution.py:74
  29.7 0.0 copy-done.1
  29.7 0.0 collective-permute-done.4.bu_peer
  29.8 0.0 copy-start.10
  29.8 0.0 collective-permute-done.2.wo_peer
  29.8 0.0 copy-start.9
  29.8 0.0 collective-permute-done.3.wu_peer
  29.8 0.0 copy-start.8
  29.8 0.0 collective-permute-done.5.wd_peer
  29.8 0.5 copy-done.10
  30.3 0.3 copy-done.9
  30.6 0.7 copy-done.8
  31.4 30.6 %feed.1 = (f32[1024,768]{1,0:T(8,128)}, bf16[1024,1536]{1,0:T(8,128)(2,1)}, bf16[1024,1536]{1,0:T(8,128)(2,1)}, bf16[1024,1536]{1,0:T(8,128)(2,1)}, bf16[1024,15...) custom-call(bf16[1024,384]{1,0:T(8,128)(2,1)} %get-tuple-element.48., ...), custom_call_target="tpu_custom_call" | custom-call | flops 12079595520 | bytes 50331648 | tf_op jit(solution)/shard_map/feed/pallas_call | solution.py:179
  61.9 147.9 %backward.1 = (bf16[36,256,384]{2,1,0:T(8,128)(2,1)}, f32[1024,768]{1,0:T(8,128)}, f32[16,768]{1,0:T(8,128)}) custom-call(s32[2]{0:T(128)} %dynamic_slice.3.lens_ref, bf16[1024,1536]{1,0:T(8,128)(2,1)} %get-tuple-element.51.h_own, bf16[1024,1536]{1,0:T(8,128)(2,1)} %get-tuple-element.52.h_peer, bf16[1024,1536]{1,0:T(8,128)(2,1)} %get-tuple-element.53.gp_own, ...), custom_call_target="tpu_custom_call" | custom-call | flops 64424509440 | bytes 67108864 | tf_op jit(solution)/shard_map/backward/pallas_call | solution.py:672
  209.8 13.8 %unpack.1 = (f32[1024,768]{1,0:T(8,128)}, f32[3,768,384]{2,1,0:T(8,128)}, f32[2,384]{1,0:T(2,128)}, f32[384,768]{1,0:T(8,128)}, f32[768,1536]{1,0:T(8,128)}, /*i...) custom-call(bf16[36,256,384]{2,1,0:T(8,128)(2,1)} %get-tuple-element, ...), custom_call_target="tpu_custom_call" | custom-call | tf_op jit(solution)/shard_map/unpack/pallas_call | solution.py:752
  (7 shorter events, 0.0 us)
Async XLA Ops:
  0.6 16.3 %collective-permute-start = (bf16[3,768,384]{2,1,0:T(8,128)(2,1)}, bf16[3,768,384]{2,1,0:T(8,128)(2,1)}, u32[]{:S(2)}, u32[]{:S(2)}) collective-permute-start(bf16[3,768,384]{2,1,0:T(8,128)(2,1)} %w_own.1), channel_id=1, source_target_pairs={{0,1},{1,0},{2,3},{3,2},{4,5},{5,4},{6,7},{7,6},{8,9},{9,8},{10,11... | collective-permute-start | bytes 5308424 | tf_op jit(solution)/shard_map/ppermute | solution.py:779
  1.2 28.6 %collective-permute-start.3 = (bf16[768,1536]{1,0:T(8,128)(2,1)}, bf16[768,1536]{1,0:T(8,128)(2,1)S(1)}, u32[]{:S(2)}, u32[]{:S(2)}) collective-permute-start(bf16[768,1536]{1,0:T(8,128)(2,1)} %wu_own.3), channel_id=1, source_target_pairs={{0,1},{1,0},{2,3},{3,2},{4,5},{5,4},{6,7},{7,6},{8,9},{9,8},{10,11... | collective-permute-start | bytes 7077896 | tf_op jit(solution)/shard_map/ppermute | solution.py:779
  1.3 28.5 %collective-permute-start.5 = (bf16[1536,768]{1,0:T(8,128)(2,1)}, bf16[1536,768]{1,0:T(8,128)(2,1)}, u32[]{:S(2)}, u32[]{:S(2)}) collective-permute-start(bf16[1536,768]{1,0:T(8,128)(2,1)} %wd_own.3), channel_id=1, source_target_pairs={{0,1},{1,0},{2,3},{3,2},{4,5},{5,4},{6,7},{7,6},{8,9},{9,8},{10,11... | collective-permute-start | bytes 7077896 | tf_op jit(solution)/shard_map/ppermute | solution.py:779
  1.7 15.1 %collective-permute-start.1 = (f32[2,384]{1,0:T(2,128)}, f32[2,384]{1,0:T(2,128)S(1)}, u32[]{:S(2)}, u32[]{:S(2)}) collective-permute-start(f32[2,384]{1,0:T(2,128)} %b_ref.1), channel_id=1, source_target_pairs={{0,1},{1,0},{2,3},{3,2},{4,5},{5,4},{6,7},{7,6},{8,9},{9,8},{10,11... | collective-permute-start | bytes 9224 | tf_op jit(solution)/shard_map/ppermute | solution.py:779
  1.8 28.0 %collective-permute-start.2 = (bf16[384,768]{1,0:T(8,128)(2,1)}, bf16[384,768]{1,0:T(8,128)(2,1)S(1)}, u32[]{:S(2)}, u32[]{:S(2)}) collective-permute-start(bf16[384,768]{1,0:T(8,128)(2,1)} %wo_own.3), channel_id=1, source_target_pairs={{0,1},{1,0},{2,3},{3,2},{4,5},{5,4},{6,7},{7,6},{8,9},{9,8},{10,11... | collective-permute-start | bytes 1769480 | tf_op jit(solution)/shard_map/ppermute | solution.py:779
  3.5 12.5 %copy-start = (f32[1536]{0:T(1024)S(1)}, f32[1536]{0:T(1024)}, u32[]{:S(2)}) copy-start(f32[1536]{0:T(1024)} %param.24) | copy-start | bytes 18436
  3.5 12.5 %copy-start.2 = (f32[768]{0:T(1024)S(1)}, f32[768]{0:T(1024)}, u32[]{:S(2)}) copy-start(f32[768]{0:T(1024)} %param.20) | copy-start | bytes 9220
  3.5 12.6 %copy-start.3 = (f32[768]{0:T(1024)S(1)}, f32[768]{0:T(1024)}, u32[]{:S(2)}) copy-start(f32[768]{0:T(1024)} %param.21) | copy-start | bytes 9220
  3.5 12.6 %copy-start.4 = (f32[768]{0:T(1024)S(1)}, f32[768]{0:T(1024)}, u32[]{:S(2)}) copy-start(f32[768]{0:T(1024)} %param.22) | copy-start | bytes 9220
  3.5 12.6 %copy-start.5 = (f32[768]{0:T(1024)S(1)}, f32[768]{0:T(1024)}, u32[]{:S(2)}) copy-start(f32[768]{0:T(1024)} %param.26) | copy-start | bytes 9220
  3.5 12.6 %copy-start.6 = (f32[768]{0:T(1024)S(1)}, f32[768]{0:T(1024)}, u32[]{:S(2)}) copy-start(f32[768]{0:T(1024)} %param.27) | copy-start | bytes 9220
  3.5 12.6 %copy-start.7 = (f32[768]{0:T(1024)S(1)}, f32[768]{0:T(1024)}, u32[]{:S(2)}) copy-start(f32[768]{0:T(1024)} %param.28) | copy-start | bytes 9220
  16.0 13.7 %copy-start.1 = (f32[1,1536]{1,0:T(1,128)}, f32[1,1536]{1,0:T(1,128)S(1)}, u32[]{:S(2)}) copy-start(f32[1,1536]{1,0:T(1,128)S(1)} %reshape.31.bu_own) | copy-start | bytes 18436
  16.8 0.6 copy-start.11
  16.8 12.9 %collective-permute-start.4 = (f32[1,1536]{1,0:T(1,128)S(1)}, f32[1,1536]{1,0:T(1,128)S(1)}, u32[]{:S(2)}, u32[]{:S(2)}) collective-permute-start(f32[1,1536]{1,0:T(1,128)S(1)} %reshape.31.bu_own), channel_id=1, source_target_pairs={{0,1},{1,0},{2,3},{3,2},{4,5},{5,4},{6,7},{7,6},{8,9},{9,8},{10,11... | collective-permute-start | bytes 18440 | tf_op jit(solution)/shard_map/ppermute | solution.py:779
  29.8 0.6 copy-start.10
  29.8 0.8 copy-start.9
  29.8 1.6 copy-start.8

commit v6 on v5

--- a/solution.py
+++ b/solution.py
@@ -40,6 +40,7 @@
     q_ref[...] = (dot(x, w_ref[0]) + b_ref[0:1, :]).astype(BF) * jnp.asarray(scale, BF)
     k_ref[...] = dot(x, w_ref[1]).astype(BF)
     v_ref[...] = (dot(x, w_ref[2]) + b_ref[1:2, :]).astype(BF)
+    hide = jnp.where(lax.broadcasted_iota(jnp.int32, (rows, 1), 0) < length, 0.0, NEG)
     for pair in range(width // 128):
         lanes = slice(pair * 128, pair * 128 + 128)
         k = k_ref[:, lanes]
@@ -53,8 +54,7 @@
             for head in range(2):
                 q_head = jnp.where(low, q, zero) if head == 0 else jnp.where(low, zero, q)
                 s = dot_nt(k, q_head)
-                is_valid = lax.broadcasted_iota(jnp.int32, s.shape, 0) < length
-                s = jnp.where(is_valid, s, NEG)
+                s = s + hide
                 top = jnp.max(s, axis=0, keepdims=True)
                 e = jnp.exp(s - top)
                 total = jnp.sum(e, axis=0, keepdims=True)
@@ -118,10 +118,25 @@
 
 def ffn_kernel(
     chunk,
-    c_own, c_peer, x_ref, cot_ref, wo_own, wo_peer, wu_own, wu_peer, bu_own, bu_peer, wd_own, wd_peer, vec_ref,
+    c_own, c_peer, x_ref, cot_ref, wo_own_in, wo_peer_in, wu_own_in, wu_peer_in, bu_own, bu_peer, wd_own_in, wd_peer_in, vec_ref,
     out_ref, h_own, h_peer, gp_own, gp_peer, mid_ref, glow_ref, gs_ref, fin_ref, small_ref,
+    wo_own, wo_peer, wu_own, wu_peer, wd_own, wd_peer, sem,
 ):
     step = pl.program_id(0)
+    pieces = ((wo_own_in, wo_own), (wo_peer_in, wo_peer), (wu_own_in, wu_own), (wd_own_in, wd_own), (wu_peer_in, wu_peer), (wd_peer_in, wd_peer))
+    copies = [pltpu.make_async_copy(src, dst, sem.at[i]) for i, (src, dst) in enumerate(pieces)]
+
+    @pl.when(step == 0)
+    def _():
+        for copy in copies:
+            copy.start()
+
+    def arrived(group):
+        @pl.when(step == 0)
+        def _():
+            for copy in copies[2 * group:2 * group + 2]:
+                copy.wait()
+
     wide = wu_own.shape[1]
     out_bias, gain1, shift1, down_bias, gain2, shift2 = (vec_ref[i:i + 1, :] for i in range(6))
 
@@ -132,6 +147,7 @@
     def colsum(index, value):
         small_ref[index:index + 1, :] += jnp.sum(value, axis=0, keepdims=True)
 
+    arrived(0)
     attn_sum = dot(c_own[...], wo_own[...]) + dot(c_peer[...], wo_peer[...])
     first_in = x_ref[...].astype(F32) + attn_sum + out_bias
     fin_ref[...] = first_in
@@ -140,7 +156,8 @@
     middle = first_out.astype(BF)
     mid_ref[...] = middle
     ffn_sum = jnp.zeros_like(first_out)
-    for wu, bu, wd, h_ref, gp_ref in ((wu_own, bu_own, wd_own, h_own, gp_own), (wu_peer, bu_peer, wd_peer, h_peer, gp_peer)):
+    for group, (wu, bu, wd, h_ref, gp_ref) in enumerate(((wu_own, bu_own, wd_own, h_own, gp_own), (wu_peer, bu_peer, wd_peer, h_peer, gp_peer))):
+        arrived(group + 1)
         for at in range(0, wide, chunk):
             cols = slice(at, at + chunk)
             u = dot(middle, wu[:, cols]) + bu[:, cols]
@@ -175,6 +192,7 @@
     def sds(cols, dtype):
         return jax.ShapeDtypeStruct((rows, cols), dtype)
 
+    hbm = pl.BlockSpec(memory_space=pl.ANY)
     fixed_in = (wo_own, wo_peer, wu_own, wu_peer, bu_own, bu_peer, wd_own, wd_peer, vecs)
     return pl.pallas_call(
         functools.partial(ffn_kernel, chunk),
@@ -184,12 +202,13 @@
             sds(depth, BF), sds(depth, BF), sds(depth, F32), sds(depth, F32),
             jax.ShapeDtypeStruct((16, depth), F32),
         ),
-        in_specs=[tiled(half), tiled(half), tiled(depth), tiled(depth)] + [fixed(a.shape) for a in fixed_in],
+        in_specs=[tiled(half), tiled(half), tiled(depth), tiled(depth)] + [hbm if a.dtype == BF else fixed(a.shape) for a in fixed_in],
         out_specs=[
             tiled(depth), tiled(wide), tiled(wide), tiled(wide), tiled(wide),
             tiled(depth), tiled(depth), tiled(depth), tiled(depth),
             pl.BlockSpec((16, depth), lambda i: (0, 0)),
         ],
+        scratch_shapes=[pltpu.VMEM(a.shape, BF) for a in (wo_own, wo_peer, wu_own, wu_peer, wd_own, wd_peer)] + [pltpu.SemaphoreType.DMA((6,))],
         compiler_params=pltpu.CompilerParams(vmem_limit_bytes=60 << 20),
         cost_estimate=pl.CostEstimate(flops=rows * depth * (4 * 2 * wide + 4 * depth), bytes_accessed=48 << 20, transcendentals=rows * wide * 2),
         name="feed",
@@ -385,24 +404,27 @@
             def _():
                 lanes = pl.ds(pl.multiple_of(((index & 1)) * JC, 128), JC)
                 small[8 + 2 * side + row:9 + 2 * side + row, lanes] = total
+        blocks[slot, side] = grad_up
         emit_side(index + 4, side, tall(dot_tn(mid[...], grad_up)))
-        acc[...] = acc[...] + dot_nt(grad_up, wv[side, slot])
-        if side == 1:
-            start_blocks(index + 6)
-
-            @pl.when(index < 2)
-            def _():
-                start_weights(index + 2)
-
-            @pl.when(index == 2)
-            def _():
-                load(17).start()
-                load(18).start()
-
-            @pl.when(index == 3)
-            def _():
-                for i in (12, 13, 14):
-                    load(i).start()
+
+    def first_phase(index):
+        slot = index & 1
+        acc[...] = acc[...] + (dot_nt(blocks[slot, 0], wv[0, slot]) + dot_nt(blocks[slot, 1], wv[1, slot]))
+        start_blocks(index + 6)
+
+        @pl.when(index < 2)
+        def _():
+            start_weights(index + 2)
+
+        @pl.when(index == 2)
+        def _():
+            load(17).start()
+            load(18).start()
+
+        @pl.when(index == 3)
+        def _():
+            for i in (12, 13, 14):
+                load(i).start()
 
     def norm_phase(index):
         @pl.when(index == 0)
@@ -493,6 +515,7 @@
         k = kv[span, lanes]
         v = vv[span, lanes]
         k_t = k.T
+        hide = jnp.where(lax.broadcasted_iota(jnp.int32, (seq_len, 1), 0) < length, 0.0, NEG)
         low = half_masks((1, 128), 1)
         qb = seq_len // BLOCKS
         grad_k = jnp.zeros((seq_len, 128), F32)
@@ -507,8 +530,7 @@
                 q_head = jnp.where(pick, q, jnp.zeros_like(q))
                 do_head = jnp.where(pick, do, jnp.zeros_like(do))
                 s = dot_nt(k, q_head)
-                is_valid = lax.broadcasted_iota(jnp.int32, s.shape, 0) < length
-                s = jnp.where(is_valid, s, NEG)
+                s = s + hide
                 e = jnp.exp(s - jnp.max(s, axis=0, keepdims=True))
                 weights = e * (1.0 / jnp.sum(e, axis=0, keepdims=True))
                 grad_probs = dot_nt(v, do_head)
@@ -576,22 +598,29 @@
         load(i).start()
     pl.semaphore_wait(barrier, levels + 1)
 
-    norm_at = 4 + 2 * 4
+    norm_at = 4 + 3 * 4
     first = norm_at + 2 + 1
     turn = 3 * seqs
     after = first + turn * (pairs // 2)
-    end = max(JOBS + LAGS[2 * levels], after + 2 * levels + 4)
+    early = JOBS - 3
+    gap = max(after - 1 - early, 0)
+    end = max(JOBS + gap + LAGS[2 * levels], after + 2 * levels + 4)
 
     def comm(step, low, high):
         for stage in range(2 * levels, -1, -1):
-            job = step - LAGS[stage]
+            slot = step - LAGS[stage]
             most, least = high - LAGS[stage], low - LAGS[stage]
-            if most < 0 or least >= JOBS:
+            if most < 0:
                 continue
-            if least >= 0 and most < JOBS:
+            if most < early:
+                job, here = slot, slot >= 0
+            else:
+                job = slot - jnp.where(slot >= early, gap, 0)
+                here = (slot >= 0) & ((slot < early) | (job >= early)) & (job < JOBS)
+            if least >= 0 and most < early:
                 stage_op(stage, job)
             else:
-                @pl.when((job >= 0) & (job < JOBS))
+                @pl.when(here)
                 def _():
                     stage_op(stage, job)
 
@@ -602,8 +631,10 @@
 
     def up_part(i, carry):
         for side in range(2):
-            comm(4 + 2 * i + side, 4, norm_at - 1)
+            comm(4 + 3 * i + side, 4, norm_at - 1)
             up_phase(i, side)
+        comm(6 + 3 * i, 4, norm_at - 1)
+        first_phase(i)
         return carry
 
     def norm_part(i, carry):

time: 224 us -> 222 us (level)
    pallas_call x1, Pallas kernels: 148 us -> 146 us  [backward(): pl.pallas_call(functools.partial(back_kernel, levels), out_shape=(jax.Sha...]
where the time goes in v6:
time: 222 us
  Pallas kernels  215 us (97%)
  local copies, waits for them, and re-layouts  4.01 us (2%)
    pallas_call x1, Pallas kernels, backward(): pl.pallas_call(functools.partial(back_kernel, levels), out_shape=(jax.Sha...  146 us
    pallas_call x1, Pallas kernels, ffn(): pl.pallas_call(functools.partial(ffn_kernel, chunk), grid=(rows // tile,)...  31 us
    pallas_call x2, Pallas kernels, attention(): pl.pallas_call(functools.partial(attn_kernel, qb), out_shape=(out, out, o...  24.5 us
    pallas_call x1, Pallas kernels, unpack(): pl.pallas_call(unpack_kernel, grid=(GROUPS,), out_shape=(jax.ShapeDtypeSt...  13.8 us
  transfers between devices with their start and end apart: 6, of which 0 were waited for; matrix products, arithmetic and copies ran while one was open for 1% of the time, Pallas kernels for 11%

profile of v6, /device:TPU:0, one launch (start us, length us, event | category | flops | bytes accessed | tf_op | source)
XLA Modules:
  0.0 221.7 jit_solution(260717478818137584)
XLA Ops:
  0.6 0.6 collective-permute-start
  1.2 0.1 collective-permute-start.3
  1.3 0.4 collective-permute-start.5
  1.7 0.1 collective-permute-start.1
  1.8 0.4 collective-permute-start.2
  2.2 1.2 dynamic_slice.3.lens_ref
  3.5 0.0 copy-start
  3.5 0.0 copy-start.2
  3.5 0.0 copy-start.3
  3.5 0.0 copy-start.4
  3.5 0.0 copy-start.5
  3.5 0.0 copy-start.6
  3.5 0.0 copy-start.7
  3.5 12.3 %attend.2 = (bf16[1024,384]{1,0:T(8,128)(2,1)}, bf16[1024,384]{1,0:T(8,128)(2,1)}, bf16[1024,384]{1,0:T(8,128)(2,1)}, bf16[1024,384]{1,0:T(8,128)(2,1)}) custom-call(s32[2]{0:T(128)} %dynamic_slice.3.lens_ref, bf16[1024,768]{1,0:T(8,128)(2,1)} %x_in.1, bf16[3,768,384]{2,1,0:T(8,128)(2,1)} %w_own.1, f32[2,384]{1,0:T(2,128)} %b_ref.1), custom_call_target="tpu_custom_call" | custom-call | flops 7851737088 | bytes 12582912 | tf_op jit(solution)/shard_map/attend/pallas_call | solution.py:74
  15.8 0.0 copy-done
  15.9 0.0 copy-done.2
  15.9 0.0 copy-start.1
  15.9 0.0 copy-done.3
  15.9 0.0 copy-done.4
  15.9 0.0 copy-done.5
  16.0 0.0 copy-done.6
  16.0 0.0 copy-done.7
  16.0 0.7 stack.29.vec_ref.vec_in
  16.7 0.0 collective-permute-done.1.b_ref
  16.7 0.0 copy-start.11
  16.7 0.1 collective-permute-start.4
  16.7 0.0 collective-permute-done.w_ref.w_peer
  16.8 0.5 copy-done.11
  17.2 12.2 %attend.3 = (bf16[1024,384]{1,0:T(8,128)(2,1)}, bf16[1024,384]{1,0:T(8,128)(2,1)}, bf16[1024,384]{1,0:T(8,128)(2,1)}, bf16[1024,384]{1,0:T(8,128)(2,1)}) custom-call(s32[2]{0:T(128)} %dynamic_slice.3.lens_ref, bf16[1024,768]{1,0:T(8,128)(2,1)} %x_in.1, bf16[3,768,384]{2,1,0:T(8,128)(2,1)} %collective-permute-done.w_ref.w_peer, f32[2,384]{1,0:T(2,128)} %copy-done.11), custom_call_target="tpu_custom_call" | custom-call | flops 7851737088 | bytes 12582912 | tf_op jit(solution)/shard_map/attend/pallas_call | solution.py:74
  29.5 0.0 copy-done.1
  29.5 0.0 collective-permute-done.4.bu_peer
  29.5 0.0 copy-start.10
  29.5 0.0 collective-permute-done.2.wo_peer_in.wo_peer
  29.5 0.0 copy-start.9
  29.5 0.0 collective-permute-done.3.wu_peer_in.wu_peer
  29.5 0.0 copy-start.8
  29.5 0.0 collective-permute-done.5.wd_peer_in.wd_peer
  29.5 0.5 copy-done.10
  30.0 0.3 copy-done.9
  30.3 0.7 copy-done.8
  31.1 31.0 %feed.1 = (f32[1024,768]{1,0:T(8,128)}, bf16[1024,1536]{1,0:T(8,128)(2,1)}, bf16[1024,1536]{1,0:T(8,128)(2,1)}, bf16[1024,1536]{1,0:T(8,128)(2,1)}, bf16[1024,15...) custom-call(bf16[1024,384]{1,0:T(8,128)(2,1)} %get-tuple-element.48., ...), custom_call_target="tpu_custom_call" | custom-call | flops 12079595520 | bytes 50331648 | tf_op jit(solution)/shard_map/feed/pallas_call | solution.py:197
  62.1 145.6 %backward.1 = (bf16[36,256,384]{2,1,0:T(8,128)(2,1)}, f32[1024,768]{1,0:T(8,128)}, f32[16,768]{1,0:T(8,128)}) custom-call(s32[2]{0:T(128)} %dynamic_slice.3.lens_ref, bf16[1024,1536]{1,0:T(8,128)(2,1)} %get-tuple-element.51.h_own, bf16[1024,1536]{1,0:T(8,128)(2,1)} %get-tuple-element.52.h_peer, bf16[1024,1536]{1,0:T(8,128)(2,1)} %get-tuple-element.53.gp_own, ...), custom_call_target="tpu_custom_call" | custom-call | flops 64424509440 | bytes 67108864 | tf_op jit(solution)/shard_map/backward/pallas_call | solution.py:703
  207.7 13.8 %unpack.1 = (f32[1024,768]{1,0:T(8,128)}, f32[3,768,384]{2,1,0:T(8,128)}, f32[2,384]{1,0:T(2,128)}, f32[384,768]{1,0:T(8,128)}, f32[768,1536]{1,0:T(8,128)}, /*i...) custom-call(bf16[36,256,384]{2,1,0:T(8,128)(2,1)} %get-tuple-element, ...), custom_call_target="tpu_custom_call" | custom-call | tf_op jit(solution)/shard_map/unpack/pallas_call | solution.py:783
  (7 shorter events, 0.0 us)
Async XLA Ops:
  0.6 16.1 %collective-permute-start = (bf16[3,768,384]{2,1,0:T(8,128)(2,1)}, bf16[3,768,384]{2,1,0:T(8,128)(2,1)}, u32[]{:S(2)}, u32[]{:S(2)}) collective-permute-start(bf16[3,768,384]{2,1,0:T(8,128)(2,1)} %w_own.1), channel_id=1, source_target_pairs={{0,1},{1,0},{2,3},{3,2},{4,5},{5,4},{6,7},{7,6},{8,9},{9,8},{10,11... | collective-permute-start | bytes 5308424 | tf_op jit(solution)/shard_map/ppermute | solution.py:810
  1.2 28.3 %collective-permute-start.3 = (bf16[768,1536]{1,0:T(8,128)(2,1)}, bf16[768,1536]{1,0:T(8,128)(2,1)S(1)}, u32[]{:S(2)}, u32[]{:S(2)}) collective-permute-start(bf16[768,1536]{1,0:T(8,128)(2,1)} %wu_own.1), channel_id=1, source_target_pairs={{0,1},{1,0},{2,3},{3,2},{4,5},{5,4},{6,7},{7,6},{8,9},{9,8},{10,11... | collective-permute-start | bytes 7077896 | tf_op jit(solution)/shard_map/ppermute | solution.py:810
  1.3 28.2 %collective-permute-start.5 = (bf16[1536,768]{1,0:T(8,128)(2,1)}, bf16[1536,768]{1,0:T(8,128)(2,1)}, u32[]{:S(2)}, u32[]{:S(2)}) collective-permute-start(bf16[1536,768]{1,0:T(8,128)(2,1)} %wd_own.1), channel_id=1, source_target_pairs={{0,1},{1,0},{2,3},{3,2},{4,5},{5,4},{6,7},{7,6},{8,9},{9,8},{10,11... | collective-permute-start | bytes 7077896 | tf_op jit(solution)/shard_map/ppermute | solution.py:810
  1.7 15.0 %collective-permute-start.1 = (f32[2,384]{1,0:T(2,128)}, f32[2,384]{1,0:T(2,128)S(1)}, u32[]{:S(2)}, u32[]{:S(2)}) collective-permute-start(f32[2,384]{1,0:T(2,128)} %b_ref.1), channel_id=1, source_target_pairs={{0,1},{1,0},{2,3},{3,2},{4,5},{5,4},{6,7},{7,6},{8,9},{9,8},{10,11... | collective-permute-start | bytes 9224 | tf_op jit(solution)/shard_map/ppermute | solution.py:810
  1.8 27.7 %collective-permute-start.2 = (bf16[384,768]{1,0:T(8,128)(2,1)}, bf16[384,768]{1,0:T(8,128)(2,1)S(1)}, u32[]{:S(2)}, u32[]{:S(2)}) collective-permute-start(bf16[384,768]{1,0:T(8,128)(2,1)} %wo_own.1), channel_id=1, source_target_pairs={{0,1},{1,0},{2,3},{3,2},{4,5},{5,4},{6,7},{7,6},{8,9},{9,8},{10,11... | collective-permute-start | bytes 1769480 | tf_op jit(solution)/shard_map/ppermute | solution.py:810
  3.5 12.4 %copy-start = (f32[1536]{0:T(1024)S(1)}, f32[1536]{0:T(1024)}, u32[]{:S(2)}) copy-start(f32[1536]{0:T(1024)} %param.24) | copy-start | bytes 18436
  3.5 12.4 %copy-start.2 = (f32[768]{0:T(1024)S(1)}, f32[768]{0:T(1024)}, u32[]{:S(2)}) copy-start(f32[768]{0:T(1024)} %param.20) | copy-start | bytes 9220
  3.5 12.4 %copy-start.3 = (f32[768]{0:T(1024)S(1)}, f32[768]{0:T(1024)}, u32[]{:S(2)}) copy-start(f32[768]{0:T(1024)} %param.21) | copy-start | bytes 9220
  3.5 12.4 %copy-start.4 = (f32[768]{0:T(1024)S(1)}, f32[768]{0:T(1024)}, u32[]{:S(2)}) copy-start(f32[768]{0:T(1024)} %param.22) | copy-start | bytes 9220
  3.5 12.5 %copy-start.5 = (f32[768]{0:T(1024)S(1)}, f32[768]{0:T(1024)}, u32[]{:S(2)}) copy-start(f32[768]{0:T(1024)} %param.26) | copy-start | bytes 9220
  3.5 12.5 %copy-start.6 = (f32[768]{0:T(1024)S(1)}, f32[768]{0:T(1024)}, u32[]{:S(2)}) copy-start(f32[768]{0:T(1024)} %param.27) | copy-start | bytes 9220
  3.5 12.5 %copy-start.7 = (f32[768]{0:T(1024)S(1)}, f32[768]{0:T(1024)}, u32[]{:S(2)}) copy-start(f32[768]{0:T(1024)} %param.28) | copy-start | bytes 9220
  15.9 13.6 %copy-start.1 = (f32[1,1536]{1,0:T(1,128)}, f32[1,1536]{1,0:T(1,128)S(1)}, u32[]{:S(2)}) copy-start(f32[1,1536]{1,0:T(1,128)S(1)} %reshape.31.bu_own) | copy-start | bytes 18436
  16.7 0.6 copy-start.11
  16.7 12.8 %collective-permute-start.4 = (f32[1,1536]{1,0:T(1,128)S(1)}, f32[1,1536]{1,0:T(1,128)S(1)}, u32[]{:S(2)}, u32[]{:S(2)}) collective-permute-start(f32[1,1536]{1,0:T(1,128)S(1)} %reshape.31.bu_own), channel_id=1, source_target_pairs={{0,1},{1,0},{2,3},{3,2},{4,5},{5,4},{6,7},{7,6},{8,9},{9,8},{10,11... | collective-permute-start | bytes 18440 | tf_op jit(solution)/shard_map/ppermute | solution.py:810
  29.5 0.6 copy-start.10
  29.5 0.8 copy-start.9
  29.5 1.6 copy-start.8

commit v7 on v6

--- a/solution.py
+++ b/solution.py
@@ -331,7 +331,6 @@
             return
         before = hop(job, stage - 1)
         before.wait_recv()
-        before.wait_send()
         if stage <= levels:
             level = stage - 1
             size = JR >> stage
@@ -344,6 +343,7 @@
             hop(job, stage).start()
         else:
             pltpu.make_async_copy(prec.at[job], job_out.at[job], out_sem.at[job]).start()
+        before.wait_send()
 
     def emit_side(group, which, pieces):
         for i, (top, bottom) in enumerate(pieces):
@@ -357,8 +357,8 @@
                 core_copy(job).start()
 
     def emit(group, own, peer):
+        emit_side(group, 1, peer)
         emit_side(group, 0, own)
-        emit_side(group, 1, peer)
 
     def free_ring(group):
         @pl.when(group >= 3)
@@ -554,7 +554,7 @@
 
         free_ring(index + 9)
         left = mid[...]
-        for side in range(2):
+        for side in (1, 0):
             lanes = pl.ds(pl.multiple_of(side * half + index * 128, 128), 128)
             right = jnp.concatenate([dq[:, lanes], dk[:, lanes], dv[:, lanes]], axis=1)
             emit_side(index + 9, side, tall(dot_tn(left, right)))

time: 222 us -> 223 us (level)
  no operation moved by 1% of the time
where the time goes in v7:
time: 223 us; the launch traced here: 222 us
  Pallas kernels  215 us (96%)
  local copies, waits for them, and re-layouts  4.01 us (2%)
    pallas_call x1, Pallas kernels, backward(): pl.pallas_call(functools.partial(back_kernel, levels), out_shape=(jax.Sha...  146 us
    pallas_call x1, Pallas kernels, ffn(): pl.pallas_call(functools.partial(ffn_kernel, chunk), grid=(rows // tile,)...  31 us
    pallas_call x2, Pallas kernels, attention(): pl.pallas_call(functools.partial(attn_kernel, qb), out_shape=(out, out, o...  24.5 us
    pallas_call x1, Pallas kernels, unpack(): pl.pallas_call(unpack_kernel, grid=(GROUPS,), out_shape=(jax.ShapeDtypeSt...  13.8 us
  transfers between devices with their start and end apart: 6, of which 0 were waited for; matrix products, arithmetic and copies ran while one was open for 1% of the time, Pallas kernels for 11%

profile of v7, /device:TPU:0, one launch (start us, length us, event | category | flops | bytes accessed | tf_op | source)
XLA Modules:
  0.0 222.2 jit_solution(57020801313949361)
XLA Ops:
  0.6 0.6 collective-permute-start
  1.2 0.1 collective-permute-start.3
  1.3 0.4 collective-permute-start.5
  1.7 0.1 collective-permute-start.1
  1.8 0.4 collective-permute-start.2
  2.2 1.2 dynamic_slice.3.lens_ref
  3.5 0.0 copy-start
  3.5 0.0 copy-start.2
  3.5 0.0 copy-start.3
  3.5 0.0 copy-start.4
  3.5 0.0 copy-start.5
  3.5 0.0 copy-start.6
  3.5 0.0 copy-start.7
  3.5 12.3 %attend.2 = (bf16[1024,384]{1,0:T(8,128)(2,1)}, bf16[1024,384]{1,0:T(8,128)(2,1)}, bf16[1024,384]{1,0:T(8,128)(2,1)}, bf16[1024,384]{1,0:T(8,128)(2,1)}) custom-call(s32[2]{0:T(128)} %dynamic_slice.3.lens_ref, bf16[1024,768]{1,0:T(8,128)(2,1)} %x_in.1, bf16[3,768,384]{2,1,0:T(8,128)(2,1)} %w_own.1, f32[2,384]{1,0:T(2,128)} %b_ref.1), custom_call_target="tpu_custom_call" | custom-call | flops 7851737088 | bytes 12582912 | tf_op jit(solution)/shard_map/attend/pallas_call | solution.py:74
  15.8 0.0 copy-done
  15.9 0.0 copy-done.2
  15.9 0.0 copy-start.1
  15.9 0.0 copy-done.3
  15.9 0.0 copy-done.4
  15.9 0.0 copy-done.5
  16.0 0.0 copy-done.6
  16.0 0.0 copy-done.7
  16.0 0.7 stack.29.vec_ref.vec_in
  16.7 0.0 collective-permute-done.1.b_ref
  16.7 0.0 copy-start.11
  16.7 0.1 collective-permute-start.4
  16.7 0.0 collective-permute-done.w_ref.w_peer
  16.8 0.5 copy-done.11
  17.2 12.2 %attend.3 = (bf16[1024,384]{1,0:T(8,128)(2,1)}, bf16[1024,384]{1,0:T(8,128)(2,1)}, bf16[1024,384]{1,0:T(8,128)(2,1)}, bf16[1024,384]{1,0:T(8,128)(2,1)}) custom-call(s32[2]{0:T(128)} %dynamic_slice.3.lens_ref, bf16[1024,768]{1,0:T(8,128)(2,1)} %x_in.1, bf16[3,768,384]{2,1,0:T(8,128)(2,1)} %collective-permute-done.w_ref.w_peer, f32[2,384]{1,0:T(2,128)} %copy-done.11), custom_call_target="tpu_custom_call" | custom-call | flops 7851737088 | bytes 12582912 | tf_op jit(solution)/shard_map/attend/pallas_call | solution.py:74
  29.5 0.0 copy-done.1
  29.5 0.0 collective-permute-done.4.bu_peer
  29.5 0.0 copy-start.10
  29.5 0.0 collective-permute-done.2.wo_peer_in.wo_peer
  29.5 0.0 copy-start.9
  29.5 0.0 collective-permute-done.3.wu_peer_in.wu_peer
  29.5 0.0 copy-start.8
  29.5 0.0 collective-permute-done.5.wd_peer_in.wd_peer
  29.5 0.5 copy-done.10
  30.0 0.3 copy-done.9
  30.3 0.7 copy-done.8
  31.1 31.0 %feed.1 = (f32[1024,768]{1,0:T(8,128)}, bf16[1024,1536]{1,0:T(8,128)(2,1)}, bf16[1024,1536]{1,0:T(8,128)(2,1)}, bf16[1024,1536]{1,0:T(8,128)(2,1)}, bf16[1024,15...) custom-call(bf16[1024,384]{1,0:T(8,128)(2,1)} %get-tuple-element.48., ...), custom_call_target="tpu_custom_call" | custom-call | flops 12079595520 | bytes 50331648 | tf_op jit(solution)/shard_map/feed/pallas_call | solution.py:197
  62.1 146.1 %backward.1 = (bf16[36,256,384]{2,1,0:T(8,128)(2,1)}, f32[1024,768]{1,0:T(8,128)}, f32[16,768]{1,0:T(8,128)}) custom-call(s32[2]{0:T(128)} %dynamic_slice.3.lens_ref, bf16[1024,1536]{1,0:T(8,128)(2,1)} %get-tuple-element.51.h_own, bf16[1024,1536]{1,0:T(8,128)(2,1)} %get-tuple-element.52.h_peer, bf16[1024,1536]{1,0:T(8,128)(2,1)} %get-tuple-element.53.gp_own, ...), custom_call_target="tpu_custom_call" | custom-call | flops 64424509440 | bytes 67108864 | tf_op jit(solution)/shard_map/backward/pallas_call | solution.py:703
  208.2 13.8 %unpack.1 = (f32[1024,768]{1,0:T(8,128)}, f32[3,768,384]{2,1,0:T(8,128)}, f32[2,384]{1,0:T(2,128)}, f32[384,768]{1,0:T(8,128)}, f32[768,1536]{1,0:T(8,128)}, /*i...) custom-call(bf16[36,256,384]{2,1,0:T(8,128)(2,1)} %get-tuple-element, ...), custom_call_target="tpu_custom_call" | custom-call | tf_op jit(solution)/shard_map/unpack/pallas_call | solution.py:783
  (7 shorter events, 0.0 us)
Async XLA Ops:
  0.6 16.1 %collective-permute-start = (bf16[3,768,384]{2,1,0:T(8,128)(2,1)}, bf16[3,768,384]{2,1,0:T(8,128)(2,1)}, u32[]{:S(2)}, u32[]{:S(2)}) collective-permute-start(bf16[3,768,384]{2,1,0:T(8,128)(2,1)} %w_own.1), channel_id=1, source_target_pairs={{0,1},{1,0},{2,3},{3,2},{4,5},{5,4},{6,7},{7,6},{8,9},{9,8},{10,11... | collective-permute-start | bytes 5308424 | tf_op jit(solution)/shard_map/ppermute | solution.py:810
  1.2 28.3 %collective-permute-start.3 = (bf16[768,1536]{1,0:T(8,128)(2,1)}, bf16[768,1536]{1,0:T(8,128)(2,1)S(1)}, u32[]{:S(2)}, u32[]{:S(2)}) collective-permute-start(bf16[768,1536]{1,0:T(8,128)(2,1)} %wu_own.1), channel_id=1, source_target_pairs={{0,1},{1,0},{2,3},{3,2},{4,5},{5,4},{6,7},{7,6},{8,9},{9,8},{10,11... | collective-permute-start | bytes 7077896 | tf_op jit(solution)/shard_map/ppermute | solution.py:810
  1.3 28.2 %collective-permute-start.5 = (bf16[1536,768]{1,0:T(8,128)(2,1)}, bf16[1536,768]{1,0:T(8,128)(2,1)}, u32[]{:S(2)}, u32[]{:S(2)}) collective-permute-start(bf16[1536,768]{1,0:T(8,128)(2,1)} %wd_own.1), channel_id=1, source_target_pairs={{0,1},{1,0},{2,3},{3,2},{4,5},{5,4},{6,7},{7,6},{8,9},{9,8},{10,11... | collective-permute-start | bytes 7077896 | tf_op jit(solution)/shard_map/ppermute | solution.py:810
  1.7 15.0 %collective-permute-start.1 = (f32[2,384]{1,0:T(2,128)}, f32[2,384]{1,0:T(2,128)S(1)}, u32[]{:S(2)}, u32[]{:S(2)}) collective-permute-start(f32[2,384]{1,0:T(2,128)} %b_ref.1), channel_id=1, source_target_pairs={{0,1},{1,0},{2,3},{3,2},{4,5},{5,4},{6,7},{7,6},{8,9},{9,8},{10,11... | collective-permute-start | bytes 9224 | tf_op jit(solution)/shard_map/ppermute | solution.py:810
  1.8 27.7 %collective-permute-start.2 = (bf16[384,768]{1,0:T(8,128)(2,1)}, bf16[384,768]{1,0:T(8,128)(2,1)S(1)}, u32[]{:S(2)}, u32[]{:S(2)}) collective-permute-start(bf16[384,768]{1,0:T(8,128)(2,1)} %wo_own.1), channel_id=1, source_target_pairs={{0,1},{1,0},{2,3},{3,2},{4,5},{5,4},{6,7},{7,6},{8,9},{9,8},{10,11... | collective-permute-start | bytes 1769480 | tf_op jit(solution)/shard_map/ppermute | solution.py:810
  3.5 12.4 %copy-start = (f32[1536]{0:T(1024)S(1)}, f32[1536]{0:T(1024)}, u32[]{:S(2)}) copy-start(f32[1536]{0:T(1024)} %param.24) | copy-start | bytes 18436
  3.5 12.4 %copy-start.2 = (f32[768]{0:T(1024)S(1)}, f32[768]{0:T(1024)}, u32[]{:S(2)}) copy-start(f32[768]{0:T(1024)} %param.20) | copy-start | bytes 9220
  3.5 12.4 %copy-start.3 = (f32[768]{0:T(1024)S(1)}, f32[768]{0:T(1024)}, u32[]{:S(2)}) copy-start(f32[768]{0:T(1024)} %param.21) | copy-start | bytes 9220
  3.5 12.4 %copy-start.4 = (f32[768]{0:T(1024)S(1)}, f32[768]{0:T(1024)}, u32[]{:S(2)}) copy-start(f32[768]{0:T(1024)} %param.22) | copy-start | bytes 9220
  3.5 12.5 %copy-start.5 = (f32[768]{0:T(1024)S(1)}, f32[768]{0:T(1024)}, u32[]{:S(2)}) copy-start(f32[768]{0:T(1024)} %param.26) | copy-start | bytes 9220
  3.5 12.5 %copy-start.6 = (f32[768]{0:T(1024)S(1)}, f32[768]{0:T(1024)}, u32[]{:S(2)}) copy-start(f32[768]{0:T(1024)} %param.27) | copy-start | bytes 9220
  3.5 12.5 %copy-start.7 = (f32[768]{0:T(1024)S(1)}, f32[768]{0:T(1024)}, u32[]{:S(2)}) copy-start(f32[768]{0:T(1024)} %param.28) | copy-start | bytes 9220
  15.9 13.6 %copy-start.1 = (f32[1,1536]{1,0:T(1,128)}, f32[1,1536]{1,0:T(1,128)S(1)}, u32[]{:S(2)}) copy-start(f32[1,1536]{1,0:T(1,128)S(1)} %reshape.31.bu_own) | copy-start | bytes 18436
  16.7 0.6 copy-start.11
  16.7 12.8 %collective-permute-start.4 = (f32[1,1536]{1,0:T(1,128)S(1)}, f32[1,1536]{1,0:T(1,128)S(1)}, u32[]{:S(2)}, u32[]{:S(2)}) collective-permute-start(f32[1,1536]{1,0:T(1,128)S(1)} %reshape.31.bu_own), channel_id=1, source_target_pairs={{0,1},{1,0},{2,3},{3,2},{4,5},{5,4},{6,7},{7,6},{8,9},{9,8},{10,11... | collective-permute-start | bytes 18440 | tf_op jit(solution)/shard_map/ppermute | solution.py:810
  29.5 0.6 copy-start.10
  29.5 0.8 copy-start.9
  29.5 1.6 copy-start.8
